TPU v7x, 32 devices: a whole 2x2x4 slice. The times are simulated.
32 devices in a mesh: groups: 2 (over y), seq: 4 (over z), tensor: 4 (over x, core).
Axes of the slice: x: 2, y: 2, z: 4, core: 2. Of those that a mesh axis runs over, the one named last changes fastest.
Arguments:
- activations: bfloat16 [2048, 4096], P(('groups', 'seq')), parts along dimension 0, may hold values from -6 to 6
- token_adapter_index: int32 [2048], P(('groups', 'seq')), parts along dimension 0, may hold values from 0 to 15
- gate_scanned_weight: bfloat16 [4096, 2, 8192], P('seq', None, 'tensor'), may hold values from -0.09375 to 0.09375
- state_vector_weight: bfloat16 [4096, 2, 1024], P('seq'), may hold values from -0.09375 to 0.09375
- time_step_weight: bfloat16 [4096, 128], P('seq', 'tensor'), may hold values from -0.09375 to 0.09375
- adapter_down_maps: bfloat16 [4096, 256], P('seq'), may hold values from -0.09375 to 0.09375
- adapter_up_maps: bfloat16 [256, 2, 8192], P(None, None, 'tensor'), may hold values from -1.5 to 1.5
- scanned_channel_taps: float32 [4, 8192], P(None, 'tensor'), may hold values from -3 to 3
- state_vector_taps: float32 [4, 2, 1024], replicated, may hold values from -3 to 3
- earlier_scanned_channels: bfloat16 [6, 8192], P('groups', 'tensor'), parts along dimension 0, may hold values from -6 to 6
- earlier_state_vectors: bfloat16 [6, 2, 1024], P('groups'), parts along dimension 0, may hold values from -6 to 6
- head_step_bias: float32 [128], P('tensor'), may hold values from -4 to -1
- adapter_step_shift: float32 [16, 128], P(None, 'tensor'), may hold values from -3 to 3
- head_decay_rate: float32 [128], P('tensor'), may hold values from 0.0001953125 to 0.3
- starting_head_state: float32 [256, 64, 128], P(('groups', 'tensor')), parts along dimension 0, may hold values from -6 to 6
- gated_norm_gain: float32 [8192], P('tensor'), may hold values from 0.1 to 1.9
- output_projection_weight: bfloat16 [8192, 4096], P('tensor', 'seq'), may hold values from -0.0625 to 0.0625
Outputs:
- mixed: bfloat16 [2048, 4096], P(('groups', 'tensor'), 'seq'), parts along dimension 0
- checkpoints: float32 [8, 128, 64, 128], P(('groups', 'seq'), 'tensor'), parts along dimension 0
There are 2 independent parts, one for each index of `groups`. A program takes and returns all parts, laid end to end along the dimension named above; an argument that names none is the same for every part. Nothing has to cross between parts.
All inputs are finite; a program needn't handle non-finite values.
Results may differ from a plain program's by a relative error of at most 0.02.
Values may be sent and summed in bfloat16 or wider, within the bound.
No kernel may reach another device: no remote copies, remote signals or barrier semaphores. Data moves between devices by JAX's collectives and lax.ppermute only.
A program may use at most 192 MiB of HBM per device.

v0:
```python
import functools
import jax
import jax.numpy as jnp
from jax import lax
from jax.experimental import pallas as pl
from jax.experimental.pallas import tpu as pltpu
from jax.sharding import PartitionSpec as P


HEADS = 128
HEAD_DIM = 64
STATE = 128
HEAD_SETS = 8
ADAPTER_COUNT = 16
ADAPTER_RANK = 16
CONV = 4
BLOCK = 128
LANES = 128


bf16 = jnp.bfloat16
f32 = jnp.float32


def silu(v):
    return v / (1.0 + jnp.exp(-v))


def project_kernel(where, mine, other, down, weight, up, small, mixed_out, gate_out, values, held, *, rows):
    half = mine.shape[2]
    count = mine.shape[0]
    depth = 2 * half
    core = where[0]
    step = pl.program_id(0)
    ch = gate_out.shape[2]
    tile = held.shape[1]
    per_end = ch // tile

    def plane(end):
        return jnp.where(where[1] == 1, 1 - end, end)

    @pl.when(step == 0)
    def _():
        rank = down.shape[1]
        span = min(half, rows)
        owner = lax.broadcasted_iota(jnp.int32, (rank, span), 0) // ADAPTER_RANK
        near = pl.ds(pl.multiple_of(core * half, half), half)
        far = pl.ds(pl.multiple_of((1 - core) * half, half), half)
        masks = []
        for b in range(count):
            values[b * rows : (b + 1) * rows, near] = mine[where[2 + b], :rows, :]
            values[b * rows : (b + 1) * rows, far] = other[where[2 + b], :rows, :]
            for part in range(rows // span):
                index = mine[where[2 + b], rows : rows + 16, :span].astype(f32)
                index = index[part : part + 1].astype(jnp.int32)
                masks.append((owner == index).astype(f32).T)
        mask = masks[0] if len(masks) == 1 else jnp.concatenate(masks, axis=0)
        full = jnp.dot(values[:, :depth], down[...], preferred_element_type=f32)
        values[:, depth:] = jnp.where(mask > 0.5, full, 0.0).astype(bf16)
        for end in range(2):
            mixed_out[plane(end), :, ch:] = jnp.dot(
                values[:, :depth], small[end], preferred_element_type=f32
            ).astype(bf16)

    end = step // per_end
    dst = pl.ds(pl.multiple_of((step - end * per_end) * tile, tile), tile)
    for pair, out in ((0, gate_out), (1, mixed_out)):
        held[:depth, :] = weight[:, pair].reshape(depth, tile)
        held[depth:, :] = up[:, pair].reshape(held.shape[0] - depth, tile)
        chunk = min(512, values.shape[0])

        def some_rows(at, carry):
            part = pl.ds(pl.multiple_of(at * chunk, chunk), chunk)
            out[plane(end), part, dst] = jnp.dot(
                values[part, :], held[...], preferred_element_type=f32
            ).astype(bf16)
            return carry

        lax.fori_loop(0, values.shape[0] // chunk, some_rows, 0)


def project(where, mine, other, down, weight, up, small, rows, ch):
    n, _, half = mine.shape
    tile = min(256, ch)
    whole = lambda a: pl.BlockSpec(a.shape, lambda b, w: (0,) * a.ndim)
    striped = lambda a: pl.BlockSpec((*a.shape[:3], tile), lambda b, w: (0, 0, 0, b))
    wide = ch + small.shape[2]
    held = lambda c: pl.BlockSpec((2, n * rows, c), lambda b, w: (0, 0, 0))
    full = 2 * half + down.shape[1]
    return pl.pallas_call(
        functools.partial(project_kernel, rows=rows),
        out_shape=(
            jax.ShapeDtypeStruct((2, n * rows, wide), bf16),
            jax.ShapeDtypeStruct((2, n * rows, ch), bf16),
        ),
        grid_spec=pltpu.PrefetchScalarGridSpec(
            num_scalar_prefetch=1,
            grid=(2 * ch // tile,),
            in_specs=[
                whole(mine), whole(other), whole(down), striped(weight), striped(up), whole(small)
            ],
            out_specs=[held(wide), held(ch)],
            scratch_shapes=[pltpu.VMEM((n * rows, full), bf16), pltpu.VMEM((full, tile), bf16)],
        ),
        cost_estimate=pl.CostEstimate(
            flops=4 * n * rows * full * (ch + wide),
            bytes_accessed=2 * weight.size + 4 * n * rows * (ch + wide),
            transcendentals=0,
        ),
        name="project",
    )(where, mine, other, down, weight, up, small)


def merge_kernel(where, gate_a, gate_b, came_a, came_b, gated, go_a, go_b, *, passing):
    ch = gated.shape[1]
    go_a[:, :ch] = (gate_a[0].astype(f32) + came_b[:, :ch].astype(f32)).astype(bf16)
    go_b[:, :ch] = (gate_b[0].astype(f32) + came_a[:, :ch].astype(f32)).astype(bf16)
    own = gated[...]
    if passing:
        own = jnp.where(where[0] == 1, own.astype(f32), came_b[:, ch:].astype(f32)).astype(bf16)
        go_b[:, ch:] = came_a[:, ch:]
    else:
        go_b[:, ch:] = own
    go_a[:, ch:] = own


def merge(where, gates, came, gated):
    ch = gated.shape[1]
    passing = came[0].shape[1] > ch
    whole = lambda a: pl.BlockSpec(a.shape, lambda b, w: (0,) * a.ndim)
    out = jax.ShapeDtypeStruct((BLOCK, 2 * ch), bf16)
    return pl.pallas_call(
        functools.partial(merge_kernel, passing=passing),
        out_shape=(out, out),
        grid_spec=pltpu.PrefetchScalarGridSpec(
            num_scalar_prefetch=1,
            grid=(1,),
            in_specs=[
                pl.BlockSpec((1, BLOCK, ch), lambda b, w: (0, w[1], 0)),
                pl.BlockSpec((1, BLOCK, ch), lambda b, w: (1, w[2], 0)),
                whole(came[0]), whole(came[1]), whole(gated),
            ],
            out_specs=[whole(out), whole(out)],
        ),
        cost_estimate=pl.CostEstimate(
            flops=4 * BLOCK * ch, bytes_accessed=22 * BLOCK * ch, transcendentals=0
        ),
        name="merge",
    )(where, gates, gates, *came, gated)


def scan_kernel(
    gates, sums, tail, state, index, table, rate, taps,
    gated_out, state_out, tail_out, rows, cum_rows, step_rows,
):
    ch = state.shape[1]
    wide = ch + 2 * STATE
    rows[0:8, :] = tail[...]
    rows[8 : 8 + BLOCK, :] = sums[:, :wide].astype(f32)
    tail_out[...] = rows[BLOCK : BLOCK + 8, :]

    def conv(at):
        total = jnp.zeros((BLOCK, LANES), f32)
        for k in range(CONV):
            begin = 8 - (CONV - 1) + k
            total = total + taps[k : k + 1, at] * rows[begin : begin + BLOCK, at]
        return silu(total).astype(bf16)

    input_vec = conv(pl.ds(ch, STATE))
    output_vec = conv(pl.ds(ch + STATE, STATE))
    row = lax.broadcasted_iota(jnp.int32, (BLOCK, BLOCK), 0)
    col = lax.broadcasted_iota(jnp.int32, (BLOCK, BLOCK), 1)
    causal = row >= col
    chosen = (row == index[...].astype(jnp.int32)).astype(f32).T
    shift = jnp.dot(
        chosen, table[...], precision=lax.Precision.HIGHEST, preferred_element_type=f32
    )
    raw = sums[:, wide:].astype(f32) + shift
    step = jnp.maximum(raw, 0.0) + jnp.log1p(jnp.exp(-jnp.abs(raw)))
    cum = jnp.dot(
        causal.astype(f32),
        -rate[...] * step,
        precision=lax.Precision.HIGHEST,
        preferred_element_type=f32,
    )
    cum_rows[...] = cum.T
    step_rows[...] = step.T
    scores = lax.dot_general(
        output_vec, input_vec, (((1,), (1,)), ((), ())), preferred_element_type=f32
    )
    scores = jnp.where(causal, scores, 0.0)
    first_half = col < HEAD_DIM
    input_t = input_vec.T

    def two_heads(pair, carry):
        lanes = pl.ds(pl.multiple_of(pair * LANES, LANES), LANES)
        x = conv(lanes)
        held = state[:, lanes]
        high = held.astype(bf16)
        low = (held - high.astype(f32)).astype(bf16)
        inter = jnp.dot(output_vec, high, preferred_element_type=f32) + jnp.dot(
            output_vec, low, preferred_element_type=f32
        )
        turned = LANES - 2 * pair
        cum_here = pltpu.roll(cum, turned, 1)
        step_here = pltpu.roll(step, turned, 1)
        cums, steps, outs = [], [], []
        for h in range(2):
            row_of = pl.ds(2 * pair + h, 1)
            cum_i = jnp.broadcast_to(cum_here[:, h : h + 1], (BLOCK, BLOCK))
            weight = jnp.exp(jnp.minimum(cum_i - cum_rows[row_of, :], 0.0))
            mixing = (scores * weight * step_rows[row_of, :]).astype(bf16)
            outs.append(jnp.dot(mixing, x, preferred_element_type=f32))
            cums.append(cum_i)
            steps.append(jnp.broadcast_to(step_here[:, h : h + 1], (BLOCK, BLOCK)))
        cum_i = jnp.where(first_half, cums[0], cums[1])
        total = cum_i[BLOCK - 1 :, :]
        out = jnp.where(first_half, outs[0], outs[1]) + jnp.exp(cum_i) * inter
        gated_out[:, lanes] = (out * silu(gates[:, lanes].astype(f32))).astype(bf16)
        factor = jnp.where(first_half, steps[0], steps[1]) * jnp.exp(total - cum_i)
        scaled = (x.astype(f32) * factor).astype(bf16)
        state_out[:, lanes] = jnp.exp(total) * held + jnp.dot(
            input_t, scaled, preferred_element_type=f32
        )
        return carry

    lax.fori_loop(0, ch // LANES, two_heads, 0, unroll=2)


def scan_block(gates, sums, tail, state, index, table, rate, taps):
    ch = state.shape[1]
    wide = ch + 2 * STATE
    whole = lambda a: pl.BlockSpec(a.shape, lambda b: (0,) * a.ndim)
    others = (sums, tail, state, index, table, rate, taps)
    outs = (
        jax.ShapeDtypeStruct((BLOCK, ch), bf16),
        jax.ShapeDtypeStruct((STATE, ch), f32),
        jax.ShapeDtypeStruct((8, wide), f32),
    )
    return pl.pallas_call(
        scan_kernel,
        out_shape=outs,
        grid=(1,),
        in_specs=[pl.BlockSpec((BLOCK, ch), lambda b: (0, 0)), *map(whole, others)],
        out_specs=[whole(o) for o in outs],
        scratch_shapes=[
            pltpu.VMEM((BLOCK + 8, wide), f32),
            pltpu.VMEM((LANES, BLOCK), f32),
            pltpu.VMEM((LANES, BLOCK), f32),
        ],
        cost_estimate=pl.CostEstimate(
            flops=8 * BLOCK * BLOCK * ch,
            bytes_accessed=16 * BLOCK * ch,
            transcendentals=2 * BLOCK * BLOCK * ch // HEAD_DIM,
        ),
        name="scan_block",
    )(gates, *others)


def output_kernel(where, *refs, n, count):
    blocks = refs[: 2 * n * count]
    gain, weight, out, held, sems = refs[2 * n * count :]
    ch = held.shape[1] // 2
    width = weight.shape[1]
    here = where[0]

    def fetch(act):
        for block in range(count):
            for side in range(2):
                place = here if side == 0 else n - 1 - here
                for k in range(n):
                    source = blocks[(block * 2 + side) * n + k]
                    start = source.shape[1] - ch

                    @pl.when(place == k)
                    def _():
                        act(
                            pltpu.make_async_copy(
                                source.at[:, start:],
                                held.at[pl.ds(block * BLOCK, BLOCK), pl.ds(side * ch, ch)],
                                sems.at[block, side],
                            )
                        )

    fetch(lambda copy: copy.start())
    fetch(lambda copy: copy.wait())
    values = held[...].astype(f32)
    squares = jnp.sum(values * values, axis=1, keepdims=True)
    held[...] = (values * gain[...]).astype(bf16)
    tile = min(256, width)

    def some_columns(at, carry):
        part = pl.ds(pl.multiple_of(at * tile, tile), tile)
        out[:, part] = jnp.dot(
            held[...], weight[:, part], preferred_element_type=f32
        ).astype(bf16)
        return carry

    lax.fori_loop(0, width // tile, some_columns, 0)
    out[:, width:] = jnp.broadcast_to(squares, (count * BLOCK, LANES)).astype(bf16)


def output_block(where, blocks, n, gain, weight, ch):
    count = len(blocks) // (2 * n)
    width = weight.shape[1]
    whole = lambda a: pl.BlockSpec(a.shape, lambda b, w: (0, 0))
    return pl.pallas_call(
        functools.partial(output_kernel, n=n, count=count),
        out_shape=jax.ShapeDtypeStruct((count * BLOCK, width + LANES), bf16),
        grid_spec=pltpu.PrefetchScalarGridSpec(
            num_scalar_prefetch=1,
            grid=(1,),
            in_specs=[*(pl.BlockSpec(memory_space=pl.ANY) for _ in blocks), whole(gain), whole(weight)],
            out_specs=pl.BlockSpec((count * BLOCK, width + LANES), lambda b, w: (0, 0)),
            scratch_shapes=[
                pltpu.VMEM((count * BLOCK, 2 * ch), bf16),
                pltpu.SemaphoreType.DMA((count, 2)),
            ],
        ),
        cost_estimate=pl.CostEstimate(
            flops=4 * count * BLOCK * ch * width, bytes_accessed=4 * ch * width + 8 * count * BLOCK * ch, transcendentals=0
        ),
        name="output_block",
    )(where, *blocks, gain, weight)


def per_device(
    activations,
    token_adapter_index,
    gate_scanned_weight,
    state_vector_weight,
    time_step_weight,
    adapter_down_maps,
    adapter_up_maps,
    scanned_channel_taps,
    state_vector_taps,
    earlier_scanned_channels,
    earlier_state_vectors,
    head_step_bias,
    adapter_step_shift,
    head_decay_rate,
    starting_head_state,
    gated_norm_gain,
    output_projection_weight,
):
    n = lax.axis_size("seq")
    here = lax.axis_index("seq")
    shards = lax.axis_size("tensor")
    shard = lax.axis_index("tensor")
    core = shard % 2
    rows = activations.shape[0]
    tokens = rows * n
    depth = gate_scanned_weight.shape[0]
    heads_here = time_step_weight.shape[1]
    heads = heads_here // 2
    ch = heads * HEAD_DIM
    per_set = HEADS // HEAD_SETS
    size = tokens // shards
    assert per_set % heads == 0 and n % 2 == 0 and shards % 2 == 0 and size % BLOCK == 0
    blocks = tokens // BLOCK
    pairs_a = [(j, j ^ 1) for j in range(n)]
    pairs_b = [(j, ((j - 1) ^ 1) + 1) for j in range(1, n - 1)]
    swap = [(j, j ^ 1) for j in range(shards)]
    at_first = here == 0
    at_end = at_first | (here == n - 1)
    odd = here % 2
    as_int = lambda v: v.astype(jnp.int32)

    def own(array, start, count, axis):
        return lax.dynamic_slice_in_dim(array, start, count, axis)

    half = depth // 2
    index_rows = 16 * -(-rows // (16 * half))
    index_pad = jnp.pad(
        token_adapter_index.astype(bf16), (0, index_rows * half - rows)
    ).reshape(index_rows, half)

    def piece(dest):
        part = lax.dynamic_slice(activations, (0, dest * depth + core * half), (rows, half))
        return jnp.concatenate([part, index_pad], axis=0)

    pieces = [piece(here)]
    for k in range(1, n):
        pairs = [(j, (j + k) % n) for j in range(n)]
        pieces.append(lax.ppermute(piece((here + k) % n), "seq", pairs))

    def by_pair(array):
        split = array.reshape(array.shape[0] // 16, 16, 2, array.shape[2])
        return jnp.swapaxes(split, 1, 2)

    weight = by_pair(gate_scanned_weight)
    up = by_pair(adapter_up_maps)

    def small_of(end):
        first = (shard * heads_here + end * heads) // per_set * STATE
        io = own(state_vector_weight, first, STATE, 2).reshape(depth, 2 * STATE)
        steps = time_step_weight[:, end * heads : (end + 1) * heads]
        return jnp.concatenate([io, jnp.pad(steps, ((0, 0), (0, LANES - heads)))], axis=1)

    small = jnp.stack([small_of(0), small_of(1)])
    mine, weight, up, small = lax.optimization_barrier((jnp.stack(pieces), weight, up, small))
    other = lax.ppermute(mine, "tensor", swap)
    index = mine[:, rows:].reshape(n, -1)[:, :rows]
    index = jnp.concatenate(
        [lax.dynamic_index_in_dim(index, (here - b) % n, 0, False) for b in range(n)]
    ).astype(f32).reshape(blocks, 1, BLOCK)

    order = [as_int(core), as_int(1 - odd)] + [as_int((here - b) % n) for b in range(n)]
    mixed, gates = project(
        jnp.stack(order), mine, other, adapter_down_maps, weight, up, small, rows, ch
    )

    end = jnp.where(at_first, 0, 1)
    first_head = end * heads
    first_ch = end * ch
    first_io = (shard * heads_here + first_head) // per_set * STATE
    taps = jnp.concatenate(
        [
            own(scanned_channel_taps, first_ch, ch, 1),
            own(state_vector_taps, first_io, STATE, 2).reshape(CONV, 2 * STATE),
        ],
        axis=1,
    )
    tail = jnp.concatenate(
        [
            own(earlier_scanned_channels, first_ch, ch, 1),
            own(earlier_state_vectors, first_io, STATE, 2).reshape(CONV - 1, 2 * STATE),
        ],
        axis=1,
    ).astype(f32)
    tail = jnp.pad(tail, ((8 - (CONV - 1), 0), (0, 0)))
    table = own(adapter_step_shift + head_step_bias, first_head, heads, 1)
    table = jnp.pad(table, ((0, LANES - ADAPTER_COUNT), (0, LANES - heads)))
    rate = jnp.pad(own(head_decay_rate, first_head, heads, 0), (0, LANES - heads))[None]
    state = own(starting_head_state, first_head, heads, 0).reshape(ch, STATE).T
    gain = gated_norm_gain[None]

    def turn(step):
        to_last = jnp.clip(step - here, 0, blocks - 1)
        to_first = jnp.clip(step - (n - 1 - here), 0, blocks - 1)
        return jnp.where(odd == 0, to_last, to_first), jnp.where(odd == 0, to_first, to_last)

    def taken(array, step):
        shape = (1, BLOCK, array.shape[2])
        return tuple(
            lax.dynamic_slice(array, (side, at * BLOCK, 0), shape)[0]
            for side, at in enumerate(turn(step))
        )

    def added(a, b):
        return (a.astype(f32) + b.astype(f32)).astype(bf16)

    def onward(pair):
        from_a = lax.ppermute(pair[0], "seq", pairs_a)
        from_b = lax.ppermute(pair[1], "seq", pairs_b)
        return from_a, from_b

    def tied(*pairs):
        flat = lax.optimization_barrier(tuple(a for pair in pairs for a in pair))
        return [tuple(flat[k : k + 2]) for k in range(0, len(flat), 2)]

    sends = blocks + n - 2
    last_step = blocks + 2 * n - 3
    per = size // BLOCK
    sums = came = before = gated = None
    went, arrived, states, outs = {}, {}, [], []
    pending = None
    for step in range(last_step + 1):
        block = step - (n - 1)
        if step <= sends:
            go = taken(mixed, step)
            if step > 1:
                sums, before = tied(sums, before)
            if step > 0:
                go = added(go[0], sums[1]), added(go[1], sums[0])
                came, sums = tied(came, sums)
            before = came
            if step < sends:
                sums = onward(go)
        else:
            (came,) = tied(came)
        if step < n:
            gate = taken(gates, step)
            if step > 0:
                gate = added(gate[0], came[1]), added(gate[1], came[0])
            onto = gate
            if step == n - 1 and sends > step:
                onto = gate
        if n <= step < sends:
            where = jnp.stack([as_int(at_end), *map(as_int, turn(step))])
            onto = gate = merge(where, gates, came, gated)
        elif step == sends:
            gate = (None, added(taken(gates, step)[1], came[0][:, :ch]))
        if step >= max(n, sends):
            onto = came[1][:, -ch:], came[0][:, -ch:]
            if gated is not None:
                onto = jnp.where(at_end, gated, onto[0]), onto[1]
        came = onward(onto)
        arrived[step] = came
        if block >= 0:
            if gated is not None:
                went[block - 1] = onto[0]
            gated = None
        if 0 <= block < blocks:
            gated, state, tail = scan_block(
                gate[1], go[1], tail, state, index[block], table, rate, taps
            )
            if pending is not None:
                state, outs[pending] = lax.optimization_barrier((state, outs[pending]))
                pending = None
            if (block + 1) * BLOCK % rows == 0:
                states.append(state.astype(bf16).T)
        elif pending is not None:
            came, (outs[pending], _) = tied(came, (outs[pending], state))
            pending = None
        done = step - (2 * n - 2)
        if done >= 0 and (done + 1) % per == 0:
            needed = []
            for b in range(done + 1 - per, done + 1):
                for _ in range(2):
                    needed.append(went[b])
                    needed.extend(arrived[b + n - 1 + k][1 - k % 2] for k in range(1, n))
            outs.append(
                output_block(as_int(here)[None], needed, n, gain, output_projection_weight, ch)
            )
            pending = len(outs) - 1

    landed = [jnp.where(at_first, states[0], states[n - 1])]
    for k in range(1, n):
        leaving = jnp.where(at_first, states[k], states[n - 1 - k])
        landed.append(lax.ppermute(leaving, "seq", [(0, k), (n - 1, n - 1 - k)]))
    landed = jnp.stack(landed)
    finish = jnp.concatenate(
        [lax.dynamic_index_in_dim(landed, which, 0, False) for which in (here, n - 1 - here)], axis=0
    ).astype(f32).reshape(heads_here, HEAD_DIM, STATE)

    chips = shards // 2
    chip = shard // 2
    if chips == 2:
        total = None
        for t in range(shards):
            give = [(j, j ^ 1) for j in range(shards) if j % 2 != t % 2]
            both = added(outs[t], lax.ppermute(outs[t], "tensor", give))
            came = lax.ppermute(both, "tensor", [(t ^ 2, t)])
            both = both.astype(f32) + came.astype(f32)
            total = both if total is None else jnp.where(shard == t, both, total)
    else:
        halves = []
        for k in range(chips):
            keep = jnp.where(core == 0, outs[2 * k], outs[2 * k + 1])
            give = jnp.where(core == 0, outs[2 * k + 1], outs[2 * k])
            halves.append(added(keep, lax.ppermute(give, "tensor", swap)))
        halves = jnp.stack(halves)
        total = lax.dynamic_index_in_dim(halves, chip, 0, False).astype(f32)
        for k in range(1, chips):
            pairs = [(j, (j + 2 * k) % shards) for j in range(shards)]
            give = lax.dynamic_index_in_dim(halves, (chip + k) % chips, 0, False)
            total = total + lax.ppermute(give, "tensor", pairs).astype(f32)
    width = output_projection_weight.shape[1]
    scale = lax.rsqrt(total[:, width : width + 1] / (HEADS * HEAD_DIM) + 1e-05)
    mixed = (total[:, :width] * scale).astype(bf16)
    return (mixed, finish[None])


def solution(mesh):
    return jax.shard_map(
        per_device,
        mesh=mesh,
        in_specs=(
            P(("groups", "seq"), None),
            P(("groups", "seq")),
            P("seq", None, "tensor"),
            P("seq", None, None),
            P("seq", "tensor"),
            P("seq", None),
            P(None, None, "tensor"),
            P(None, "tensor"),
            P(),
            P("groups", "tensor"),
            P("groups", None, None),
            P("tensor"),
            P(None, "tensor"),
            P("tensor"),
            P(("groups", "tensor"), None, None),
            P("tensor"),
            P("tensor", "seq"),
        ),
        out_specs=(P(("groups", "tensor"), "seq"), P(("groups", "seq"), "tensor", None, None)),
        check_vma=False,
    )
```

profile of v0, /device:TPU:0, one launch (start us, length us, event | category | flops | bytes accessed | tf_op | source)
XLA Modules:
  0.0 353.9 jit_solution(11351370837802499618)
XLA Ops:
  13.7 11.5 %copy.48 = bf16[64,16,2,2048]{3,1,2,0:T(8,128)(2,1)} copy(bf16[64,16,2,2048]{3,2,1,0:T(2,128)(2,1)} %bitcast.182) | data formatting | bytes 16777216 | tf_op jit(solution)/shard_map/reshape | solution.py:388
  33.2 27.1 %project.1 = (bf16[2,1024,1408]{2,1,0:T(8,128)(2,1)}, bf16[2,1024,1024]{2,1,0:T(8,128)(2,1)}) custom-call(s32[6]{0:T(128)} %stack.136.where, bf16[4,272,512]{2,1,0:T(8,128)(2,1)} %copy-done.34, bf16[4,272,512]{2,1,0:T(8,128)(2,1)} %collective-permute-done.3.other, bf16[1024,256]{1,0:T(8,128)(2,1)} %down.1, bf16[64,2,16,2048]{3,2,1,0:T(8,128)(2,1)} %bitcast.183, ...), custom_call_target="tpu_custom_call" | custom-call | flops 12750684160 | bytes 18350080 | tf_op jit(solution)/shard_map/project/pallas_call | solution.py:90
  61.5 5.3 %collective-permute-start.6 = (bf16[128,1408]{1,0:T(8,128)(2,1)S(1)}, bf16[128,1408]{1,0:T(8,128)(2,1)S(1)}, u32[]{:S(2)}, u32[]{:S(2)}) collective-permute-start(bf16[128,1408]{1,0:T(8,128)(2,1)S(1)} %get-tuple-element.201), channel_id=1, source_target_pairs={{0,4},{4,0},{8,12},{12,8},{1,5},{5,1},{9,13},{13,9},{2,6},{6,2},{1... | collective-permute-start | bytes 1081352 | tf_op jit(solution)/shard_map/ppermute | solution.py:454
  68.6 7.0 %collective-permute-done.6 = bf16[128,1408]{1,0:T(8,128)(2,1)S(1)} collective-permute-done((bf16[128,1408]{1,0:T(8,128)(2,1)S(1)}, bf16[128,1408]{1,0:T(8,128)(2,1)S(1)}, u32[]{:S(2)}, u32[]{:S(2)}) %collective-permute-start.6) | collective-permute-done | bytes 360480 | tf_op jit(solution)/shard_map/ppermute | solution.py:454
  87.5 6.6 %collective-permute-done.4 = bf16[128,1024]{1,0:T(8,128)(2,1)S(1)} collective-permute-done((bf16[128,1024]{1,0:T(8,128)(2,1)S(1)}, bf16[128,1024]{1,0:T(8,128)(2,1)S(1)}, u32[]{:S(2)}, u32[]{:S(2)}) %collective-permute-start.4) | collective-permute-done | bytes 262176 | tf_op jit(solution)/shard_map/ppermute | solution.py:454
  105.6 6.1 %collective-permute-done.8 = bf16[128,1024]{1,0:T(8,128)(2,1)S(1)} collective-permute-done((bf16[128,1024]{1,0:T(8,128)(2,1)S(1)}, bf16[128,1024]{1,0:T(8,128)(2,1)S(1)}, u32[]{:S(2)}, u32[]{:S(2)}) %collective-permute-start.8) | collective-permute-done | bytes 262176 | tf_op jit(solution)/shard_map/ppermute | solution.py:454
  138.9 4.8 %scan_block.8 = (bf16[128,1024]{1,0:T(8,128)(2,1)}, f32[128,1024]{1,0:T(8,128)}, f32[8,1280]{1,0:T(8,128)}) custom-call(bf16[128,1024]{1,0:T(8,128)(2,1)} %copy-done.35, bf16[128,1408]{1,0:T(8,128)(2,1)} %copy-done.28, f32[8,1280]{1,0:T(8,128)} %fusion.40.tail, f32[128,1024]{1,0:T(8,128)} %bitcast.188, f32[1,128]{1,0:T(1,128)} %get-tuple-element.235.index, ...), custom_call_target="tpu_custom_call" | custom-call | flops 134217728 | bytes 2097152 | tf_op jit(solution)/shard_map/scan_block/pallas_call | solution.py:240
  157.4 4.9 %scan_block.9 = (bf16[128,1024]{1,0:T(8,128)(2,1)}, f32[128,1024]{1,0:T(8,128)}, f32[8,1280]{1,0:T(8,128)}) custom-call(bf16[128,2048]{1,0:T(8,128)(2,1)} %get-tuple-element.112.gates, bf16[128,1408]{1,0:T(8,128)(2,1)} %copy-done.29, f32[8,1280]{1,0:T(8,128)} %get-tuple-element.117.tail, f32[128,1024]{1,0:T(8,128)} %get-tuple-element.118.state, ...), custom_call_target="tpu_custom_call" | custom-call | flops 134217728 | bytes 2097152 | tf_op jit(solution)/shard_map/scan_block/pallas_call | solution.py:240
  176.6 4.8 %scan_block.10 = (bf16[128,1024]{1,0:T(8,128)(2,1)}, f32[128,1024]{1,0:T(8,128)}, f32[8,1280]{1,0:T(8,128)}) custom-call(bf16[128,2048]{1,0:T(8,128)(2,1)} %get-tuple-element.121.gates, bf16[128,1408]{1,0:T(8,128)(2,1)} %copy-done.30, f32[8,1280]{1,0:T(8,128)} %get-tuple-element.126.tail, f32[128,1024]{1,0:T(8,128)} %get-tuple-element.127.state, ...), custom_call_target="tpu_custom_call" | custom-call | flops 134217728 | bytes 2097152 | tf_op jit(solution)/shard_map/scan_block/pallas_call | solution.py:240
  197.3 4.9 %scan_block.11 = (bf16[128,1024]{1,0:T(8,128)(2,1)}, f32[128,1024]{1,0:T(8,128)}, f32[8,1280]{1,0:T(8,128)}) custom-call(bf16[128,2048]{1,0:T(8,128)(2,1)} %get-tuple-element.130.gates, bf16[128,1408]{1,0:T(8,128)(2,1)} %copy-done.31, f32[8,1280]{1,0:T(8,128)} %get-tuple-element.135.tail, f32[128,1024]{1,0:T(8,128)} %get-tuple-element.136.state, ...), custom_call_target="tpu_custom_call" | custom-call | flops 134217728 | bytes 2097152 | tf_op jit(solution)/shard_map/scan_block/pallas_call | solution.py:240
  212.0 4.4 %collective-permute-start.38 = (bf16[128,1408]{1,0:T(8,128)(2,1)S(1)}, bf16[128,1408]{1,0:T(8,128)(2,1)S(1)}, u32[]{:S(2)}, u32[]{:S(2)}) collective-permute-start(bf16[128,1408]{1,0:T(8,128)(2,1)S(1)} %get-tuple-element.184), channel_id=1, source_target_pairs={{0,4},{4,0},{8,12},{12,8},{1,5},{5,1},{9,13},{13,9},{2,6},{6,2},{1... | collective-permute-start | bytes 1081352 | tf_op jit(solution)/shard_map/ppermute | solution.py:454
  217.0 5.0 %scan_block.12 = (bf16[128,1024]{1,0:T(8,128)(2,1)}, f32[128,1024]{1,0:T(8,128)}, f32[8,1280]{1,0:T(8,128)}) custom-call(bf16[128,2048]{1,0:T(8,128)(2,1)} %get-tuple-element.139.gates, bf16[128,1408]{1,0:T(8,128)(2,1)} %copy-done.32, f32[8,1280]{1,0:T(8,128)} %get-tuple-element.144.tail, f32[128,1024]{1,0:T(8,128)} %get-tuple-element.145.state, ...), custom_call_target="tpu_custom_call" | custom-call | flops 134217728 | bytes 2097152 | tf_op jit(solution)/shard_map/scan_block/pallas_call | solution.py:240
  236.5 4.9 %scan_block.13 = (bf16[128,1024]{1,0:T(8,128)(2,1)}, f32[128,1024]{1,0:T(8,128)}, f32[8,1280]{1,0:T(8,128)}) custom-call(bf16[128,2048]{1,0:T(8,128)(2,1)} %get-tuple-element.148.gates, bf16[128,1408]{1,0:T(8,128)(2,1)} %copy-done.33, f32[8,1280]{1,0:T(8,128)} %get-tuple-element.153.tail, f32[128,1024]{1,0:T(8,128)} %get-tuple-element.154.state, ...), custom_call_target="tpu_custom_call" | custom-call | flops 134217728 | bytes 2097152 | tf_op jit(solution)/shard_map/scan_block/pallas_call | solution.py:240
  247.3 6.5 %output_block.4 = bf16[256,1152]{1,0:T(8,128)(2,1)} custom-call(s32[1]{0:T(128)} %bitcast.where, bf16[128,2048]{1,0:T(8,128)(2,1)} %get-tuple-element.111.refs_0_.refs_4_, bf16[128,2048]{1,0:T(8,128)(2,1)} %copy-done.6, bf16[128,2048]{1,0:T(8,128)(2,1)} %copy-done.8, bf16[128,2048]{1,0:T(8,128)(2,1)} %copy-done.2, ...), custom_call_target="tpu_custom_call" | custom-call | flops 1073741824 | bytes 6291456 | tf_op jit(solution)/shard_map/output_block/pallas_call | solution.py:307
  255.9 4.9 %scan_block.14 = (bf16[128,1024]{1,0:T(8,128)(2,1)}, f32[128,1024]{1,0:T(8,128)}, f32[8,1280]{1,0:T(8,128)}) custom-call(bf16[128,2048]{1,0:T(8,128)(2,1)} %get-tuple-element.156.gates, bf16[128,1408]{1,0:T(8,128)(2,1)} %get-tuple-element.182.sums, f32[8,1280]{1,0:T(8,128)} %get-tuple-element.157.tail, f32[128,1024]{1,0:T(8,128)} %get-tuple-element.159.state, ...), custom_call_target="tpu_custom_call" | custom-call | flops 134217728 | bytes 2097152 | tf_op jit(solution)/shard_map/scan_block/pallas_call | solution.py:240
  267.0 5.0 %scan_block.15 = (bf16[128,1024]{1,0:T(8,128)(2,1)}, f32[128,1024]{1,0:T(8,128)}, f32[8,1280]{1,0:T(8,128)}) custom-call(bf16[128,1024]{1,0:T(8,128)(2,1)} %fusion.26.gates, bf16[128,1408]{1,0:T(8,128)(2,1)} %get-tuple-element.183.sums, f32[8,1280]{1,0:T(8,128)} %get-tuple-element.166.tail, f32[128,1024]{1,0:T(8,128)} %get-tuple-element.167.state, ...), custom_call_target="tpu_custom_call" | custom-call | flops 134217728 | bytes 2097152 | tf_op jit(solution)/shard_map/scan_block/pallas_call | solution.py:240
  280.3 3.9 %collective-permute-start.47 = (bf16[128,1024]{1,0:T(8,128)(2,1)S(1)}, bf16[128,1024]{1,0:T(8,128)(2,1)S(1)}, u32[]{:S(2)}, u32[]{:S(2)}) collective-permute-start(bf16[128,1024]{1,0:T(8,128)(2,1)S(1)} %collective-permute-done.45.refs_2_.refs_6_), channel_id=1, source_target_pairs={{0,4},{4,0},{8,12},{12,8},{1,5},{5,1},{9,13},{13,9},{2,6},{6,2},{1... | collective-permute-start | bytes 786440 | tf_op jit(solution)/shard_map/ppermute | solution.py:454
  286.5 4.6 %collective-permute-start.58 = (bf16[1024,128]{0,1:T(8,128)(2,1)}, bf16[1024,128]{0,1:T(8,128)(2,1)}, u32[]{:S(2)}, u32[]{:S(2)}) collective-permute-start(bf16[1024,128]{0,1:T(8,128)(2,1)} %get-tuple-element.220), channel_id=1, source_target_pairs={{0,4},{12,8},{1,5},{13,9},{2,6},{14,10},{3,7},{15,11},{16,20},{28,... | collective-permute-start | bytes 786440 | tf_op jit(solution)/shard_map/ppermute | solution.py:531
  293.0 6.5 %output_block.6 = bf16[256,1152]{1,0:T(8,128)(2,1)} custom-call(s32[1]{0:T(128)} %bitcast.where, bf16[128,2048]{1,0:T(8,128)(2,1)} %get-tuple-element.129.refs_0_.refs_4_, bf16[128,2048]{1,0:T(8,128)(2,1)} %copy-done.2, bf16[128,2048]{1,0:T(8,128)(2,1)} %copy-done.9, bf16[128,2048]{1,0:T(8,128)(2,1)} %copy-done.4, ...), custom_call_target="tpu_custom_call" | custom-call | flops 1073741824 | bytes 6291456 | tf_op jit(solution)/shard_map/output_block/pallas_call | solution.py:307
  299.6 6.6 %output_block.5 = bf16[256,1152]{1,0:T(8,128)(2,1)} custom-call(s32[1]{0:T(128)} %bitcast.where, bf16[128,2048]{1,0:T(8,128)(2,1)} %get-tuple-element.147.refs_0_.refs_4_, bf16[128,2048]{1,0:T(8,128)(2,1)} %copy-done.4, bf16[128,2048]{1,0:T(8,128)(2,1)} %copy-done.14, bf16[128,1024]{1,0:T(8,128)(2,1)} %copy-done.12, ...), custom_call_target="tpu_custom_call" | custom-call | flops 1073741824 | bytes 6291456 | tf_op jit(solution)/shard_map/output_block/pallas_call | solution.py:307
  316.3 6.5 %output_block.7 = bf16[256,1152]{1,0:T(8,128)(2,1)} custom-call(s32[1]{0:T(128)} %bitcast.where, bf16[128,1024]{1,0:T(8,128)(2,1)} %copy-done.22, bf16[128,1024]{1,0:T(8,128)(2,1)} %copy-done.12, bf16[128,1024]{1,0:T(8,128)(2,1)} %copy-done.36, bf16[128,1024]{1,0:T(8,128)(2,1)} %copy-done.37, bf16[128,1024]{1,0:T(8,128)(2,1)} %copy-done.22, ...), custom_call_target="tpu_custom_call" | custom-call | flops 1073741824 | bytes 6291456 | tf_op jit(solution)/shard_map/output_block/pallas_call | solution.py:307
  322.9 3.9 %collective-permute-start.50 = (bf16[256,1152]{1,0:T(8,128)(2,1)}, bf16[256,1152]{1,0:T(8,128)(2,1)S(1)}, u32[]{:S(2)}, u32[]{:S(2)}) collective-permute-start(bf16[256,1152]{1,0:T(8,128)(2,1)} %output_block.7), channel_id=1, source_target_pairs={{0,1},{2,3},{4,5},{6,7},{8,9},{10,11},{12,13},{14,15},{16,17},{18,... | collective-permute-start | bytes 1769480 | tf_op jit(solution)/shard_map/ppermute | solution.py:543
  334.5 4.2 %collective-permute-start.53 = (bf16[256,1152]{1,0:T(8,128)(2,1)S(1)}, bf16[256,1152]{1,0:T(8,128)(2,1)}, u32[]{:S(2)}, u32[]{:S(2)}) collective-permute-start(bf16[256,1152]{1,0:T(8,128)(2,1)S(1)} %add_convert_fusion.2), channel_id=1, source_target_pairs={{0,2},{4,6},{8,10},{12,14},{16,18},{20,22},{24,26},{28,30}} | collective-permute-start | bytes 1769480 | tf_op jit(solution)/shard_map/ppermute | solution.py:544
  345.4 5.2 %collective-permute-done.53 = bf16[256,1152]{1,0:T(8,128)(2,1)} collective-permute-done((bf16[256,1152]{1,0:T(8,128)(2,1)S(1)}, bf16[256,1152]{1,0:T(8,128)(2,1)}, u32[]{:S(2)}, u32[]{:S(2)}) %collective-permute-start.53) | collective-permute-done | bytes 589856 | tf_op jit(solution)/shard_map/ppermute | solution.py:544
  (291 shorter events, 197.1 us)
Async XLA Ops:
  3.6 25.3 %collective-permute-start = (bf16[272,512]{1,0:T(8,128)(2,1)}, bf16[272,512]{1,0:T(8,128)(2,1)}, u32[]{:S(2)}, u32[]{:S(2)}) collective-permute-start(bf16[272,512]{1,0:T(8,128)(2,1)} %get-tuple-element.225), channel_id=1, source_target_pairs={{0,4},{4,8},{8,12},{12,0},{1,5},{5,9},{9,13},{13,1},{2,6},{6,10},{... | collective-permute-start | bytes 835592 | tf_op jit(solution)/shard_map/ppermute | solution.py:385
  6.7 22.3 %collective-permute-start.1 = (bf16[272,512]{1,0:T(8,128)(2,1)S(1)}, bf16[272,512]{1,0:T(8,128)(2,1)}, u32[]{:S(2)}, u32[]{:S(2)}) collective-permute-start(bf16[272,512]{1,0:T(8,128)(2,1)S(1)} %get-tuple-element.226), channel_id=1, source_target_pairs={{0,8},{4,12},{8,0},{12,4},{1,9},{5,13},{9,1},{13,5},{2,10},{6,14},... | collective-permute-start | bytes 835592 | tf_op jit(solution)/shard_map/ppermute | solution.py:385
  9.3 19.7 %collective-permute-start.2 = (bf16[272,512]{1,0:T(8,128)(2,1)S(1)}, bf16[272,512]{1,0:T(8,128)(2,1)}, u32[]{:S(2)}, u32[]{:S(2)}) collective-permute-start(bf16[272,512]{1,0:T(8,128)(2,1)S(1)} %get-tuple-element.227), channel_id=1, source_target_pairs={{0,12},{4,0},{8,4},{12,8},{1,13},{5,1},{9,5},{13,9},{2,14},{6,2},{... | collective-permute-start | bytes 835592 | tf_op jit(solution)/shard_map/ppermute | solution.py:385
  76.8 17.3 %collective-permute-start.10 = (bf16[128,1408]{1,0:T(8,128)(2,1)S(1)}, bf16[128,1408]{1,0:T(8,128)(2,1)S(1)}, u32[]{:S(2)}, u32[]{:S(2)}) collective-permute-start(bf16[128,1408]{1,0:T(8,128)(2,1)S(1)} %get-tuple-element.199), channel_id=1, source_target_pairs={{0,4},{4,0},{8,12},{12,8},{1,5},{5,1},{9,13},{13,9},{2,6},{6,2},{1... | collective-permute-start | bytes 1081352 | tf_op jit(solution)/shard_map/ppermute | solution.py:454
  95.4 16.3 %collective-permute-start.14 = (bf16[128,1408]{1,0:T(8,128)(2,1)S(1)}, bf16[128,1408]{1,0:T(8,128)(2,1)S(1)}, u32[]{:S(2)}, u32[]{:S(2)}) collective-permute-start(bf16[128,1408]{1,0:T(8,128)(2,1)S(1)} %get-tuple-element.197), channel_id=1, source_target_pairs={{0,4},{4,0},{8,12},{12,8},{1,5},{5,1},{9,13},{13,9},{2,6},{6,2},{1... | collective-permute-start | bytes 1081352 | tf_op jit(solution)/shard_map/ppermute | solution.py:454
  113.0 15.5 %collective-permute-start.18 = (bf16[128,1408]{1,0:T(8,128)(2,1)S(1)}, bf16[128,1408]{1,0:T(8,128)(2,1)S(1)}, u32[]{:S(2)}, u32[]{:S(2)}) collective-permute-start(bf16[128,1408]{1,0:T(8,128)(2,1)S(1)} %get-tuple-element.195), channel_id=1, source_target_pairs={{0,4},{4,0},{8,12},{12,8},{1,5},{5,1},{9,13},{13,9},{2,6},{6,2},{1... | collective-permute-start | bytes 1081352 | tf_op jit(solution)/shard_map/ppermute | solution.py:454
  129.7 22.6 %collective-permute-start.22 = (bf16[128,1408]{1,0:T(8,128)(2,1)S(1)}, bf16[128,1408]{1,0:T(8,128)(2,1)S(1)}, u32[]{:S(2)}, u32[]{:S(2)}) collective-permute-start(bf16[128,1408]{1,0:T(8,128)(2,1)S(1)} %get-tuple-element.193), channel_id=1, source_target_pairs={{0,4},{4,0},{8,12},{12,8},{1,5},{5,1},{9,13},{13,9},{2,6},{6,2},{1... | collective-permute-start | bytes 1081352 | tf_op jit(solution)/shard_map/ppermute | solution.py:454
  133.4 18.9 %collective-permute-start.23 = (bf16[128,1408]{1,0:T(8,128)(2,1)S(1)}, bf16[128,1408]{1,0:T(8,128)(2,1)S(1)}, u32[]{:S(2)}, u32[]{:S(2)}) collective-permute-start(bf16[128,1408]{1,0:T(8,128)(2,1)S(1)} %get-tuple-element.192.sums), channel_id=1, source_target_pairs={{4,8},{8,4},{5,9},{9,5},{6,10},{10,6},{7,11},{11,7},{20,24},{24,20... | collective-permute-start | bytes 1081352 | tf_op jit(solution)/shard_map/ppermute | solution.py:455
  148.1 15.5 %collective-permute-start.20 = (bf16[128,2048]{1,0:T(8,128)(2,1)}, bf16[128,2048]{1,0:T(8,128)(2,1)S(1)}, u32[]{:S(2)}, u32[]{:S(2)}) collective-permute-start(bf16[128,2048]{1,0:T(8,128)(2,1)} %get-tuple-element.111.refs_0_.refs_4_), channel_id=1, source_target_pairs={{0,4},{4,0},{8,12},{12,8},{1,5},{5,1},{9,13},{13,9},{2,6},{6,2},{1... | collective-permute-start | bytes 1572872 | tf_op jit(solution)/shard_map/ppermute | solution.py:454
  153.7 18.3 %collective-permute-start.26 = (bf16[128,1408]{1,0:T(8,128)(2,1)S(1)}, bf16[128,1408]{1,0:T(8,128)(2,1)S(1)}, u32[]{:S(2)}, u32[]{:S(2)}) collective-permute-start(bf16[128,1408]{1,0:T(8,128)(2,1)S(1)} %get-tuple-element.191), channel_id=1, source_target_pairs={{0,4},{4,0},{8,12},{12,8},{1,5},{5,1},{9,13},{13,9},{2,6},{6,2},{1... | collective-permute-start | bytes 1081352 | tf_op jit(solution)/shard_map/ppermute | solution.py:454
  156.1 15.9 %collective-permute-start.27 = (bf16[128,1408]{1,0:T(8,128)(2,1)S(1)}, bf16[128,1408]{1,0:T(8,128)(2,1)S(1)}, u32[]{:S(2)}, u32[]{:S(2)}) collective-permute-start(bf16[128,1408]{1,0:T(8,128)(2,1)S(1)} %get-tuple-element.190.sums), channel_id=1, source_target_pairs={{4,8},{8,4},{5,9},{9,5},{6,10},{10,6},{7,11},{11,7},{20,24},{24,20... | collective-permute-start | bytes 1081352 | tf_op jit(solution)/shard_map/ppermute | solution.py:455
  173.3 18.3 %collective-permute-start.30 = (bf16[128,1408]{1,0:T(8,128)(2,1)S(1)}, bf16[128,1408]{1,0:T(8,128)(2,1)S(1)}, u32[]{:S(2)}, u32[]{:S(2)}) collective-permute-start(bf16[128,1408]{1,0:T(8,128)(2,1)S(1)} %get-tuple-element.189), channel_id=1, source_target_pairs={{0,4},{4,0},{8,12},{12,8},{1,5},{5,1},{9,13},{13,9},{2,6},{6,2},{1... | collective-permute-start | bytes 1081352 | tf_op jit(solution)/shard_map/ppermute | solution.py:454
  175.9 15.7 %collective-permute-start.31 = (bf16[128,1408]{1,0:T(8,128)(2,1)S(1)}, bf16[128,1408]{1,0:T(8,128)(2,1)S(1)}, u32[]{:S(2)}, u32[]{:S(2)}) collective-permute-start(bf16[128,1408]{1,0:T(8,128)(2,1)S(1)} %get-tuple-element.188.sums), channel_id=1, source_target_pairs={{4,8},{8,4},{5,9},{9,5},{6,10},{10,6},{7,11},{11,7},{20,24},{24,20... | collective-permute-start | bytes 1081352 | tf_op jit(solution)/shard_map/ppermute | solution.py:455
  192.9 17.1 %collective-permute-start.34 = (bf16[128,1408]{1,0:T(8,128)(2,1)S(1)}, bf16[128,1408]{1,0:T(8,128)(2,1)S(1)}, u32[]{:S(2)}, u32[]{:S(2)}) collective-permute-start(bf16[128,1408]{1,0:T(8,128)(2,1)S(1)} %get-tuple-element.187), channel_id=1, source_target_pairs={{0,4},{4,0},{8,12},{12,8},{1,5},{5,1},{9,13},{13,9},{2,6},{6,2},{1... | collective-permute-start | bytes 1081352 | tf_op jit(solution)/shard_map/ppermute | solution.py:454
  206.4 15.6 %collective-permute-start.32 = (bf16[128,2048]{1,0:T(8,128)(2,1)}, bf16[128,2048]{1,0:T(8,128)(2,1)S(1)}, u32[]{:S(2)}, u32[]{:S(2)}) collective-permute-start(bf16[128,2048]{1,0:T(8,128)(2,1)} %get-tuple-element.138.refs_8_.refs_12_), channel_id=1, source_target_pairs={{0,4},{4,0},{8,12},{12,8},{1,5},{5,1},{9,13},{13,9},{2,6},{6,2},{1... | collective-permute-start | bytes 1572872 | tf_op jit(solution)/shard_map/ppermute | solution.py:454
  233.2 20.5 %collective-permute-start.42 = (bf16[128,1408]{1,0:T(8,128)(2,1)S(1)}, bf16[128,1408]{1,0:T(8,128)(2,1)S(1)}, u32[]{:S(2)}, u32[]{:S(2)}) collective-permute-start(bf16[128,1408]{1,0:T(8,128)(2,1)S(1)} %fusion.8), channel_id=1, source_target_pairs={{0,4},{4,0},{8,12},{12,8},{1,5},{5,1},{9,13},{13,9},{2,6},{6,2},{1... | collective-permute-start | bytes 1081352 | tf_op jit(solution)/shard_map/ppermute | solution.py:454
  276.6 31.8 %collective-permute-start.56 = (bf16[256,1152]{1,0:T(8,128)(2,1)S(1)}, bf16[256,1152]{1,0:T(8,128)(2,1)}, u32[]{:S(2)}, u32[]{:S(2)}) collective-permute-start(bf16[256,1152]{1,0:T(8,128)(2,1)S(1)} %copy-done.15), channel_id=1, source_target_pairs={{1,0},{3,2},{5,4},{7,6},{9,8},{11,10},{13,12},{15,14},{17,16},{19,... | collective-permute-start | bytes 1769480 | tf_op jit(solution)/shard_map/ppermute | solution.py:543
  280.3 25.8 %collective-permute-start.47 = (bf16[128,1024]{1,0:T(8,128)(2,1)S(1)}, bf16[128,1024]{1,0:T(8,128)(2,1)S(1)}, u32[]{:S(2)}, u32[]{:S(2)}) collective-permute-start(bf16[128,1024]{1,0:T(8,128)(2,1)S(1)} %collective-permute-done.45.refs_2_.refs_6_), channel_id=1, source_target_pairs={{0,4},{4,0},{8,12},{12,8},{1,5},{5,1},{9,13},{13,9},{2,6},{6,2},{1... | collective-permute-start | bytes 786440 | tf_op jit(solution)/shard_map/ppermute | solution.py:454
  284.2 24.2 %collective-permute-start.48 = (bf16[128,1024]{1,0:T(8,128)(2,1)S(1)}, bf16[128,1024]{1,0:T(8,128)(2,1)}, u32[]{:S(2)}, u32[]{:S(2)}) collective-permute-start(bf16[128,1024]{1,0:T(8,128)(2,1)S(1)} %collective-permute-done.46.refs_11_.refs_15_.refs_9_.refs_13_), channel_id=1, source_target_pairs={{4,8},{8,4},{5,9},{9,5},{6,10},{10,6},{7,11},{11,7},{20,24},{24,20... | collective-permute-start | bytes 786440 | tf_op jit(solution)/shard_map/ppermute | solution.py:455
  286.5 48.1 %collective-permute-start.58 = (bf16[1024,128]{0,1:T(8,128)(2,1)}, bf16[1024,128]{0,1:T(8,128)(2,1)}, u32[]{:S(2)}, u32[]{:S(2)}) collective-permute-start(bf16[1024,128]{0,1:T(8,128)(2,1)} %get-tuple-element.220), channel_id=1, source_target_pairs={{0,4},{12,8},{1,5},{13,9},{2,6},{14,10},{3,7},{15,11},{16,20},{28,... | collective-permute-start | bytes 786440 | tf_op jit(solution)/shard_map/ppermute | solution.py:531
  291.0 47.7 %collective-permute-start.59 = (bf16[1024,128]{0,1:T(8,128)(2,1)}, bf16[1024,128]{0,1:T(8,128)(2,1)}, u32[]{:S(2)}, u32[]{:S(2)}) collective-permute-start(bf16[1024,128]{0,1:T(8,128)(2,1)} %get-tuple-element.221), channel_id=1, source_target_pairs={{0,8},{12,4},{1,9},{13,5},{2,10},{14,6},{3,11},{15,7},{16,24},{28,... | collective-permute-start | bytes 786440 | tf_op jit(solution)/shard_map/ppermute | solution.py:531
  306.2 16.7 %collective-permute-start.54 = (bf16[256,1152]{1,0:T(8,128)(2,1)S(1)}, bf16[256,1152]{1,0:T(8,128)(2,1)}, u32[]{:S(2)}, u32[]{:S(2)}) collective-permute-start(bf16[256,1152]{1,0:T(8,128)(2,1)S(1)} %copy-done.19), channel_id=1, source_target_pairs={{0,1},{2,3},{4,5},{6,7},{8,9},{10,11},{12,13},{14,15},{16,17},{18,... | collective-permute-start | bytes 1769480 | tf_op jit(solution)/shard_map/ppermute | solution.py:543
  309.7 35.7 %collective-permute-start.57 = (bf16[256,1152]{1,0:T(8,128)(2,1)S(1)}, bf16[256,1152]{1,0:T(8,128)(2,1)}, u32[]{:S(2)}, u32[]{:S(2)}) collective-permute-start(bf16[256,1152]{1,0:T(8,128)(2,1)S(1)} %add_convert_fusion), channel_id=1, source_target_pairs={{2,0},{6,4},{10,8},{14,12},{18,16},{22,20},{26,24},{30,28}} | collective-permute-start | bytes 1769480 | tf_op jit(solution)/shard_map/ppermute | solution.py:544
  334.5 16.0 %collective-permute-start.53 = (bf16[256,1152]{1,0:T(8,128)(2,1)S(1)}, bf16[256,1152]{1,0:T(8,128)(2,1)}, u32[]{:S(2)}, u32[]{:S(2)}) collective-permute-start(bf16[256,1152]{1,0:T(8,128)(2,1)S(1)} %add_convert_fusion.2), channel_id=1, source_target_pairs={{0,2},{4,6},{8,10},{12,14},{16,18},{20,22},{24,26},{28,30}} | collective-permute-start | bytes 1769480 | tf_op jit(solution)/shard_map/ppermute | solution.py:544
  (86 other events, 839.3 us)
where the time goes:
time: 357 us; the launch traced here: 354 us
  starting transfers between devices  123 us (34%)
  Pallas kernels  111 us (31%)
  waiting for transfers between devices  43.8 us (12%)
  other arithmetic  40.7 us (11%)
  local copies, waits for them, and re-layouts  33.6 us (9%)
    ppermute x24, starting transfers between devices, onward(): from_a = lax.ppermute(pair[0], 'seq', pairs_a)  72.1 us
    pallas_call x8, Pallas kernels, scan_block(): pl.pallas_call(scan_kernel, out_shape=outs, grid=(1,), in_specs=[pl.Block...  39.1 us
    ppermute x24, waiting for transfers between devices, onward(): from_a = lax.ppermute(pair[0], 'seq', pairs_a)  36.5 us
    pallas_call x1, Pallas kernels, project(): pl.pallas_call(functools.partial(project_kernel, rows=rows), out_shape=(j...  27.1 us
    pallas_call x4, Pallas kernels, output_block(): pl.pallas_call(functools.partial(output_kernel, n=n, count=count), out_sh...  26.1 us
    convert_element_type x18, other arithmetic, added(): return (a.astype(f32) + b.astype(f32)).astype(bf16)  22.5 us
    pallas_call x6, Pallas kernels, merge(): pl.pallas_call(functools.partial(merge_kernel, passing=passing), out_shap...  19 us
    ppermute x22, starting transfers between devices, onward(): from_b = lax.ppermute(pair[1], 'seq', pairs_b)  15.9 us
  transfers between devices with their start and end apart: 61, of which 14 were waited for; matrix products, arithmetic and copies ran while one was open for 15% of the time, Pallas kernels for 23%

commit v1 on v0

--- a/solution.py
+++ b/solution.py
@@ -26,9 +26,11 @@
     return v / (1.0 + jnp.exp(-v))
 
 
-def project_kernel(where, mine, other, down, weight, up, small, mixed_out, gate_out, values, held, *, rows):
+def project_kernel(where, *refs, rows, first, count):
+    mine, other, down, weight, up, small, *refs = refs
+    earlier, (mixed_out, gate_out, values, held) = refs[:-4], refs[-4:]
     half = mine.shape[2]
-    count = mine.shape[0]
+    begin = first * rows
     depth = 2 * half
     core = where[0]
     step = pl.program_id(0)
@@ -47,18 +49,22 @@
         near = pl.ds(pl.multiple_of(core * half, half), half)
         far = pl.ds(pl.multiple_of((1 - core) * half, half), half)
         masks = []
+        if earlier:
+            mixed_out[:, :begin, :] = earlier[0][...]
+            gate_out[:, :begin, :] = earlier[1][...]
         for b in range(count):
-            values[b * rows : (b + 1) * rows, near] = mine[where[2 + b], :rows, :]
-            values[b * rows : (b + 1) * rows, far] = other[where[2 + b], :rows, :]
+            source = where[2 + first + b]
+            values[b * rows : (b + 1) * rows, near] = mine[source, :rows, :]
+            values[b * rows : (b + 1) * rows, far] = other[source, :rows, :]
             for part in range(rows // span):
-                index = mine[where[2 + b], rows : rows + 16, :span].astype(f32)
+                index = mine[source, rows : rows + 16, :span].astype(f32)
                 index = index[part : part + 1].astype(jnp.int32)
                 masks.append((owner == index).astype(f32).T)
         mask = masks[0] if len(masks) == 1 else jnp.concatenate(masks, axis=0)
         full = jnp.dot(values[:, :depth], down[...], preferred_element_type=f32)
         values[:, depth:] = jnp.where(mask > 0.5, full, 0.0).astype(bf16)
         for end in range(2):
-            mixed_out[plane(end), :, ch:] = jnp.dot(
+            mixed_out[plane(end), begin:, ch:] = jnp.dot(
                 values[:, :depth], small[end], preferred_element_type=f32
             ).astype(bf16)
 
@@ -71,7 +77,8 @@
 
         def some_rows(at, carry):
             part = pl.ds(pl.multiple_of(at * chunk, chunk), chunk)
-            out[plane(end), part, dst] = jnp.dot(
+            onto = pl.ds(pl.multiple_of(begin + at * chunk, 256), chunk)
+            out[plane(end), onto, dst] = jnp.dot(
                 values[part, :], held[...], preferred_element_type=f32
             ).astype(bf16)
             return carry
@@ -79,8 +86,10 @@
         lax.fori_loop(0, values.shape[0] // chunk, some_rows, 0)
 
 
-def project(where, mine, other, down, weight, up, small, rows, ch):
-    n, _, half = mine.shape
+def project(where, mine, other, down, weight, up, small, rows, ch, count, earlier=()):
+    half = mine.shape[2]
+    first = earlier[0].shape[1] // rows if earlier else 0
+    n = first + count
     tile = min(256, ch)
     whole = lambda a: pl.BlockSpec(a.shape, lambda b, w: (0,) * a.ndim)
     striped = lambda a: pl.BlockSpec((*a.shape[:3], tile), lambda b, w: (0, 0, 0, b))
@@ -88,7 +97,7 @@
     held = lambda c: pl.BlockSpec((2, n * rows, c), lambda b, w: (0, 0, 0))
     full = 2 * half + down.shape[1]
     return pl.pallas_call(
-        functools.partial(project_kernel, rows=rows),
+        functools.partial(project_kernel, rows=rows, first=first, count=count),
         out_shape=(
             jax.ShapeDtypeStruct((2, n * rows, wide), bf16),
             jax.ShapeDtypeStruct((2, n * rows, ch), bf16),
@@ -97,18 +106,19 @@
             num_scalar_prefetch=1,
             grid=(2 * ch // tile,),
             in_specs=[
-                whole(mine), whole(other), whole(down), striped(weight), striped(up), whole(small)
+                whole(mine), whole(other), whole(down), striped(weight), striped(up), whole(small),
+                *map(whole, earlier),
             ],
             out_specs=[held(wide), held(ch)],
-            scratch_shapes=[pltpu.VMEM((n * rows, full), bf16), pltpu.VMEM((full, tile), bf16)],
+            scratch_shapes=[pltpu.VMEM((count * rows, full), bf16), pltpu.VMEM((full, tile), bf16)],
         ),
         cost_estimate=pl.CostEstimate(
-            flops=4 * n * rows * full * (ch + wide),
+            flops=4 * count * rows * full * (ch + wide),
             bytes_accessed=2 * weight.size + 4 * n * rows * (ch + wide),
             transcendentals=0,
         ),
         name="project",
-    )(where, mine, other, down, weight, up, small)
+    )(where, mine, other, down, weight, up, small, *earlier)
 
 
 def merge_kernel(where, gate_a, gate_b, came_a, came_b, gated, go_a, go_b, *, passing):
@@ -259,7 +269,7 @@
 
 def output_kernel(where, *refs, n, count):
     blocks = refs[: 2 * n * count]
-    gain, weight, out, held, sems = refs[2 * n * count :]
+    gain, weight_source, out, held, weight, sems, weight_sem = refs[2 * n * count :]
     ch = held.shape[1] // 2
     width = weight.shape[1]
     here = where[0]
@@ -283,11 +293,14 @@
                         )
 
     fetch(lambda copy: copy.start())
+    bring = pltpu.make_async_copy(weight_source, weight, weight_sem)
+    bring.start()
     fetch(lambda copy: copy.wait())
     values = held[...].astype(f32)
     squares = jnp.sum(values * values, axis=1, keepdims=True)
     held[...] = (values * gain[...]).astype(bf16)
     tile = min(256, width)
+    bring.wait()
 
     def some_columns(at, carry):
         part = pl.ds(pl.multiple_of(at * tile, tile), tile)
@@ -310,11 +323,13 @@
         grid_spec=pltpu.PrefetchScalarGridSpec(
             num_scalar_prefetch=1,
             grid=(1,),
-            in_specs=[*(pl.BlockSpec(memory_space=pl.ANY) for _ in blocks), whole(gain), whole(weight)],
+            in_specs=[*(pl.BlockSpec(memory_space=pl.ANY) for _ in blocks), whole(gain), pl.BlockSpec(memory_space=pl.ANY)],
             out_specs=pl.BlockSpec((count * BLOCK, width + LANES), lambda b, w: (0, 0)),
             scratch_shapes=[
                 pltpu.VMEM((count * BLOCK, 2 * ch), bf16),
+                pltpu.VMEM(weight.shape, bf16),
                 pltpu.SemaphoreType.DMA((count, 2)),
+                pltpu.SemaphoreType.DMA,
             ],
         ),
         cost_estimate=pl.CostEstimate(
@@ -406,9 +421,14 @@
     ).astype(f32).reshape(blocks, 1, BLOCK)
 
     order = [as_int(core), as_int(1 - odd)] + [as_int((here - b) % n) for b in range(n)]
-    mixed, gates = project(
-        jnp.stack(order), mine, other, adapter_down_maps, weight, up, small, rows, ch
-    )
+    order = jnp.stack(order)
+    projected = ()
+    versions = []
+    for count in (1, 1, n - 2) if n > 2 else (1, 1):
+        projected = project(
+            order, mine, other, adapter_down_maps, weight, up, small, rows, ch, count, projected
+        )
+        versions.append(projected)
 
     end = jnp.where(at_first, 0, 1)
     first_head = end * heads
@@ -435,9 +455,13 @@
     state = own(starting_head_state, first_head, heads, 0).reshape(ch, STATE).T
     gain = gated_norm_gain[None]
 
+    def made(step):
+        return versions[min(step * BLOCK // rows, len(versions) - 1)]
+
     def turn(step):
-        to_last = jnp.clip(step - here, 0, blocks - 1)
-        to_first = jnp.clip(step - (n - 1 - here), 0, blocks - 1)
+        limit = made(step)[0].shape[1] // BLOCK
+        to_last = jnp.clip(step - here, 0, limit - 1)
+        to_first = jnp.clip(step - (n - 1 - here), 0, limit - 1)
         return jnp.where(odd == 0, to_last, to_first), jnp.where(odd == 0, to_first, to_last)
 
     def taken(array, step):
@@ -468,7 +492,7 @@
     for step in range(last_step + 1):
         block = step - (n - 1)
         if step <= sends:
-            go = taken(mixed, step)
+            go = taken(made(step)[0], step)
             if step > 1:
                 sums, before = tied(sums, before)
             if step > 0:
@@ -480,7 +504,7 @@
         else:
             (came,) = tied(came)
         if step < n:
-            gate = taken(gates, step)
+            gate = taken(made(step)[1], step)
             if step > 0:
                 gate = added(gate[0], came[1]), added(gate[1], came[0])
             onto = gate
@@ -488,9 +512,9 @@
                 onto = gate
         if n <= step < sends:
             where = jnp.stack([as_int(at_end), *map(as_int, turn(step))])
-            onto = gate = merge(where, gates, came, gated)
+            onto = gate = merge(where, made(step)[1], came, gated)
         elif step == sends:
-            gate = (None, added(taken(gates, step)[1], came[0][:, :ch]))
+            gate = (None, added(taken(made(step)[1], step)[1], came[0][:, :ch]))
         if step >= max(n, sends):
             onto = came[1][:, -ch:], came[0][:, -ch:]
             if gated is not None:
@@ -505,12 +529,12 @@
             gated, state, tail = scan_block(
                 gate[1], go[1], tail, state, index[block], table, rate, taps
             )
-            if pending is not None:
+            if pending is not None and block + 1 < blocks:
                 state, outs[pending] = lax.optimization_barrier((state, outs[pending]))
                 pending = None
             if (block + 1) * BLOCK % rows == 0:
                 states.append(state.astype(bf16).T)
-        elif pending is not None:
+        if pending is not None and step < last_step:
             came, (outs[pending], _) = tied(came, (outs[pending], state))
             pending = None
         done = step - (2 * n - 2)
@@ -520,10 +544,10 @@
                 for _ in range(2):
                     needed.append(went[b])
                     needed.extend(arrived[b + n - 1 + k][1 - k % 2] for k in range(1, n))
+            pending = len(outs)
             outs.append(
                 output_block(as_int(here)[None], needed, n, gain, output_projection_weight, ch)
             )
-            pending = len(outs) - 1
 
     landed = [jnp.where(at_first, states[0], states[n - 1])]
     for k in range(1, n):
@@ -537,13 +561,19 @@
     chips = shards // 2
     chip = shard // 2
     if chips == 2:
-        total = None
-        for t in range(shards):
+        keep = jnp.where(core == 0, outs[0], outs[1])
+        give = jnp.where(core == 0, outs[1], outs[0])
+        both = added(keep, lax.ppermute(give, "tensor", swap))
+        came = lax.ppermute(both, "tensor", [(2, 0), (3, 1)])
+        total = both.astype(f32) + came.astype(f32)
+        for t in range(2, shards):
             give = [(j, j ^ 1) for j in range(shards) if j % 2 != t % 2]
             both = added(outs[t], lax.ppermute(outs[t], "tensor", give))
             came = lax.ppermute(both, "tensor", [(t ^ 2, t)])
             both = both.astype(f32) + came.astype(f32)
-            total = both if total is None else jnp.where(shard == t, both, total)
+            total = jnp.where(shard == t, both, total)
+            if t == shards - 2:
+                total = lax.optimization_barrier(total)
     else:
         halves = []
         for k in range(chips):

time: 357 us -> 348 us (0.975)
  waiting for transfers between devices: 43.8 us -> 24.9 us
  Pallas kernels: 111 us -> 128 us
  starting transfers between devices: 123 us -> 114 us
    ppermute x24, waiting for transfers between devices: 36.5 us -> 13.5 us  [onward(): from_a = lax.ppermute(pair[0], 'seq', pairs_a)]
    pallas_call x1 -> x3, Pallas kernels: 27.1 us -> 45.5 us  [project(): pl.pallas_call(functools.partial(project_kernel, rows=rows, first=first,...]
    ppermute x24, starting transfers between devices: 72.1 us -> 65.7 us  [onward(): from_a = lax.ppermute(pair[0], 'seq', pairs_a)]
    ppermute x4 -> x2, waiting for transfers between devices: 5.21 us -> 11.3 us  [per_device(): came = lax.ppermute(both, 'tensor', [(t ^ 2, t)])]
    ppermute x4 -> x2, starting transfers between devices: 8.69 us -> 4.44 us  [per_device(): both = added(outs[t], lax.ppermute(outs[t], 'tensor', give))]
    ppermute x4 -> x2, starting transfers between devices: 8.61 us -> 5.16 us  [per_device(): came = lax.ppermute(both, 'tensor', [(t ^ 2, t)])]
    unnamed x108 -> x110, local copies, waits for them, and re-layouts: 8.37 us -> 9.98 us
    convert_element_type x18 -> x17, other arithmetic: 22.5 us -> 23.2 us  [added(): return (a.astype(f32) + b.astype(f32)).astype(bf16)]
  transfers between devices with their start and end apart: 61 -> 59, of which waited for: 14 -> 10; matrix products, arithmetic and copies ran while one was open for 15% -> 17% of each run, Pallas kernels for 23% -> 33%
where the time goes in v1:
time: 348 us; the launch traced here: 345 us
  Pallas kernels  128 us (37%)
  starting transfers between devices  114 us (33%)
  other arithmetic  39.2 us (11%)
  local copies, waits for them, and re-layouts  36.7 us (11%)
  waiting for transfers between devices  24.9 us (7%)
    ppermute x24, starting transfers between devices, onward(): from_a = lax.ppermute(pair[0], 'seq', pairs_a)  65.7 us
    pallas_call x3, Pallas kernels, project(): pl.pallas_call(functools.partial(project_kernel, rows=rows, first=first,...  45.5 us
    pallas_call x8, Pallas kernels, scan_block(): pl.pallas_call(scan_kernel, out_shape=outs, grid=(1,), in_specs=[pl.Block...  39.1 us
    pallas_call x4, Pallas kernels, output_block(): pl.pallas_call(functools.partial(output_kernel, n=n, count=count), out_sh...  24.2 us
    convert_element_type x17, other arithmetic, added(): return (a.astype(f32) + b.astype(f32)).astype(bf16)  23.2 us
    pallas_call x6, Pallas kernels, merge(): pl.pallas_call(functools.partial(merge_kernel, passing=passing), out_shap...  19.1 us
    ppermute x22, starting transfers between devices, onward(): from_b = lax.ppermute(pair[1], 'seq', pairs_b)  17.7 us
    reshape x2, local copies, waits for them, and re-layouts, by_pair(): split = array.reshape(array.shape[0] // 16, 16, 2, array.shape[2])  13.7 us
  transfers between devices with their start and end apart: 59, of which 10 were waited for; matrix products, arithmetic and copies ran while one was open for 17% of the time, Pallas kernels for 33%

profile of v1, /device:TPU:0, one launch (start us, length us, event | category | flops | bytes accessed | tf_op | source)
XLA Modules:
  0.0 344.9 jit_solution(3944130441271883334)
XLA Ops:
  13.7 11.5 %copy.48 = bf16[64,16,2,2048]{3,1,2,0:T(8,128)(2,1)} copy(bf16[64,16,2,2048]{3,2,1,0:T(2,128)(2,1)} %bitcast.188) | data formatting | bytes 16777216 | tf_op jit(solution)/shard_map/reshape | solution.py:403
  37.6 12.4 %project.3 = (bf16[2,256,1408]{2,1,0:T(8,128)(2,1)}, bf16[2,256,1024]{2,1,0:T(8,128)(2,1)}) custom-call(s32[6]{0:T(128)} %stack.136.where, bf16[4,272,512]{2,1,0:T(8,128)(2,1)} %copy-done.6, bf16[4,272,512]{2,1,0:T(8,128)(2,1)} %copy-done.16, bf16[1024,256]{1,0:T(8,128)(2,1)} %refs_2_.5, bf16[64,2,16,2048]{3,2,1,0:T(8,128)(2,1)} %bitcast.182, ...), custom_call_target="tpu_custom_call" | custom-call | flops 3187671040 | bytes 10878976 | tf_op jit(solution)/shard_map/project/pallas_call | solution.py:99
  52.2 5.2 %collective-permute-start.6 = (bf16[128,1408]{1,0:T(8,128)(2,1)}, bf16[128,1408]{1,0:T(8,128)(2,1)S(1)}, u32[]{:S(2)}, u32[]{:S(2)}) collective-permute-start(bf16[128,1408]{1,0:T(8,128)(2,1)} %get-tuple-element.221), channel_id=1, source_target_pairs={{0,4},{4,0},{8,12},{12,8},{1,5},{5,1},{9,13},{13,9},{2,6},{6,2},{1... | collective-permute-start | bytes 1081352 | tf_op jit(solution)/shard_map/ppermute | solution.py:478
  68.7 4.1 %collective-permute-start.10 = (bf16[128,1408]{1,0:T(8,128)(2,1)}, bf16[128,1408]{1,0:T(8,128)(2,1)S(1)}, u32[]{:S(2)}, u32[]{:S(2)}) collective-permute-start(bf16[128,1408]{1,0:T(8,128)(2,1)} %get-tuple-element.219), channel_id=1, source_target_pairs={{0,4},{4,0},{8,12},{12,8},{1,5},{5,1},{9,13},{13,9},{2,6},{6,2},{1... | collective-permute-start | bytes 1081352 | tf_op jit(solution)/shard_map/ppermute | solution.py:478
  73.9 14.2 %project.4 = (bf16[2,512,1408]{2,1,0:T(8,128)(2,1)}, bf16[2,512,1024]{2,1,0:T(8,128)(2,1)}) custom-call(s32[6]{0:T(128)} %stack.136.where, bf16[4,272,512]{2,1,0:T(8,128)(2,1)} %copy-done.6, bf16[4,272,512]{2,1,0:T(8,128)(2,1)} %copy-done.16, bf16[1024,256]{1,0:T(8,128)(2,1)} %refs_2_.5, bf16[64,2,16,2048]{3,2,1,0:T(8,128)(2,1)} %bitcast.183, ...), custom_call_target="tpu_custom_call" | custom-call | flops 3187671040 | bytes 13369344 | tf_op jit(solution)/shard_map/project/pallas_call | solution.py:99
  100.6 3.7 %collective-permute-start.12 = (bf16[128,1024]{1,0:T(8,128)(2,1)S(1)}, bf16[128,1024]{1,0:T(8,128)(2,1)S(1)}, u32[]{:S(2)}, u32[]{:S(2)}) collective-permute-start(bf16[128,1024]{1,0:T(8,128)(2,1)S(1)} %get-tuple-element.213), channel_id=1, source_target_pairs={{0,4},{4,0},{8,12},{12,8},{1,5},{5,1},{9,13},{13,9},{2,6},{6,2},{1... | collective-permute-start | bytes 786440 | tf_op jit(solution)/shard_map/ppermute | solution.py:478
  112.8 18.9 %project.5 = (bf16[2,1024,1408]{2,1,0:T(8,128)(2,1)}, bf16[2,1024,1024]{2,1,0:T(8,128)(2,1)}) custom-call(s32[6]{0:T(128)} %stack.136.where, bf16[4,272,512]{2,1,0:T(8,128)(2,1)} %copy-done.6, bf16[4,272,512]{2,1,0:T(8,128)(2,1)} %copy-done.16, bf16[1024,256]{1,0:T(8,128)(2,1)} %refs_2_.5, bf16[64,2,16,2048]{3,2,1,0:T(8,128)(2,1)} %bitcast.184, ...), custom_call_target="tpu_custom_call" | custom-call | flops 6375342080 | bytes 18350080 | tf_op jit(solution)/shard_map/project/pallas_call | solution.py:99
  140.8 4.8 %scan_block.8 = (bf16[128,1024]{1,0:T(8,128)(2,1)}, f32[128,1024]{1,0:T(8,128)}, f32[8,1280]{1,0:T(8,128)}) custom-call(bf16[128,1024]{1,0:T(8,128)(2,1)} %copy-done.38, bf16[128,1408]{1,0:T(8,128)(2,1)} %copy-done.37, f32[8,1280]{1,0:T(8,128)} %fusion.40.tail, f32[128,1024]{1,0:T(8,128)} %bitcast.191, f32[1,128]{1,0:T(1,128)} %get-tuple-element.245.index, ...), custom_call_target="tpu_custom_call" | custom-call | flops 134217728 | bytes 2097152 | tf_op jit(solution)/shard_map/scan_block/pallas_call | solution.py:250
  158.3 4.9 %scan_block.9 = (bf16[128,1024]{1,0:T(8,128)(2,1)}, f32[128,1024]{1,0:T(8,128)}, f32[8,1280]{1,0:T(8,128)}) custom-call(bf16[128,2048]{1,0:T(8,128)(2,1)} %get-tuple-element.120.gates, bf16[128,1408]{1,0:T(8,128)(2,1)} %copy-done.33, f32[8,1280]{1,0:T(8,128)} %get-tuple-element.126.tail, f32[128,1024]{1,0:T(8,128)} %get-tuple-element.127.state, ...), custom_call_target="tpu_custom_call" | custom-call | flops 134217728 | bytes 2097152 | tf_op jit(solution)/shard_map/scan_block/pallas_call | solution.py:250
  176.5 4.9 %scan_block.10 = (bf16[128,1024]{1,0:T(8,128)(2,1)}, f32[128,1024]{1,0:T(8,128)}, f32[8,1280]{1,0:T(8,128)}) custom-call(bf16[128,2048]{1,0:T(8,128)(2,1)} %get-tuple-element.130.gates, bf16[128,1408]{1,0:T(8,128)(2,1)} %copy-done.34, f32[8,1280]{1,0:T(8,128)} %get-tuple-element.135.tail, f32[128,1024]{1,0:T(8,128)} %get-tuple-element.136.state, ...), custom_call_target="tpu_custom_call" | custom-call | flops 134217728 | bytes 2097152 | tf_op jit(solution)/shard_map/scan_block/pallas_call | solution.py:250
  198.1 4.9 %scan_block.11 = (bf16[128,1024]{1,0:T(8,128)(2,1)}, f32[128,1024]{1,0:T(8,128)}, f32[8,1280]{1,0:T(8,128)}) custom-call(bf16[128,2048]{1,0:T(8,128)(2,1)} %get-tuple-element.139.gates, bf16[128,1408]{1,0:T(8,128)(2,1)} %copy-done.35, f32[8,1280]{1,0:T(8,128)} %get-tuple-element.144.tail, f32[128,1024]{1,0:T(8,128)} %get-tuple-element.145.state, ...), custom_call_target="tpu_custom_call" | custom-call | flops 134217728 | bytes 2097152 | tf_op jit(solution)/shard_map/scan_block/pallas_call | solution.py:250
  212.4 3.7 %collective-permute-start.38 = (bf16[128,1408]{1,0:T(8,128)(2,1)S(1)}, bf16[128,1408]{1,0:T(8,128)(2,1)S(1)}, u32[]{:S(2)}, u32[]{:S(2)}) collective-permute-start(bf16[128,1408]{1,0:T(8,128)(2,1)S(1)} %get-tuple-element.195), channel_id=1, source_target_pairs={{0,4},{4,0},{8,12},{12,8},{1,5},{5,1},{9,13},{13,9},{2,6},{6,2},{1... | collective-permute-start | bytes 1081352 | tf_op jit(solution)/shard_map/ppermute | solution.py:478
  217.5 4.9 %scan_block.12 = (bf16[128,1024]{1,0:T(8,128)(2,1)}, f32[128,1024]{1,0:T(8,128)}, f32[8,1280]{1,0:T(8,128)}) custom-call(bf16[128,2048]{1,0:T(8,128)(2,1)} %get-tuple-element.148.gates, bf16[128,1408]{1,0:T(8,128)(2,1)} %copy-done.32, f32[8,1280]{1,0:T(8,128)} %get-tuple-element.153.tail, f32[128,1024]{1,0:T(8,128)} %get-tuple-element.154.state, ...), custom_call_target="tpu_custom_call" | custom-call | flops 134217728 | bytes 2097152 | tf_op jit(solution)/shard_map/scan_block/pallas_call | solution.py:250
  236.2 4.9 %scan_block.13 = (bf16[128,1024]{1,0:T(8,128)(2,1)}, f32[128,1024]{1,0:T(8,128)}, f32[8,1280]{1,0:T(8,128)}) custom-call(bf16[128,2048]{1,0:T(8,128)(2,1)} %get-tuple-element.157.gates, bf16[128,1408]{1,0:T(8,128)(2,1)} %copy-done.36, f32[8,1280]{1,0:T(8,128)} %get-tuple-element.162.tail, f32[128,1024]{1,0:T(8,128)} %get-tuple-element.163.state, ...), custom_call_target="tpu_custom_call" | custom-call | flops 134217728 | bytes 2097152 | tf_op jit(solution)/shard_map/scan_block/pallas_call | solution.py:250
  241.1 6.0 %output_block.4 = bf16[256,1152]{1,0:T(8,128)(2,1)} custom-call(s32[1]{0:T(128)} %bitcast.where, bf16[128,2048]{1,0:T(8,128)(2,1)} %get-tuple-element.119.refs_0_.refs_4_, bf16[128,2048]{1,0:T(8,128)(2,1)} %copy-done.10, bf16[128,2048]{1,0:T(8,128)(2,1)} %copy-done.12, bf16[128,2048]{1,0:T(8,128)(2,1)} %copy-done.2, ...), custom_call_target="tpu_custom_call" | custom-call | flops 1073741824 | bytes 6291456 | tf_op jit(solution)/shard_map/output_block/pallas_call | solution.py:320
  253.0 7.1 %collective-permute-start.56 = (bf16[1024,128]{0,1:T(8,128)(2,1)}, bf16[1024,128]{0,1:T(8,128)(2,1)}, u32[]{:S(2)}, u32[]{:S(2)}) collective-permute-start(bf16[1024,128]{0,1:T(8,128)(2,1)} %get-tuple-element.226), channel_id=1, source_target_pairs={{0,4},{12,8},{1,5},{13,9},{2,6},{14,10},{3,7},{15,11},{16,20},{28,... | collective-permute-start | bytes 786440 | tf_op jit(solution)/shard_map/ppermute | solution.py:555
  264.3 4.9 %scan_block.14 = (bf16[128,1024]{1,0:T(8,128)(2,1)}, f32[128,1024]{1,0:T(8,128)}, f32[8,1280]{1,0:T(8,128)}) custom-call(bf16[128,2048]{1,0:T(8,128)(2,1)} %get-tuple-element.165.gates, bf16[128,1408]{1,0:T(8,128)(2,1)} %get-tuple-element.193.sums, f32[8,1280]{1,0:T(8,128)} %get-tuple-element.166.tail, f32[128,1024]{1,0:T(8,128)} %get-tuple-element.168.state, ...), custom_call_target="tpu_custom_call" | custom-call | flops 134217728 | bytes 2097152 | tf_op jit(solution)/shard_map/scan_block/pallas_call | solution.py:250
  272.3 4.8 %scan_block.15 = (bf16[128,1024]{1,0:T(8,128)(2,1)}, f32[128,1024]{1,0:T(8,128)}, f32[8,1280]{1,0:T(8,128)}) custom-call(bf16[128,1024]{1,0:T(8,128)(2,1)} %fusion.26.gates, bf16[128,1408]{1,0:T(8,128)(2,1)} %get-tuple-element.192.sums, f32[8,1280]{1,0:T(8,128)} %get-tuple-element.174.tail, f32[128,1024]{1,0:T(8,128)} %get-tuple-element.175.state, ...), custom_call_target="tpu_custom_call" | custom-call | flops 134217728 | bytes 2097152 | tf_op jit(solution)/shard_map/scan_block/pallas_call | solution.py:250
  282.0 6.0 %output_block.5 = bf16[256,1152]{1,0:T(8,128)(2,1)} custom-call(s32[1]{0:T(128)} %bitcast.where, bf16[128,2048]{1,0:T(8,128)(2,1)} %get-tuple-element.138.refs_0_.refs_4_, bf16[128,2048]{1,0:T(8,128)(2,1)} %copy-done.2, bf16[128,2048]{1,0:T(8,128)(2,1)} %copy-done.13, bf16[128,2048]{1,0:T(8,128)(2,1)} %copy-done.4, ...), custom_call_target="tpu_custom_call" | custom-call | flops 1073741824 | bytes 6291456 | tf_op jit(solution)/shard_map/output_block/pallas_call | solution.py:320
  294.6 3.9 %collective-permute-start.47 = (bf16[128,1024]{1,0:T(8,128)(2,1)S(1)}, bf16[128,1024]{1,0:T(8,128)(2,1)S(1)}, u32[]{:S(2)}, u32[]{:S(2)}) collective-permute-start(bf16[128,1024]{1,0:T(8,128)(2,1)S(1)} %collective-permute-done.45.refs_2_.refs_6_), channel_id=1, source_target_pairs={{0,4},{4,0},{8,12},{12,8},{1,5},{5,1},{9,13},{13,9},{2,6},{6,2},{1... | collective-permute-start | bytes 786440 | tf_op jit(solution)/shard_map/ppermute | solution.py:478
  301.5 6.0 %output_block.6 = bf16[256,1152]{1,0:T(8,128)(2,1)} custom-call(s32[1]{0:T(128)} %bitcast.where, bf16[128,2048]{1,0:T(8,128)(2,1)} %get-tuple-element.156.refs_0_.refs_4_, bf16[128,2048]{1,0:T(8,128)(2,1)} %copy-done.4, bf16[128,2048]{1,0:T(8,128)(2,1)} %copy-done.21, bf16[128,1024]{1,0:T(8,128)(2,1)} %copy-done.19, ...), custom_call_target="tpu_custom_call" | custom-call | flops 1073741824 | bytes 6291456 | tf_op jit(solution)/shard_map/output_block/pallas_call | solution.py:320
  314.9 6.3 %output_block.7 = bf16[256,1152]{1,0:T(8,128)(2,1)} custom-call(s32[1]{0:T(128)} %bitcast.where, bf16[128,1024]{1,0:T(8,128)(2,1)} %copy-done.25, bf16[128,1024]{1,0:T(8,128)(2,1)} %copy-done.19, bf16[128,1024]{1,0:T(8,128)(2,1)} %copy-done.39, bf16[128,1024]{1,0:T(8,128)(2,1)} %copy-done.40, bf16[128,1024]{1,0:T(8,128)(2,1)} %copy-done.25, ...), custom_call_target="tpu_custom_call" | custom-call | flops 1073741824 | bytes 6291456 | tf_op jit(solution)/shard_map/output_block/pallas_call | solution.py:320
  325.6 4.5 %collective-permute-start.53 = (bf16[256,1152]{1,0:T(8,128)(2,1)S(1)}, bf16[256,1152]{1,0:T(8,128)(2,1)S(1)}, u32[]{:S(2)}, u32[]{:S(2)}) collective-permute-start(bf16[256,1152]{1,0:T(8,128)(2,1)S(1)} %add_convert_fusion.1), channel_id=1, source_target_pairs={{0,2},{4,6},{8,10},{12,14},{16,18},{20,22},{24,26},{28,30}} | collective-permute-start | bytes 1769480 | tf_op jit(solution)/shard_map/ppermute | solution.py:572
  332.1 11.3 %collective-permute-done.53 = bf16[256,1152]{1,0:T(8,128)(2,1)S(1)} collective-permute-done((bf16[256,1152]{1,0:T(8,128)(2,1)S(1)}, bf16[256,1152]{1,0:T(8,128)(2,1)S(1)}, u32[]{:S(2)}, u32[]{:S(2)}) %collective-permute-start.53) | collective-permute-done | bytes 589856 | tf_op jit(solution)/shard_map/ppermute | solution.py:572
  (292 shorter events, 179.2 us)
Async XLA Ops:
  3.6 25.3 %collective-permute-start = (bf16[272,512]{1,0:T(8,128)(2,1)}, bf16[272,512]{1,0:T(8,128)(2,1)}, u32[]{:S(2)}, u32[]{:S(2)}) collective-permute-start(bf16[272,512]{1,0:T(8,128)(2,1)} %get-tuple-element.235), channel_id=1, source_target_pairs={{0,4},{4,8},{8,12},{12,0},{1,5},{5,9},{9,13},{13,1},{2,6},{6,10},{... | collective-permute-start | bytes 835592 | tf_op jit(solution)/shard_map/ppermute | solution.py:400
  6.7 22.3 %collective-permute-start.1 = (bf16[272,512]{1,0:T(8,128)(2,1)S(1)}, bf16[272,512]{1,0:T(8,128)(2,1)}, u32[]{:S(2)}, u32[]{:S(2)}) collective-permute-start(bf16[272,512]{1,0:T(8,128)(2,1)S(1)} %get-tuple-element.236), channel_id=1, source_target_pairs={{0,8},{4,12},{8,0},{12,4},{1,9},{5,13},{9,1},{13,5},{2,10},{6,14},... | collective-permute-start | bytes 835592 | tf_op jit(solution)/shard_map/ppermute | solution.py:400
  9.3 19.7 %collective-permute-start.2 = (bf16[272,512]{1,0:T(8,128)(2,1)S(1)}, bf16[272,512]{1,0:T(8,128)(2,1)}, u32[]{:S(2)}, u32[]{:S(2)}) collective-permute-start(bf16[272,512]{1,0:T(8,128)(2,1)S(1)} %get-tuple-element.237), channel_id=1, source_target_pairs={{0,12},{4,0},{8,4},{12,8},{1,13},{5,1},{9,5},{13,9},{2,14},{6,2},{... | collective-permute-start | bytes 835592 | tf_op jit(solution)/shard_map/ppermute | solution.py:400
  62.5 25.6 %collective-permute-start.4 = (bf16[128,1024]{1,0:T(8,128)(2,1)}, bf16[128,1024]{1,0:T(8,128)(2,1)}, u32[]{:S(2)}, u32[]{:S(2)}) collective-permute-start(bf16[128,1024]{1,0:T(8,128)(2,1)} %get-tuple-element.231), channel_id=1, source_target_pairs={{0,4},{4,0},{8,12},{12,8},{1,5},{5,1},{9,13},{13,9},{2,6},{6,2},{1... | collective-permute-start | bytes 786440 | tf_op jit(solution)/shard_map/ppermute | solution.py:478
  65.1 22.9 %collective-permute-start.5 = (bf16[128,1024]{1,0:T(8,128)(2,1)}, bf16[128,1024]{1,0:T(8,128)(2,1)}, u32[]{:S(2)}, u32[]{:S(2)}) collective-permute-start(bf16[128,1024]{1,0:T(8,128)(2,1)} %get-tuple-element.230), channel_id=1, source_target_pairs={{4,8},{8,4},{5,9},{9,5},{6,10},{10,6},{7,11},{11,7},{20,24},{24,20... | collective-permute-start | bytes 786440 | tf_op jit(solution)/shard_map/ppermute | solution.py:479
  68.7 24.6 %collective-permute-start.10 = (bf16[128,1408]{1,0:T(8,128)(2,1)}, bf16[128,1408]{1,0:T(8,128)(2,1)S(1)}, u32[]{:S(2)}, u32[]{:S(2)}) collective-permute-start(bf16[128,1408]{1,0:T(8,128)(2,1)} %get-tuple-element.219), channel_id=1, source_target_pairs={{0,4},{4,0},{8,12},{12,8},{1,5},{5,1},{9,13},{13,9},{2,6},{6,2},{1... | collective-permute-start | bytes 1081352 | tf_op jit(solution)/shard_map/ppermute | solution.py:478
  72.9 20.5 %collective-permute-start.11 = (bf16[128,1408]{1,0:T(8,128)(2,1)S(1)}, bf16[128,1408]{1,0:T(8,128)(2,1)S(1)}, u32[]{:S(2)}, u32[]{:S(2)}) collective-permute-start(bf16[128,1408]{1,0:T(8,128)(2,1)S(1)} %get-tuple-element.218), channel_id=1, source_target_pairs={{4,8},{8,4},{5,9},{9,5},{6,10},{10,6},{7,11},{11,7},{20,24},{24,20... | collective-permute-start | bytes 1081352 | tf_op jit(solution)/shard_map/ppermute | solution.py:479
  100.6 31.0 %collective-permute-start.12 = (bf16[128,1024]{1,0:T(8,128)(2,1)S(1)}, bf16[128,1024]{1,0:T(8,128)(2,1)S(1)}, u32[]{:S(2)}, u32[]{:S(2)}) collective-permute-start(bf16[128,1024]{1,0:T(8,128)(2,1)S(1)} %get-tuple-element.213), channel_id=1, source_target_pairs={{0,4},{4,0},{8,12},{12,8},{1,5},{5,1},{9,13},{13,9},{2,6},{6,2},{1... | collective-permute-start | bytes 786440 | tf_op jit(solution)/shard_map/ppermute | solution.py:478
  104.3 27.3 %collective-permute-start.13 = (bf16[128,1024]{1,0:T(8,128)(2,1)S(1)}, bf16[128,1024]{1,0:T(8,128)(2,1)S(1)}, u32[]{:S(2)}, u32[]{:S(2)}) collective-permute-start(bf16[128,1024]{1,0:T(8,128)(2,1)S(1)} %get-tuple-element.212), channel_id=1, source_target_pairs={{4,8},{8,4},{5,9},{9,5},{6,10},{10,6},{7,11},{11,7},{20,24},{24,20... | collective-permute-start | bytes 786440 | tf_op jit(solution)/shard_map/ppermute | solution.py:479
  108.4 23.3 %collective-permute-start.18 = (bf16[128,1408]{1,0:T(8,128)(2,1)S(1)}, bf16[128,1408]{1,0:T(8,128)(2,1)S(1)}, u32[]{:S(2)}, u32[]{:S(2)}) collective-permute-start(bf16[128,1408]{1,0:T(8,128)(2,1)S(1)} %get-tuple-element.207), channel_id=1, source_target_pairs={{0,4},{4,0},{8,12},{12,8},{1,5},{5,1},{9,13},{13,9},{2,6},{6,2},{1... | collective-permute-start | bytes 1081352 | tf_op jit(solution)/shard_map/ppermute | solution.py:478
  112.1 19.6 %collective-permute-start.19 = (bf16[128,1408]{1,0:T(8,128)(2,1)S(1)}, bf16[128,1408]{1,0:T(8,128)(2,1)S(1)}, u32[]{:S(2)}, u32[]{:S(2)}) collective-permute-start(bf16[128,1408]{1,0:T(8,128)(2,1)S(1)} %get-tuple-element.206.sums), channel_id=1, source_target_pairs={{4,8},{8,4},{5,9},{9,5},{6,10},{10,6},{7,11},{11,7},{20,24},{24,20... | collective-permute-start | bytes 1081352 | tf_op jit(solution)/shard_map/ppermute | solution.py:479
  133.0 20.4 %collective-permute-start.22 = (bf16[128,1408]{1,0:T(8,128)(2,1)S(1)}, bf16[128,1408]{1,0:T(8,128)(2,1)S(1)}, u32[]{:S(2)}, u32[]{:S(2)}) collective-permute-start(bf16[128,1408]{1,0:T(8,128)(2,1)S(1)} %get-tuple-element.203), channel_id=1, source_target_pairs={{0,4},{4,0},{8,12},{12,8},{1,5},{5,1},{9,13},{13,9},{2,6},{6,2},{1... | collective-permute-start | bytes 1081352 | tf_op jit(solution)/shard_map/ppermute | solution.py:478
  134.7 18.7 %collective-permute-start.23 = (bf16[128,1408]{1,0:T(8,128)(2,1)S(1)}, bf16[128,1408]{1,0:T(8,128)(2,1)S(1)}, u32[]{:S(2)}, u32[]{:S(2)}) collective-permute-start(bf16[128,1408]{1,0:T(8,128)(2,1)S(1)} %get-tuple-element.202.sums), channel_id=1, source_target_pairs={{4,8},{8,4},{5,9},{9,5},{6,10},{10,6},{7,11},{11,7},{20,24},{24,20... | collective-permute-start | bytes 1081352 | tf_op jit(solution)/shard_map/ppermute | solution.py:479
  154.7 17.8 %collective-permute-start.26 = (bf16[128,1408]{1,0:T(8,128)(2,1)S(1)}, bf16[128,1408]{1,0:T(8,128)(2,1)S(1)}, u32[]{:S(2)}, u32[]{:S(2)}) collective-permute-start(bf16[128,1408]{1,0:T(8,128)(2,1)S(1)} %get-tuple-element.201), channel_id=1, source_target_pairs={{0,4},{4,0},{8,12},{12,8},{1,5},{5,1},{9,13},{13,9},{2,6},{6,2},{1... | collective-permute-start | bytes 1081352 | tf_op jit(solution)/shard_map/ppermute | solution.py:478
  173.8 18.3 %collective-permute-start.30 = (bf16[128,1408]{1,0:T(8,128)(2,1)S(1)}, bf16[128,1408]{1,0:T(8,128)(2,1)S(1)}, u32[]{:S(2)}, u32[]{:S(2)}) collective-permute-start(bf16[128,1408]{1,0:T(8,128)(2,1)S(1)} %get-tuple-element.199), channel_id=1, source_target_pairs={{0,4},{4,0},{8,12},{12,8},{1,5},{5,1},{9,13},{13,9},{2,6},{6,2},{1... | collective-permute-start | bytes 1081352 | tf_op jit(solution)/shard_map/ppermute | solution.py:478
  228.1 18.9 %collective-permute-start.36 = (bf16[128,2048]{1,0:T(8,128)(2,1)}, bf16[128,2048]{1,0:T(8,128)(2,1)S(1)}, u32[]{:S(2)}, u32[]{:S(2)}) collective-permute-start(bf16[128,2048]{1,0:T(8,128)(2,1)} %get-tuple-element.156.refs_0_.refs_4_), channel_id=1, source_target_pairs={{0,4},{4,0},{8,12},{12,8},{1,5},{5,1},{9,13},{13,9},{2,6},{6,2},{1... | collective-permute-start | bytes 1572872 | tf_op jit(solution)/shard_map/ppermute | solution.py:478
  234.2 27.9 %collective-permute-start.42 = (bf16[128,1408]{1,0:T(8,128)(2,1)}, bf16[128,1408]{1,0:T(8,128)(2,1)}, u32[]{:S(2)}, u32[]{:S(2)}) collective-permute-start(bf16[128,1408]{1,0:T(8,128)(2,1)} %fusion.8), channel_id=1, source_target_pairs={{0,4},{4,0},{8,12},{12,8},{1,5},{5,1},{9,13},{13,9},{2,6},{6,2},{1... | collective-permute-start | bytes 1081352 | tf_op jit(solution)/shard_map/ppermute | solution.py:478
  251.4 17.8 %collective-permute-start.40 = (bf16[128,2048]{1,0:T(8,128)(2,1)}, bf16[128,2048]{1,0:T(8,128)(2,1)S(1)}, u32[]{:S(2)}, u32[]{:S(2)}) collective-permute-start(bf16[128,2048]{1,0:T(8,128)(2,1)} %get-tuple-element.170.refs_8_.refs_12_), channel_id=1, source_target_pairs={{0,4},{4,0},{8,12},{12,8},{1,5},{5,1},{9,13},{13,9},{2,6},{6,2},{1... | collective-permute-start | bytes 1572872 | tf_op jit(solution)/shard_map/ppermute | solution.py:478
  251.5 17.8 %collective-permute-start.41 = (bf16[128,2048]{1,0:T(8,128)(2,1)}, bf16[128,2048]{1,0:T(8,128)(2,1)S(1)}, u32[]{:S(2)}, u32[]{:S(2)}) collective-permute-start(bf16[128,2048]{1,0:T(8,128)(2,1)} %get-tuple-element.165.gates), channel_id=1, source_target_pairs={{4,8},{8,4},{5,9},{9,5},{6,10},{10,6},{7,11},{11,7},{20,24},{24,20... | collective-permute-start | bytes 1572872 | tf_op jit(solution)/shard_map/ppermute | solution.py:479
  253.0 45.5 %collective-permute-start.56 = (bf16[1024,128]{0,1:T(8,128)(2,1)}, bf16[1024,128]{0,1:T(8,128)(2,1)}, u32[]{:S(2)}, u32[]{:S(2)}) collective-permute-start(bf16[1024,128]{0,1:T(8,128)(2,1)} %get-tuple-element.226), channel_id=1, source_target_pairs={{0,4},{12,8},{1,5},{13,9},{2,6},{14,10},{3,7},{15,11},{16,20},{28,... | collective-permute-start | bytes 786440 | tf_op jit(solution)/shard_map/ppermute | solution.py:555
  260.1 39.7 %collective-permute-start.57 = (bf16[1024,128]{0,1:T(8,128)(2,1)}, bf16[1024,128]{0,1:T(8,128)(2,1)}, u32[]{:S(2)}, u32[]{:S(2)}) collective-permute-start(bf16[1024,128]{0,1:T(8,128)(2,1)} %get-tuple-element.227), channel_id=1, source_target_pairs={{0,8},{12,4},{1,9},{13,5},{2,10},{14,6},{3,11},{15,7},{16,24},{28,... | collective-permute-start | bytes 786440 | tf_op jit(solution)/shard_map/ppermute | solution.py:555
  278.3 21.5 %collective-permute-start.58 = (bf16[1024,128]{0,1:T(8,128)(2,1)S(1)}, bf16[1024,128]{0,1:T(8,128)(2,1)S(1)}, u32[]{:S(2)}, u32[]{:S(2)}) collective-permute-start(bf16[1024,128]{0,1:T(8,128)(2,1)S(1)} %get-tuple-element.225), channel_id=1, source_target_pairs={{0,12},{12,0},{1,13},{13,1},{2,14},{14,2},{3,15},{15,3},{16,28},{2... | collective-permute-start | bytes 786440 | tf_op jit(solution)/shard_map/ppermute | solution.py:555
  312.1 20.0 %collective-permute-start.55 = (bf16[256,1152]{1,0:T(8,128)(2,1)S(1)}, bf16[256,1152]{1,0:T(8,128)(2,1)S(1)}, u32[]{:S(2)}, u32[]{:S(2)}) collective-permute-start(bf16[256,1152]{1,0:T(8,128)(2,1)S(1)} %add_convert_fusion), channel_id=1, source_target_pairs={{2,0},{3,1},{6,4},{7,5},{10,8},{11,9},{14,12},{15,13},{18,16},{19,... | collective-permute-start | bytes 1769480 | tf_op jit(solution)/shard_map/ppermute | solution.py:567
  325.6 17.8 %collective-permute-start.53 = (bf16[256,1152]{1,0:T(8,128)(2,1)S(1)}, bf16[256,1152]{1,0:T(8,128)(2,1)S(1)}, u32[]{:S(2)}, u32[]{:S(2)}) collective-permute-start(bf16[256,1152]{1,0:T(8,128)(2,1)S(1)} %add_convert_fusion.1), channel_id=1, source_target_pairs={{0,2},{4,6},{8,10},{12,14},{16,18},{20,22},{24,26},{28,30}} | collective-permute-start | bytes 1769480 | tf_op jit(solution)/shard_map/ppermute | solution.py:572
  (85 other events, 806.2 us)

commit v2 on v1

--- a/solution.py
+++ b/solution.py
@@ -28,15 +28,15 @@
 
 def project_kernel(where, *refs, rows, first, count):
     mine, other, down, weight, up, small, *refs = refs
-    earlier, (mixed_out, gate_out, values, held) = refs[:-4], refs[-4:]
+    earlier, (mixed_out, gate_out, values) = refs[:-3], refs[-3:]
     half = mine.shape[2]
     begin = first * rows
     depth = 2 * half
     core = where[0]
     step = pl.program_id(0)
-    ch = gate_out.shape[2]
-    tile = held.shape[1]
-    per_end = ch // tile
+    tile = gate_out.shape[2]
+    per_end = pl.num_programs(0) // 2
+    ch = mixed_out.shape[2] - small.shape[2]
 
     def plane(end):
         return jnp.where(where[1] == 1, 1 - end, end)
@@ -51,9 +51,8 @@
         masks = []
         if earlier:
             mixed_out[:, :begin, :] = earlier[0][...]
-            gate_out[:, :begin, :] = earlier[1][...]
         for b in range(count):
-            source = where[2 + first + b]
+            source = where[2 + first + b] if count > 1 else 0
             values[b * rows : (b + 1) * rows, near] = mine[source, :rows, :]
             values[b * rows : (b + 1) * rows, far] = other[source, :rows, :]
             for part in range(rows // span):
@@ -70,31 +69,52 @@
 
     end = step // per_end
     dst = pl.ds(pl.multiple_of((step - end * per_end) * tile, tile), tile)
-    for pair, out in ((0, gate_out), (1, mixed_out)):
-        held[:depth, :] = weight[:, pair].reshape(depth, tile)
-        held[depth:, :] = up[:, pair].reshape(held.shape[0] - depth, tile)
-        chunk = min(512, values.shape[0])
-
-        def some_rows(at, carry):
-            part = pl.ds(pl.multiple_of(at * chunk, chunk), chunk)
-            onto = pl.ds(pl.multiple_of(begin + at * chunk, 256), chunk)
-            out[plane(end), onto, dst] = jnp.dot(
-                values[part, :], held[...], preferred_element_type=f32
-            ).astype(bf16)
-            return carry
-
-        lax.fori_loop(0, values.shape[0] // chunk, some_rows, 0)
+    if earlier:
+        gate_out[0, :begin, :] = earlier[1][0]
+
+    def columns(part, pair):
+        total = jnp.dot(
+            values[part, :depth],
+            weight[:, pair].reshape(depth, tile),
+            preferred_element_type=f32,
+        )
+        return (
+            total
+            + jnp.dot(
+                values[part, depth:],
+                up[:, pair].reshape(values.shape[1] - depth, tile),
+                preferred_element_type=f32,
+            )
+        ).astype(bf16)
+
+    def some_rows(at, carry):
+        part = pl.ds(pl.multiple_of(at * rows, rows), rows)
+        onto = pl.ds(pl.multiple_of(begin + at * rows, rows), rows)
+        gate_out[0, onto, :] = columns(part, 0)
+        mixed_out[plane(end), onto, dst] = columns(part, 1)
+        return carry
+
+    lax.fori_loop(0, count, some_rows, 0)
 
 
 def project(where, mine, other, down, weight, up, small, rows, ch, count, earlier=()):
-    half = mine.shape[2]
+    height, half = mine.shape[1:]
     first = earlier[0].shape[1] // rows if earlier else 0
     n = first + count
-    tile = min(256, ch)
+    tile = min(512, ch)
+    per_end = ch // tile
     whole = lambda a: pl.BlockSpec(a.shape, lambda b, w: (0,) * a.ndim)
+    picked = lambda a: (
+        whole(a)
+        if count > 1
+        else pl.BlockSpec((1, height, half), lambda b, w: (w[2 + first], 0, 0))
+    )
     striped = lambda a: pl.BlockSpec((*a.shape[:3], tile), lambda b, w: (0, 0, 0, b))
+    gate_spot = lambda r: pl.BlockSpec(
+        (1, r, tile),
+        lambda b, w: (jnp.where(w[1] == 1, 1 - b // per_end, b // per_end), 0, b % per_end),
+    )
     wide = ch + small.shape[2]
-    held = lambda c: pl.BlockSpec((2, n * rows, c), lambda b, w: (0, 0, 0))
     full = 2 * half + down.shape[1]
     return pl.pallas_call(
         functools.partial(project_kernel, rows=rows, first=first, count=count),
@@ -104,13 +124,16 @@
         ),
         grid_spec=pltpu.PrefetchScalarGridSpec(
             num_scalar_prefetch=1,
-            grid=(2 * ch // tile,),
+            grid=(2 * per_end,),
             in_specs=[
-                whole(mine), whole(other), whole(down), striped(weight), striped(up), whole(small),
-                *map(whole, earlier),
+                picked(mine), picked(other), whole(down), striped(weight), striped(up), whole(small),
+                *((whole(earlier[0]), gate_spot(first * rows)) if earlier else ()),
             ],
-            out_specs=[held(wide), held(ch)],
-            scratch_shapes=[pltpu.VMEM((count * rows, full), bf16), pltpu.VMEM((full, tile), bf16)],
+            out_specs=[
+                pl.BlockSpec((2, n * rows, wide), lambda b, w: (0, 0, 0)),
+                gate_spot(n * rows),
+            ],
+            scratch_shapes=[pltpu.VMEM((count * rows, full), bf16)],
         ),
         cost_estimate=pl.CostEstimate(
             flops=4 * count * rows * full * (ch + wide),
@@ -269,7 +292,7 @@
 
 def output_kernel(where, *refs, n, count):
     blocks = refs[: 2 * n * count]
-    gain, weight_source, out, held, weight, sems, weight_sem = refs[2 * n * count :]
+    gain, weight_source, out, held, weight, sems, weight_sems = refs[2 * n * count :]
     ch = held.shape[1] // 2
     width = weight.shape[1]
     here = where[0]
@@ -293,23 +316,29 @@
                         )
 
     fetch(lambda copy: copy.start())
-    bring = pltpu.make_async_copy(weight_source, weight, weight_sem)
-    bring.start()
+    tile = min(256, width)
+    tiles = width // tile
+    for k in range(tiles):
+        columns = pl.ds(k * tile, tile)
+        pltpu.make_async_copy(
+            weight_source.at[:, columns], weight.at[:, columns], weight_sems.at[k]
+        ).start()
     fetch(lambda copy: copy.wait())
     values = held[...].astype(f32)
     squares = jnp.sum(values * values, axis=1, keepdims=True)
     held[...] = (values * gain[...]).astype(bf16)
-    tile = min(256, width)
-    bring.wait()
 
     def some_columns(at, carry):
         part = pl.ds(pl.multiple_of(at * tile, tile), tile)
+        pltpu.make_async_copy(
+            weight_source.at[:, part], weight.at[:, part], weight_sems.at[at]
+        ).wait()
         out[:, part] = jnp.dot(
             held[...], weight[:, part], preferred_element_type=f32
         ).astype(bf16)
         return carry
 
-    lax.fori_loop(0, width // tile, some_columns, 0)
+    lax.fori_loop(0, tiles, some_columns, 0)
     out[:, width:] = jnp.broadcast_to(squares, (count * BLOCK, LANES)).astype(bf16)
 
 
@@ -329,7 +358,7 @@
                 pltpu.VMEM((count * BLOCK, 2 * ch), bf16),
                 pltpu.VMEM(weight.shape, bf16),
                 pltpu.SemaphoreType.DMA((count, 2)),
-                pltpu.SemaphoreType.DMA,
+                pltpu.SemaphoreType.DMA((max(1, width // 256),)),
             ],
         ),
         cost_estimate=pl.CostEstimate(
@@ -424,7 +453,7 @@
     order = jnp.stack(order)
     projected = ()
     versions = []
-    for count in (1, 1, n - 2) if n > 2 else (1, 1):
+    for count in (1, n - 1):
         projected = project(
             order, mine, other, adapter_down_maps, weight, up, small, rows, ch, count, projected
         )
@@ -534,7 +563,7 @@
                 pending = None
             if (block + 1) * BLOCK % rows == 0:
                 states.append(state.astype(bf16).T)
-        if pending is not None and step < last_step:
+        if pending is not None and sends < step < last_step:
             came, (outs[pending], _) = tied(came, (outs[pending], state))
             pending = None
         done = step - (2 * n - 2)
@@ -553,25 +582,22 @@
     for k in range(1, n):
         leaving = jnp.where(at_first, states[k], states[n - 1 - k])
         landed.append(lax.ppermute(leaving, "seq", [(0, k), (n - 1, n - 1 - k)]))
-    landed = jnp.stack(landed)
-    finish = jnp.concatenate(
-        [lax.dynamic_index_in_dim(landed, which, 0, False) for which in (here, n - 1 - here)], axis=0
-    ).astype(f32).reshape(heads_here, HEAD_DIM, STATE)
 
     chips = shards // 2
     chip = shard // 2
     if chips == 2:
         keep = jnp.where(core == 0, outs[0], outs[1])
         give = jnp.where(core == 0, outs[1], outs[0])
-        both = added(keep, lax.ppermute(give, "tensor", swap))
+        back = lax.ppermute(give, "tensor", swap)
+        both = added(keep, back)
         came = lax.ppermute(both, "tensor", [(2, 0), (3, 1)])
         total = both.astype(f32) + came.astype(f32)
         for t in range(2, shards):
             give = [(j, j ^ 1) for j in range(shards) if j % 2 != t % 2]
-            both = added(outs[t], lax.ppermute(outs[t], "tensor", give))
+            back = lax.ppermute(outs[t], "tensor", give)
+            both = added(outs[t], back)
             came = lax.ppermute(both, "tensor", [(t ^ 2, t)])
-            both = both.astype(f32) + came.astype(f32)
-            total = jnp.where(shard == t, both, total)
+            total = jnp.where(shard == t, both.astype(f32) + came.astype(f32), total)
             if t == shards - 2:
                 total = lax.optimization_barrier(total)
     else:
@@ -580,12 +606,18 @@
             keep = jnp.where(core == 0, outs[2 * k], outs[2 * k + 1])
             give = jnp.where(core == 0, outs[2 * k + 1], outs[2 * k])
             halves.append(added(keep, lax.ppermute(give, "tensor", swap)))
+        both = halves[-1]
         halves = jnp.stack(halves)
         total = lax.dynamic_index_in_dim(halves, chip, 0, False).astype(f32)
         for k in range(1, chips):
             pairs = [(j, (j + 2 * k) % shards) for j in range(shards)]
             give = lax.dynamic_index_in_dim(halves, (chip + k) % chips, 0, False)
             total = total + lax.ppermute(give, "tensor", pairs).astype(f32)
+    *landed, _ = lax.optimization_barrier((*landed, both))
+    landed = jnp.stack(landed)
+    finish = jnp.concatenate(
+        [lax.dynamic_index_in_dim(landed, which, 0, False) for which in (here, n - 1 - here)], axis=0
+    ).astype(f32).reshape(heads_here, HEAD_DIM, STATE)
     width = output_projection_weight.shape[1]
     scale = lax.rsqrt(total[:, width : width + 1] / (HEADS * HEAD_DIM) + 1e-05)
     mixed = (total[:, :width] * scale).astype(bf16)

time: 348 us -> 338 us (0.971)
  Pallas kernels: 128 us -> 113 us
  waiting for transfers between devices: 24.9 us -> 35.6 us
  starting transfers between devices: 114 us -> 107 us
    pallas_call x3 -> x2, Pallas kernels: 45.5 us -> 30 us  [project(): pl.pallas_call(functools.partial(project_kernel, rows=rows, first=first,...]
    ppermute x24, waiting for transfers between devices: 13.5 us -> 20.9 us  [onward(): from_a = lax.ppermute(pair[0], 'seq', pairs_a)]
    ppermute x2, waiting for transfers between devices: 11.3 us -> 4.09 us  [per_device(): came = lax.ppermute(both, 'tensor', [(t ^ 2, t)])]
    ppermute x3, waiting for transfers between devices: 0.01 us -> 5.31 us  [per_device(): pieces.append(lax.ppermute(piece((here + k) % n), 'seq', pairs))]
    ppermute x24, starting transfers between devices: 65.7 us -> 61.4 us  [onward(): from_a = lax.ppermute(pair[0], 'seq', pairs_a)]
    ppermute x1, waiting for transfers between devices: 0.01 us -> 4.11 us  [per_device(): came = lax.ppermute(both, 'tensor', [(2, 0), (3, 1)])]
  transfers between devices with their start and end apart: 59 -> 59, of which waited for: 10 -> 15; matrix products, arithmetic and copies ran while one was open for 17% -> 16% of each run, Pallas kernels for 33% -> 31%
where the time goes in v2:
time: 338 us; the launch traced here: 336 us
  Pallas kernels  113 us (33%)
  starting transfers between devices  107 us (32%)
  other arithmetic  42.5 us (13%)
  waiting for transfers between devices  35.6 us (11%)
  local copies, waits for them, and re-layouts  35.3 us (10%)
    ppermute x24, starting transfers between devices, onward(): from_a = lax.ppermute(pair[0], 'seq', pairs_a)  61.4 us
    pallas_call x8, Pallas kernels, scan_block(): pl.pallas_call(scan_kernel, out_shape=outs, grid=(1,), in_specs=[pl.Block...  39 us
    pallas_call x2, Pallas kernels, project(): pl.pallas_call(functools.partial(project_kernel, rows=rows, first=first,...  30 us
    pallas_call x4, Pallas kernels, output_block(): pl.pallas_call(functools.partial(output_kernel, n=n, count=count), out_sh...  25.2 us
    convert_element_type x17, other arithmetic, added(): return (a.astype(f32) + b.astype(f32)).astype(bf16)  22.1 us
    ppermute x24, waiting for transfers between devices, onward(): from_a = lax.ppermute(pair[0], 'seq', pairs_a)  20.9 us
    pallas_call x6, Pallas kernels, merge(): pl.pallas_call(functools.partial(merge_kernel, passing=passing), out_shap...  19.1 us
    ppermute x22, starting transfers between devices, onward(): from_b = lax.ppermute(pair[1], 'seq', pairs_b)  16.6 us
  transfers between devices with their start and end apart: 59, of which 15 were waited for; matrix products, arithmetic and copies ran while one was open for 16% of the time, Pallas kernels for 31%

profile of v2, /device:TPU:0, one launch (start us, length us, event | category | flops | bytes accessed | tf_op | source)
XLA Modules:
  0.0 336.1 jit_solution(6683278650338161422)
XLA Ops:
  3.6 5.1 %collective-permute-start.2 = (bf16[272,512]{1,0:T(8,128)(2,1)}, bf16[272,512]{1,0:T(8,128)(2,1)}, u32[]{:S(2)}, u32[]{:S(2)}) collective-permute-start(bf16[272,512]{1,0:T(8,128)(2,1)} %get-tuple-element.241), channel_id=1, source_target_pairs={{0,12},{4,0},{8,4},{12,8},{1,13},{5,1},{9,5},{13,9},{2,14},{6,2},{... | collective-permute-start | bytes 835592 | tf_op jit(solution)/shard_map/ppermute | solution.py:429
  9.7 11.5 %copy.48 = bf16[64,16,2,2048]{3,1,2,0:T(8,128)(2,1)} copy(bf16[64,16,2,2048]{3,2,1,0:T(2,128)(2,1)} %bitcast.183) | data formatting | bytes 16777216 | tf_op jit(solution)/shard_map/reshape | solution.py:432
  27.4 5.3 %collective-permute-done.1 = bf16[272,512]{1,0:T(8,128)(2,1)} collective-permute-done((bf16[272,512]{1,0:T(8,128)(2,1)S(1)}, bf16[272,512]{1,0:T(8,128)(2,1)}, u32[]{:S(2)}, u32[]{:S(2)}) %collective-permute-start.1) | collective-permute-done | bytes 278560 | tf_op jit(solution)/shard_map/ppermute | solution.py:429
  37.0 9.8 %project.2 = (bf16[2,256,1408]{2,1,0:T(8,128)(2,1)}, bf16[2,256,1024]{2,1,0:T(8,128)(2,1)}) custom-call(s32[6]{0:T(128)} %stack.136.where, bf16[4,272,512]{2,1,0:T(8,128)(2,1)} %copy-done.8, bf16[4,272,512]{2,1,0:T(8,128)(2,1)} %collective-permute-done.3.refs_1_, bf16[1024,256]{1,0:T(8,128)(2,1)} %refs_2_.3, bf16[64,2,16,2048]{3,2,1,0:T(8,128)(2,1)} %bitcast.181, ...), custom_call_target="tpu_custom_call" | custom-call | flops 3187671040 | bytes 10878976 | tf_op jit(solution)/shard_map/project/pallas_call | solution.py:119
  65.0 20.2 %project.3 = (bf16[2,1024,1408]{2,1,0:T(8,128)(2,1)}, bf16[2,1024,1024]{2,1,0:T(8,128)(2,1)}) custom-call(s32[6]{0:T(128)} %stack.136.where, bf16[4,272,512]{2,1,0:T(8,128)(2,1)} %copy-done.8, bf16[4,272,512]{2,1,0:T(8,128)(2,1)} %collective-permute-done.3.refs_1_, bf16[1024,256]{1,0:T(8,128)(2,1)} %refs_2_.3, bf16[64,2,16,2048]{3,2,1,0:T(8,128)(2,1)} %bitcast.182, ...), custom_call_target="tpu_custom_call" | custom-call | flops 9563013120 | bytes 18350080 | tf_op jit(solution)/shard_map/project/pallas_call | solution.py:119
  97.0 5.2 %collective-permute-done.8 = bf16[128,1024]{1,0:T(8,128)(2,1)S(1)} collective-permute-done((bf16[128,1024]{1,0:T(8,128)(2,1)}, bf16[128,1024]{1,0:T(8,128)(2,1)S(1)}, u32[]{:S(2)}, u32[]{:S(2)}) %collective-permute-start.8) | collective-permute-done | bytes 262176 | tf_op jit(solution)/shard_map/ppermute | solution.py:507
  114.8 4.0 %collective-permute-done.12 = bf16[128,1024]{1,0:T(8,128)(2,1)S(1)} collective-permute-done((bf16[128,1024]{1,0:T(8,128)(2,1)S(1)}, bf16[128,1024]{1,0:T(8,128)(2,1)S(1)}, u32[]{:S(2)}, u32[]{:S(2)}) %collective-permute-start.12) | collective-permute-done | bytes 262176 | tf_op jit(solution)/shard_map/ppermute | solution.py:507
  129.2 4.8 %scan_block.8 = (bf16[128,1024]{1,0:T(8,128)(2,1)}, f32[128,1024]{1,0:T(8,128)}, f32[8,1280]{1,0:T(8,128)}) custom-call(bf16[128,1024]{1,0:T(8,128)(2,1)} %copy-done.35, bf16[128,1408]{1,0:T(8,128)(2,1)} %copy-done.28, f32[8,1280]{1,0:T(8,128)} %fusion.40.tail, f32[128,1024]{1,0:T(8,128)} %bitcast.189, f32[1,128]{1,0:T(1,128)} %get-tuple-element.249.index, ...), custom_call_target="tpu_custom_call" | custom-call | flops 134217728 | bytes 2097152 | tf_op jit(solution)/shard_map/scan_block/pallas_call | solution.py:273
  147.7 4.9 %scan_block.9 = (bf16[128,1024]{1,0:T(8,128)(2,1)}, f32[128,1024]{1,0:T(8,128)}, f32[8,1280]{1,0:T(8,128)}) custom-call(bf16[128,2048]{1,0:T(8,128)(2,1)} %get-tuple-element.121.gates, bf16[128,1408]{1,0:T(8,128)(2,1)} %copy-done.29, f32[8,1280]{1,0:T(8,128)} %get-tuple-element.126.tail, f32[128,1024]{1,0:T(8,128)} %get-tuple-element.127.state, ...), custom_call_target="tpu_custom_call" | custom-call | flops 134217728 | bytes 2097152 | tf_op jit(solution)/shard_map/scan_block/pallas_call | solution.py:273
  167.0 4.9 %scan_block.10 = (bf16[128,1024]{1,0:T(8,128)(2,1)}, f32[128,1024]{1,0:T(8,128)}, f32[8,1280]{1,0:T(8,128)}) custom-call(bf16[128,2048]{1,0:T(8,128)(2,1)} %get-tuple-element.130.gates, bf16[128,1408]{1,0:T(8,128)(2,1)} %copy-done.30, f32[8,1280]{1,0:T(8,128)} %get-tuple-element.135.tail, f32[128,1024]{1,0:T(8,128)} %get-tuple-element.136.state, ...), custom_call_target="tpu_custom_call" | custom-call | flops 134217728 | bytes 2097152 | tf_op jit(solution)/shard_map/scan_block/pallas_call | solution.py:273
  188.1 4.9 %scan_block.11 = (bf16[128,1024]{1,0:T(8,128)(2,1)}, f32[128,1024]{1,0:T(8,128)}, f32[8,1280]{1,0:T(8,128)}) custom-call(bf16[128,2048]{1,0:T(8,128)(2,1)} %get-tuple-element.139.gates, bf16[128,1408]{1,0:T(8,128)(2,1)} %copy-done.31, f32[8,1280]{1,0:T(8,128)} %get-tuple-element.144.tail, f32[128,1024]{1,0:T(8,128)} %get-tuple-element.145.state, ...), custom_call_target="tpu_custom_call" | custom-call | flops 134217728 | bytes 2097152 | tf_op jit(solution)/shard_map/scan_block/pallas_call | solution.py:273
  206.6 4.9 %scan_block.12 = (bf16[128,1024]{1,0:T(8,128)(2,1)}, f32[128,1024]{1,0:T(8,128)}, f32[8,1280]{1,0:T(8,128)}) custom-call(bf16[128,2048]{1,0:T(8,128)(2,1)} %get-tuple-element.148.gates, bf16[128,1408]{1,0:T(8,128)(2,1)} %copy-done.32, f32[8,1280]{1,0:T(8,128)} %get-tuple-element.153.tail, f32[128,1024]{1,0:T(8,128)} %get-tuple-element.154.state, ...), custom_call_target="tpu_custom_call" | custom-call | flops 134217728 | bytes 2097152 | tf_op jit(solution)/shard_map/scan_block/pallas_call | solution.py:273
  225.1 4.9 %scan_block.13 = (bf16[128,1024]{1,0:T(8,128)(2,1)}, f32[128,1024]{1,0:T(8,128)}, f32[8,1280]{1,0:T(8,128)}) custom-call(bf16[128,2048]{1,0:T(8,128)(2,1)} %get-tuple-element.157.gates, bf16[128,1408]{1,0:T(8,128)(2,1)} %copy-done.33, f32[8,1280]{1,0:T(8,128)} %get-tuple-element.162.tail, f32[128,1024]{1,0:T(8,128)} %get-tuple-element.163.state, ...), custom_call_target="tpu_custom_call" | custom-call | flops 134217728 | bytes 2097152 | tf_op jit(solution)/shard_map/scan_block/pallas_call | solution.py:273
  237.6 6.4 %output_block.4 = bf16[256,1152]{1,0:T(8,128)(2,1)} custom-call(s32[1]{0:T(128)} %bitcast.where, bf16[128,2048]{1,0:T(8,128)(2,1)} %get-tuple-element.120.refs_0_.refs_4_, bf16[128,2048]{1,0:T(8,128)(2,1)} %copy-done.9, bf16[128,2048]{1,0:T(8,128)(2,1)} %copy-done.11, bf16[128,2048]{1,0:T(8,128)(2,1)} %copy-done.2, ...), custom_call_target="tpu_custom_call" | custom-call | flops 1073741824 | bytes 6291456 | tf_op jit(solution)/shard_map/output_block/pallas_call | solution.py:349
  246.2 4.8 %scan_block.14 = (bf16[128,1024]{1,0:T(8,128)(2,1)}, f32[128,1024]{1,0:T(8,128)}, f32[8,1280]{1,0:T(8,128)}) custom-call(bf16[128,2048]{1,0:T(8,128)(2,1)} %get-tuple-element.165.gates, bf16[128,1408]{1,0:T(8,128)(2,1)} %get-tuple-element.196.sums, f32[8,1280]{1,0:T(8,128)} %get-tuple-element.166.tail, f32[128,1024]{1,0:T(8,128)} %get-tuple-element.168.state, ...), custom_call_target="tpu_custom_call" | custom-call | flops 134217728 | bytes 2097152 | tf_op jit(solution)/shard_map/scan_block/pallas_call | solution.py:273
  255.4 4.9 %scan_block.15 = (bf16[128,1024]{1,0:T(8,128)(2,1)}, f32[128,1024]{1,0:T(8,128)}, f32[8,1280]{1,0:T(8,128)}) custom-call(bf16[128,1024]{1,0:T(8,128)(2,1)} %fusion.26.gates, bf16[128,1408]{1,0:T(8,128)(2,1)} %get-tuple-element.197.sums, f32[8,1280]{1,0:T(8,128)} %get-tuple-element.175.tail, f32[128,1024]{1,0:T(8,128)} %get-tuple-element.176.state, ...), custom_call_target="tpu_custom_call" | custom-call | flops 134217728 | bytes 2097152 | tf_op jit(solution)/shard_map/scan_block/pallas_call | solution.py:273
  265.1 6.4 %output_block.5 = bf16[256,1152]{1,0:T(8,128)(2,1)} custom-call(s32[1]{0:T(128)} %bitcast.where, bf16[128,2048]{1,0:T(8,128)(2,1)} %get-tuple-element.138.refs_0_.refs_4_, bf16[128,2048]{1,0:T(8,128)(2,1)} %copy-done.2, bf16[128,2048]{1,0:T(8,128)(2,1)} %copy-done.12, bf16[128,2048]{1,0:T(8,128)(2,1)} %copy-done.4, ...), custom_call_target="tpu_custom_call" | custom-call | flops 1073741824 | bytes 6291456 | tf_op jit(solution)/shard_map/output_block/pallas_call | solution.py:349
  277.3 4.2 %collective-permute-start.56 = (bf16[1024,128]{0,1:T(8,128)(2,1)}, bf16[1024,128]{0,1:T(8,128)(2,1)}, u32[]{:S(2)}, u32[]{:S(2)}) collective-permute-start(bf16[1024,128]{0,1:T(8,128)(2,1)} %get-tuple-element.231), channel_id=1, source_target_pairs={{0,4},{12,8},{1,5},{13,9},{2,6},{14,10},{3,7},{15,11},{16,20},{28,... | collective-permute-start | bytes 786440 | tf_op jit(solution)/shard_map/ppermute | solution.py:584
  284.2 6.4 %output_block.6 = bf16[256,1152]{1,0:T(8,128)(2,1)} custom-call(s32[1]{0:T(128)} %bitcast.where, bf16[128,2048]{1,0:T(8,128)(2,1)} %get-tuple-element.156.refs_0_.refs_4_, bf16[128,2048]{1,0:T(8,128)(2,1)} %copy-done.4, bf16[128,2048]{1,0:T(8,128)(2,1)} %copy-done.17, bf16[128,1024]{1,0:T(8,128)(2,1)} %copy-done.15, ...), custom_call_target="tpu_custom_call" | custom-call | flops 1073741824 | bytes 6291456 | tf_op jit(solution)/shard_map/output_block/pallas_call | solution.py:349
  294.3 4.7 %collective-permute-done.49.refs_11_.refs_15_ = bf16[128,1024]{1,0:T(8,128)(2,1)S(1)} collective-permute-done((bf16[128,1024]{1,0:T(8,128)(2,1)}, bf16[128,1024]{1,0:T(8,128)(2,1)S(1)}, u32[]{:S(2)}, u32[]{:S(2)}) %collective-permute-start.49) | collective-permute-done | bytes 262176 | tf_op jit(solution)/shard_map/ppermute | solution.py:507
  300.4 6.0 %output_block.7 = bf16[256,1152]{1,0:T(8,128)(2,1)} custom-call(s32[1]{0:T(128)} %bitcast.where, bf16[128,1024]{1,0:T(8,128)(2,1)} %copy-done.21, bf16[128,1024]{1,0:T(8,128)(2,1)} %copy-done.15, bf16[128,1024]{1,0:T(8,128)(2,1)} %copy-done.36, bf16[128,1024]{1,0:T(8,128)(2,1)} %copy-done.37, bf16[128,1024]{1,0:T(8,128)(2,1)} %copy-done.21, ...), custom_call_target="tpu_custom_call" | custom-call | flops 1073741824 | bytes 6291456 | tf_op jit(solution)/shard_map/output_block/pallas_call | solution.py:349
  314.3 5.4 %collective-permute-start.53 = (bf16[256,1152]{1,0:T(8,128)(2,1)S(1)}, bf16[256,1152]{1,0:T(8,128)(2,1)}, u32[]{:S(2)}, u32[]{:S(2)}) collective-permute-start(bf16[256,1152]{1,0:T(8,128)(2,1)S(1)} %add_convert_fusion.1), channel_id=1, source_target_pairs={{0,2},{4,6},{8,10},{12,14},{16,18},{20,22},{24,26},{28,30}} | collective-permute-start | bytes 1769480 | tf_op jit(solution)/shard_map/ppermute | solution.py:599
  324.1 4.1 %collective-permute-done.55 = bf16[256,1152]{1,0:T(8,128)(2,1)S(1)} collective-permute-done((bf16[256,1152]{1,0:T(8,128)(2,1)S(1)}, bf16[256,1152]{1,0:T(8,128)(2,1)S(1)}, u32[]{:S(2)}, u32[]{:S(2)}) %collective-permute-start.55) | collective-permute-done | bytes 589856 | tf_op jit(solution)/shard_map/ppermute | solution.py:593
  328.2 4.1 %collective-permute-done.53 = bf16[256,1152]{1,0:T(8,128)(2,1)} collective-permute-done((bf16[256,1152]{1,0:T(8,128)(2,1)S(1)}, bf16[256,1152]{1,0:T(8,128)(2,1)}, u32[]{:S(2)}, u32[]{:S(2)}) %collective-permute-start.53) | collective-permute-done | bytes 589856 | tf_op jit(solution)/shard_map/ppermute | solution.py:599
  (291 shorter events, 186.3 us)
Async XLA Ops:
  3.6 23.8 %collective-permute-start.2 = (bf16[272,512]{1,0:T(8,128)(2,1)}, bf16[272,512]{1,0:T(8,128)(2,1)}, u32[]{:S(2)}, u32[]{:S(2)}) collective-permute-start(bf16[272,512]{1,0:T(8,128)(2,1)} %get-tuple-element.241), channel_id=1, source_target_pairs={{0,12},{4,0},{8,4},{12,8},{1,13},{5,1},{9,5},{13,9},{2,14},{6,2},{... | collective-permute-start | bytes 835592 | tf_op jit(solution)/shard_map/ppermute | solution.py:429
  8.7 24.0 %collective-permute-start.1 = (bf16[272,512]{1,0:T(8,128)(2,1)S(1)}, bf16[272,512]{1,0:T(8,128)(2,1)}, u32[]{:S(2)}, u32[]{:S(2)}) collective-permute-start(bf16[272,512]{1,0:T(8,128)(2,1)S(1)} %get-tuple-element.240), channel_id=1, source_target_pairs={{0,8},{4,12},{8,0},{12,4},{1,9},{5,13},{9,1},{13,5},{2,10},{6,14},... | collective-permute-start | bytes 835592 | tf_op jit(solution)/shard_map/ppermute | solution.py:429
  8.7 24.0 %collective-permute-start = (bf16[272,512]{1,0:T(8,128)(2,1)S(1)}, bf16[272,512]{1,0:T(8,128)(2,1)}, u32[]{:S(2)}, u32[]{:S(2)}) collective-permute-start(bf16[272,512]{1,0:T(8,128)(2,1)S(1)} %get-tuple-element.239), channel_id=1, source_target_pairs={{0,4},{4,8},{8,12},{12,0},{1,5},{5,9},{9,13},{13,1},{2,6},{6,10},{... | collective-permute-start | bytes 835592 | tf_op jit(solution)/shard_map/ppermute | solution.py:429
  54.4 30.8 %collective-permute-start.4 = (bf16[128,1024]{1,0:T(8,128)(2,1)}, bf16[128,1024]{1,0:T(8,128)(2,1)}, u32[]{:S(2)}, u32[]{:S(2)}) collective-permute-start(bf16[128,1024]{1,0:T(8,128)(2,1)} %get-tuple-element.235), channel_id=1, source_target_pairs={{0,4},{4,0},{8,12},{12,8},{1,5},{5,1},{9,13},{13,9},{2,6},{6,2},{1... | collective-permute-start | bytes 786440 | tf_op jit(solution)/shard_map/ppermute | solution.py:507
  58.2 27.0 %collective-permute-start.5 = (bf16[128,1024]{1,0:T(8,128)(2,1)}, bf16[128,1024]{1,0:T(8,128)(2,1)}, u32[]{:S(2)}, u32[]{:S(2)}) collective-permute-start(bf16[128,1024]{1,0:T(8,128)(2,1)} %get-tuple-element.234), channel_id=1, source_target_pairs={{4,8},{8,4},{5,9},{9,5},{6,10},{10,6},{7,11},{11,7},{20,24},{24,20... | collective-permute-start | bytes 786440 | tf_op jit(solution)/shard_map/ppermute | solution.py:508
  60.9 24.3 %collective-permute-start.10 = (bf16[128,1408]{1,0:T(8,128)(2,1)}, bf16[128,1408]{1,0:T(8,128)(2,1)S(1)}, u32[]{:S(2)}, u32[]{:S(2)}) collective-permute-start(bf16[128,1408]{1,0:T(8,128)(2,1)} %get-tuple-element.223), channel_id=1, source_target_pairs={{0,4},{4,0},{8,12},{12,8},{1,5},{5,1},{9,13},{13,9},{2,6},{6,2},{1... | collective-permute-start | bytes 1081352 | tf_op jit(solution)/shard_map/ppermute | solution.py:507
  64.1 21.1 %collective-permute-start.11 = (bf16[128,1408]{1,0:T(8,128)(2,1)}, bf16[128,1408]{1,0:T(8,128)(2,1)S(1)}, u32[]{:S(2)}, u32[]{:S(2)}) collective-permute-start(bf16[128,1408]{1,0:T(8,128)(2,1)} %get-tuple-element.222), channel_id=1, source_target_pairs={{4,8},{8,4},{5,9},{9,5},{6,10},{10,6},{7,11},{11,7},{20,24},{24,20... | collective-permute-start | bytes 1081352 | tf_op jit(solution)/shard_map/ppermute | solution.py:508
  120.1 22.8 %collective-permute-start.22 = (bf16[128,1408]{1,0:T(8,128)(2,1)S(1)}, bf16[128,1408]{1,0:T(8,128)(2,1)S(1)}, u32[]{:S(2)}, u32[]{:S(2)}) collective-permute-start(bf16[128,1408]{1,0:T(8,128)(2,1)S(1)} %get-tuple-element.207), channel_id=1, source_target_pairs={{0,4},{4,0},{8,12},{12,8},{1,5},{5,1},{9,13},{13,9},{2,6},{6,2},{1... | collective-permute-start | bytes 1081352 | tf_op jit(solution)/shard_map/ppermute | solution.py:507
  123.8 19.2 %collective-permute-start.23 = (bf16[128,1408]{1,0:T(8,128)(2,1)S(1)}, bf16[128,1408]{1,0:T(8,128)(2,1)S(1)}, u32[]{:S(2)}, u32[]{:S(2)}) collective-permute-start(bf16[128,1408]{1,0:T(8,128)(2,1)S(1)} %get-tuple-element.206.sums), channel_id=1, source_target_pairs={{4,8},{8,4},{5,9},{9,5},{6,10},{10,6},{7,11},{11,7},{20,24},{24,20... | collective-permute-start | bytes 1081352 | tf_op jit(solution)/shard_map/ppermute | solution.py:508
  138.6 15.8 %collective-permute-start.20 = (bf16[128,2048]{1,0:T(8,128)(2,1)}, bf16[128,2048]{1,0:T(8,128)(2,1)S(1)}, u32[]{:S(2)}, u32[]{:S(2)}) collective-permute-start(bf16[128,2048]{1,0:T(8,128)(2,1)} %get-tuple-element.120.refs_0_.refs_4_), channel_id=1, source_target_pairs={{0,4},{4,0},{8,12},{12,8},{1,5},{5,1},{9,13},{13,9},{2,6},{6,2},{1... | collective-permute-start | bytes 1572872 | tf_op jit(solution)/shard_map/ppermute | solution.py:507
  144.2 18.5 %collective-permute-start.26 = (bf16[128,1408]{1,0:T(8,128)(2,1)S(1)}, bf16[128,1408]{1,0:T(8,128)(2,1)S(1)}, u32[]{:S(2)}, u32[]{:S(2)}) collective-permute-start(bf16[128,1408]{1,0:T(8,128)(2,1)S(1)} %get-tuple-element.205), channel_id=1, source_target_pairs={{0,4},{4,0},{8,12},{12,8},{1,5},{5,1},{9,13},{13,9},{2,6},{6,2},{1... | collective-permute-start | bytes 1081352 | tf_op jit(solution)/shard_map/ppermute | solution.py:507
  146.4 16.4 %collective-permute-start.27 = (bf16[128,1408]{1,0:T(8,128)(2,1)S(1)}, bf16[128,1408]{1,0:T(8,128)(2,1)S(1)}, u32[]{:S(2)}, u32[]{:S(2)}) collective-permute-start(bf16[128,1408]{1,0:T(8,128)(2,1)S(1)} %get-tuple-element.204.sums), channel_id=1, source_target_pairs={{4,8},{8,4},{5,9},{9,5},{6,10},{10,6},{7,11},{11,7},{20,24},{24,20... | collective-permute-start | bytes 1081352 | tf_op jit(solution)/shard_map/ppermute | solution.py:508
  164.1 18.3 %collective-permute-start.30 = (bf16[128,1408]{1,0:T(8,128)(2,1)S(1)}, bf16[128,1408]{1,0:T(8,128)(2,1)S(1)}, u32[]{:S(2)}, u32[]{:S(2)}) collective-permute-start(bf16[128,1408]{1,0:T(8,128)(2,1)S(1)} %get-tuple-element.203), channel_id=1, source_target_pairs={{0,4},{4,0},{8,12},{12,8},{1,5},{5,1},{9,13},{13,9},{2,6},{6,2},{1... | collective-permute-start | bytes 1081352 | tf_op jit(solution)/shard_map/ppermute | solution.py:507
  166.3 16.1 %collective-permute-start.31 = (bf16[128,1408]{1,0:T(8,128)(2,1)S(1)}, bf16[128,1408]{1,0:T(8,128)(2,1)S(1)}, u32[]{:S(2)}, u32[]{:S(2)}) collective-permute-start(bf16[128,1408]{1,0:T(8,128)(2,1)S(1)} %get-tuple-element.202.sums), channel_id=1, source_target_pairs={{4,8},{8,4},{5,9},{9,5},{6,10},{10,6},{7,11},{11,7},{20,24},{24,20... | collective-permute-start | bytes 1081352 | tf_op jit(solution)/shard_map/ppermute | solution.py:508
  183.7 17.7 %collective-permute-start.34 = (bf16[128,1408]{1,0:T(8,128)(2,1)S(1)}, bf16[128,1408]{1,0:T(8,128)(2,1)S(1)}, u32[]{:S(2)}, u32[]{:S(2)}) collective-permute-start(bf16[128,1408]{1,0:T(8,128)(2,1)S(1)} %get-tuple-element.201), channel_id=1, source_target_pairs={{0,4},{4,0},{8,12},{12,8},{1,5},{5,1},{9,13},{13,9},{2,6},{6,2},{1... | collective-permute-start | bytes 1081352 | tf_op jit(solution)/shard_map/ppermute | solution.py:507
  202.7 17.7 %collective-permute-start.38 = (bf16[128,1408]{1,0:T(8,128)(2,1)S(1)}, bf16[128,1408]{1,0:T(8,128)(2,1)S(1)}, u32[]{:S(2)}, u32[]{:S(2)}) collective-permute-start(bf16[128,1408]{1,0:T(8,128)(2,1)S(1)} %get-tuple-element.199), channel_id=1, source_target_pairs={{0,4},{4,0},{8,12},{12,8},{1,5},{5,1},{9,13},{13,9},{2,6},{6,2},{1... | collective-permute-start | bytes 1081352 | tf_op jit(solution)/shard_map/ppermute | solution.py:507
  221.4 22.6 %collective-permute-start.42 = (bf16[128,1408]{1,0:T(8,128)(2,1)S(1)}, bf16[128,1408]{1,0:T(8,128)(2,1)S(1)}, u32[]{:S(2)}, u32[]{:S(2)}) collective-permute-start(bf16[128,1408]{1,0:T(8,128)(2,1)S(1)} %fusion.8), channel_id=1, source_target_pairs={{0,4},{4,0},{8,12},{12,8},{1,5},{5,1},{9,13},{13,9},{2,6},{6,2},{1... | collective-permute-start | bytes 1081352 | tf_op jit(solution)/shard_map/ppermute | solution.py:507
  273.8 32.6 %collective-permute-start.54 = (bf16[256,1152]{1,0:T(8,128)(2,1)}, bf16[256,1152]{1,0:T(8,128)(2,1)}, u32[]{:S(2)}, u32[]{:S(2)}) collective-permute-start(bf16[256,1152]{1,0:T(8,128)(2,1)} %broadcast_select_fusion), channel_id=1, source_target_pairs={{0,1},{1,0},{2,3},{3,2},{4,5},{5,4},{6,7},{7,6},{8,9},{9,8},{10,11... | collective-permute-start | bytes 1769480 | tf_op jit(solution)/shard_map/ppermute | solution.py:591
  273.8 16.8 %collective-permute-start.47 = (bf16[128,1024]{1,0:T(8,128)(2,1)S(1)}, bf16[128,1024]{1,0:T(8,128)(2,1)S(1)}, u32[]{:S(2)}, u32[]{:S(2)}) collective-permute-start(bf16[128,1024]{1,0:T(8,128)(2,1)S(1)} %collective-permute-done.45.refs_2_.refs_6_), channel_id=1, source_target_pairs={{0,4},{4,0},{8,12},{12,8},{1,5},{5,1},{9,13},{13,9},{2,6},{6,2},{1... | collective-permute-start | bytes 786440 | tf_op jit(solution)/shard_map/ppermute | solution.py:507
  277.3 42.5 %collective-permute-start.56 = (bf16[1024,128]{0,1:T(8,128)(2,1)}, bf16[1024,128]{0,1:T(8,128)(2,1)}, u32[]{:S(2)}, u32[]{:S(2)}) collective-permute-start(bf16[1024,128]{0,1:T(8,128)(2,1)} %get-tuple-element.231), channel_id=1, source_target_pairs={{0,4},{12,8},{1,5},{13,9},{2,6},{14,10},{3,7},{15,11},{16,20},{28,... | collective-permute-start | bytes 786440 | tf_op jit(solution)/shard_map/ppermute | solution.py:584
  281.5 39.8 %collective-permute-start.57 = (bf16[1024,128]{0,1:T(8,128)(2,1)}, bf16[1024,128]{0,1:T(8,128)(2,1)}, u32[]{:S(2)}, u32[]{:S(2)}) collective-permute-start(bf16[1024,128]{0,1:T(8,128)(2,1)} %get-tuple-element.230), channel_id=1, source_target_pairs={{0,8},{12,4},{1,9},{13,5},{2,10},{14,6},{3,11},{15,7},{16,24},{28,... | collective-permute-start | bytes 786440 | tf_op jit(solution)/shard_map/ppermute | solution.py:584
  291.5 29.9 %collective-permute-start.58 = (bf16[1024,128]{0,1:T(8,128)(2,1)}, bf16[1024,128]{0,1:T(8,128)(2,1)}, u32[]{:S(2)}, u32[]{:S(2)}) collective-permute-start(bf16[1024,128]{0,1:T(8,128)(2,1)} %get-tuple-element.228), channel_id=1, source_target_pairs={{0,12},{12,0},{1,13},{13,1},{2,14},{14,2},{3,15},{15,3},{16,28},{2... | collective-permute-start | bytes 786440 | tf_op jit(solution)/shard_map/ppermute | solution.py:584
  311.6 16.6 %collective-permute-start.55 = (bf16[256,1152]{1,0:T(8,128)(2,1)S(1)}, bf16[256,1152]{1,0:T(8,128)(2,1)S(1)}, u32[]{:S(2)}, u32[]{:S(2)}) collective-permute-start(bf16[256,1152]{1,0:T(8,128)(2,1)S(1)} %add_convert_fusion), channel_id=1, source_target_pairs={{2,0},{3,1},{6,4},{7,5},{10,8},{11,9},{14,12},{15,13},{18,16},{19,... | collective-permute-start | bytes 1769480 | tf_op jit(solution)/shard_map/ppermute | solution.py:593
  314.3 18.0 %collective-permute-start.53 = (bf16[256,1152]{1,0:T(8,128)(2,1)S(1)}, bf16[256,1152]{1,0:T(8,128)(2,1)}, u32[]{:S(2)}, u32[]{:S(2)}) collective-permute-start(bf16[256,1152]{1,0:T(8,128)(2,1)S(1)} %add_convert_fusion.1), channel_id=1, source_target_pairs={{0,2},{4,6},{8,10},{12,14},{16,18},{20,22},{24,26},{28,30}} | collective-permute-start | bytes 1769480 | tf_op jit(solution)/shard_map/ppermute | solution.py:599
  (85 other events, 759.8 us)

commit v3 on v2

--- a/solution.py
+++ b/solution.py
@@ -515,6 +515,10 @@
     sends = blocks + n - 2
     last_step = blocks + 2 * n - 3
     per = size // BLOCK
+    chips = shards // 2
+    chip = shard // 2
+    groups = [2, 1, 1] if chips == 2 else [1] * shards
+    group_ends = [sum(groups[: k + 1]) for k in range(len(groups))]
     sums = came = before = gated = None
     went, arrived, states, outs = {}, {}, [], []
     pending = None
@@ -567,9 +571,9 @@
             came, (outs[pending], _) = tied(came, (outs[pending], state))
             pending = None
         done = step - (2 * n - 2)
-        if done >= 0 and (done + 1) % per == 0:
+        if done >= 0 and (done + 1) % per == 0 and (done + 1) // per in group_ends:
             needed = []
-            for b in range(done + 1 - per, done + 1):
+            for b in range(done + 1 - per * groups[len(outs)], done + 1):
                 for _ in range(2):
                     needed.append(went[b])
                     needed.extend(arrived[b + n - 1 + k][1 - k % 2] for k in range(1, n))
@@ -583,19 +587,17 @@
         leaving = jnp.where(at_first, states[k], states[n - 1 - k])
         landed.append(lax.ppermute(leaving, "seq", [(0, k), (n - 1, n - 1 - k)]))
 
-    chips = shards // 2
-    chip = shard // 2
     if chips == 2:
-        keep = jnp.where(core == 0, outs[0], outs[1])
-        give = jnp.where(core == 0, outs[1], outs[0])
+        keep = own(outs[0], core * size, size, 0)
+        give = own(outs[0], (1 - core) * size, size, 0)
         back = lax.ppermute(give, "tensor", swap)
         both = added(keep, back)
         came = lax.ppermute(both, "tensor", [(2, 0), (3, 1)])
         total = both.astype(f32) + came.astype(f32)
         for t in range(2, shards):
             give = [(j, j ^ 1) for j in range(shards) if j % 2 != t % 2]
-            back = lax.ppermute(outs[t], "tensor", give)
-            both = added(outs[t], back)
+            back = lax.ppermute(outs[t - 1], "tensor", give)
+            both = added(outs[t - 1], back)
             came = lax.ppermute(both, "tensor", [(t ^ 2, t)])
             total = jnp.where(shard == t, both.astype(f32) + came.astype(f32), total)
             if t == shards - 2:

time: 338 us -> 336 us (level)
  Pallas kernels: 113 us -> 109 us
    pallas_call x4 -> x3, Pallas kernels: 25.2 us -> 20.4 us  [output_block(): pl.pallas_call(functools.partial(output_kernel, n=n, count=count), out_sh...]
    unnamed x110 -> x108, local copies, waits for them, and re-layouts: 9.99 us -> 9.94 us
  transfers between devices with their start and end apart: 59 -> 59, of which waited for: 15 -> 15; matrix products, arithmetic and copies ran while one was open for 16% -> 16% of each run, Pallas kernels for 31% -> 30%
where the time goes in v3:
time: 336 us; the launch traced here: 333 us
  starting transfers between devices  109 us (32%)
  Pallas kernels  109 us (32%)
  other arithmetic  40.1 us (12%)
  local copies, waits for them, and re-layouts  37.4 us (11%)
  waiting for transfers between devices  36.8 us (11%)
    ppermute x24, starting transfers between devices, onward(): from_a = lax.ppermute(pair[0], 'seq', pairs_a)  63.4 us
    pallas_call x8, Pallas kernels, scan_block(): pl.pallas_call(scan_kernel, out_shape=outs, grid=(1,), in_specs=[pl.Block...  39 us
    pallas_call x2, Pallas kernels, project(): pl.pallas_call(functools.partial(project_kernel, rows=rows, first=first,...  30 us
    ppermute x24, waiting for transfers between devices, onward(): from_a = lax.ppermute(pair[0], 'seq', pairs_a)  22 us
    convert_element_type x17, other arithmetic, added(): return (a.astype(f32) + b.astype(f32)).astype(bf16)  21.9 us
    pallas_call x3, Pallas kernels, output_block(): pl.pallas_call(functools.partial(output_kernel, n=n, count=count), out_sh...  20.4 us
    pallas_call x6, Pallas kernels, merge(): pl.pallas_call(functools.partial(merge_kernel, passing=passing), out_shap...  19.2 us
    ppermute x22, starting transfers between devices, onward(): from_b = lax.ppermute(pair[1], 'seq', pairs_b)  16.6 us
  transfers between devices with their start and end apart: 59, of which 15 were waited for; matrix products, arithmetic and copies ran while one was open for 16% of the time, Pallas kernels for 30%

profile of v3, /device:TPU:0, one launch (start us, length us, event | category | flops | bytes accessed | tf_op | source)
XLA Modules:
  0.0 333.4 jit_solution(3345850825954029945)
XLA Ops:
  3.6 5.1 %collective-permute-start.2 = (bf16[272,512]{1,0:T(8,128)(2,1)}, bf16[272,512]{1,0:T(8,128)(2,1)}, u32[]{:S(2)}, u32[]{:S(2)}) collective-permute-start(bf16[272,512]{1,0:T(8,128)(2,1)} %get-tuple-element.237), channel_id=1, source_target_pairs={{0,12},{4,0},{8,4},{12,8},{1,13},{5,1},{9,5},{13,9},{2,14},{6,2},{... | collective-permute-start | bytes 835592 | tf_op jit(solution)/shard_map/ppermute | solution.py:429
  9.7 11.5 %copy.48 = bf16[64,16,2,2048]{3,1,2,0:T(8,128)(2,1)} copy(bf16[64,16,2,2048]{3,2,1,0:T(2,128)(2,1)} %bitcast.183) | data formatting | bytes 16777216 | tf_op jit(solution)/shard_map/reshape | solution.py:432
  27.4 5.3 %collective-permute-done.1 = bf16[272,512]{1,0:T(8,128)(2,1)} collective-permute-done((bf16[272,512]{1,0:T(8,128)(2,1)S(1)}, bf16[272,512]{1,0:T(8,128)(2,1)}, u32[]{:S(2)}, u32[]{:S(2)}) %collective-permute-start.1) | collective-permute-done | bytes 278560 | tf_op jit(solution)/shard_map/ppermute | solution.py:429
  37.0 9.8 %project.2 = (bf16[2,256,1408]{2,1,0:T(8,128)(2,1)}, bf16[2,256,1024]{2,1,0:T(8,128)(2,1)}) custom-call(s32[6]{0:T(128)} %stack.136.where, bf16[4,272,512]{2,1,0:T(8,128)(2,1)} %copy-done.6, bf16[4,272,512]{2,1,0:T(8,128)(2,1)} %collective-permute-done.3.refs_1_, bf16[1024,256]{1,0:T(8,128)(2,1)} %refs_2_.3, bf16[64,2,16,2048]{3,2,1,0:T(8,128)(2,1)} %bitcast.181, ...), custom_call_target="tpu_custom_call" | custom-call | flops 3187671040 | bytes 10878976 | tf_op jit(solution)/shard_map/project/pallas_call | solution.py:119
  54.4 3.8 %collective-permute-start.4 = (bf16[128,1024]{1,0:T(8,128)(2,1)}, bf16[128,1024]{1,0:T(8,128)(2,1)}, u32[]{:S(2)}, u32[]{:S(2)}) collective-permute-start(bf16[128,1024]{1,0:T(8,128)(2,1)} %get-tuple-element.231), channel_id=1, source_target_pairs={{0,4},{4,0},{8,12},{12,8},{1,5},{5,1},{9,13},{13,9},{2,6},{6,2},{1... | collective-permute-start | bytes 786440 | tf_op jit(solution)/shard_map/ppermute | solution.py:507
  65.0 20.2 %project.3 = (bf16[2,1024,1408]{2,1,0:T(8,128)(2,1)}, bf16[2,1024,1024]{2,1,0:T(8,128)(2,1)}) custom-call(s32[6]{0:T(128)} %stack.136.where, bf16[4,272,512]{2,1,0:T(8,128)(2,1)} %copy-done.6, bf16[4,272,512]{2,1,0:T(8,128)(2,1)} %collective-permute-done.3.refs_1_, bf16[1024,256]{1,0:T(8,128)(2,1)} %refs_2_.3, bf16[64,2,16,2048]{3,2,1,0:T(8,128)(2,1)} %bitcast.182, ...), custom_call_target="tpu_custom_call" | custom-call | flops 9563013120 | bytes 18350080 | tf_op jit(solution)/shard_map/project/pallas_call | solution.py:119
  97.1 5.2 %collective-permute-done.8 = bf16[128,1024]{1,0:T(8,128)(2,1)S(1)} collective-permute-done((bf16[128,1024]{1,0:T(8,128)(2,1)}, bf16[128,1024]{1,0:T(8,128)(2,1)S(1)}, u32[]{:S(2)}, u32[]{:S(2)}) %collective-permute-start.8) | collective-permute-done | bytes 262176 | tf_op jit(solution)/shard_map/ppermute | solution.py:507
  114.8 4.1 %collective-permute-done.12 = bf16[128,1024]{1,0:T(8,128)(2,1)S(1)} collective-permute-done((bf16[128,1024]{1,0:T(8,128)(2,1)S(1)}, bf16[128,1024]{1,0:T(8,128)(2,1)S(1)}, u32[]{:S(2)}, u32[]{:S(2)}) %collective-permute-start.12) | collective-permute-done | bytes 262176 | tf_op jit(solution)/shard_map/ppermute | solution.py:507
  129.0 4.8 %scan_block.8 = (bf16[128,1024]{1,0:T(8,128)(2,1)}, f32[128,1024]{1,0:T(8,128)}, f32[8,1280]{1,0:T(8,128)}) custom-call(bf16[128,1024]{1,0:T(8,128)(2,1)} %copy-done.34, bf16[128,1408]{1,0:T(8,128)(2,1)} %copy-done.27, f32[8,1280]{1,0:T(8,128)} %fusion.40.tail, f32[128,1024]{1,0:T(8,128)} %bitcast.189, f32[1,128]{1,0:T(1,128)} %get-tuple-element.245.index, ...), custom_call_target="tpu_custom_call" | custom-call | flops 134217728 | bytes 2097152 | tf_op jit(solution)/shard_map/scan_block/pallas_call | solution.py:273
  147.8 4.9 %scan_block.9 = (bf16[128,1024]{1,0:T(8,128)(2,1)}, f32[128,1024]{1,0:T(8,128)}, f32[8,1280]{1,0:T(8,128)}) custom-call(bf16[128,2048]{1,0:T(8,128)(2,1)} %get-tuple-element.119.gates, bf16[128,1408]{1,0:T(8,128)(2,1)} %copy-done.28, f32[8,1280]{1,0:T(8,128)} %get-tuple-element.124.tail, f32[128,1024]{1,0:T(8,128)} %get-tuple-element.125.state, ...), custom_call_target="tpu_custom_call" | custom-call | flops 134217728 | bytes 2097152 | tf_op jit(solution)/shard_map/scan_block/pallas_call | solution.py:273
  167.2 4.9 %scan_block.10 = (bf16[128,1024]{1,0:T(8,128)(2,1)}, f32[128,1024]{1,0:T(8,128)}, f32[8,1280]{1,0:T(8,128)}) custom-call(bf16[128,2048]{1,0:T(8,128)(2,1)} %get-tuple-element.128.gates, bf16[128,1408]{1,0:T(8,128)(2,1)} %copy-done.29, f32[8,1280]{1,0:T(8,128)} %get-tuple-element.133.tail, f32[128,1024]{1,0:T(8,128)} %get-tuple-element.134.state, ...), custom_call_target="tpu_custom_call" | custom-call | flops 134217728 | bytes 2097152 | tf_op jit(solution)/shard_map/scan_block/pallas_call | solution.py:273
  187.5 4.9 %scan_block.11 = (bf16[128,1024]{1,0:T(8,128)(2,1)}, f32[128,1024]{1,0:T(8,128)}, f32[8,1280]{1,0:T(8,128)}) custom-call(bf16[128,2048]{1,0:T(8,128)(2,1)} %get-tuple-element.137.gates, bf16[128,1408]{1,0:T(8,128)(2,1)} %copy-done.30, f32[8,1280]{1,0:T(8,128)} %get-tuple-element.142.tail, f32[128,1024]{1,0:T(8,128)} %get-tuple-element.143.state, ...), custom_call_target="tpu_custom_call" | custom-call | flops 134217728 | bytes 2097152 | tf_op jit(solution)/shard_map/scan_block/pallas_call | solution.py:273
  206.0 4.9 %scan_block.12 = (bf16[128,1024]{1,0:T(8,128)(2,1)}, f32[128,1024]{1,0:T(8,128)}, f32[8,1280]{1,0:T(8,128)}) custom-call(bf16[128,2048]{1,0:T(8,128)(2,1)} %get-tuple-element.146.gates, bf16[128,1408]{1,0:T(8,128)(2,1)} %copy-done.31, f32[8,1280]{1,0:T(8,128)} %get-tuple-element.151.tail, f32[128,1024]{1,0:T(8,128)} %get-tuple-element.152.state, ...), custom_call_target="tpu_custom_call" | custom-call | flops 134217728 | bytes 2097152 | tf_op jit(solution)/shard_map/scan_block/pallas_call | solution.py:273
  224.5 4.9 %scan_block.13 = (bf16[128,1024]{1,0:T(8,128)(2,1)}, f32[128,1024]{1,0:T(8,128)}, f32[8,1280]{1,0:T(8,128)}) custom-call(bf16[128,2048]{1,0:T(8,128)(2,1)} %get-tuple-element.155.gates, bf16[128,1408]{1,0:T(8,128)(2,1)} %copy-done.32, f32[8,1280]{1,0:T(8,128)} %get-tuple-element.160.tail, f32[128,1024]{1,0:T(8,128)} %get-tuple-element.161.state, ...), custom_call_target="tpu_custom_call" | custom-call | flops 134217728 | bytes 2097152 | tf_op jit(solution)/shard_map/scan_block/pallas_call | solution.py:273
  240.3 4.9 %scan_block.14 = (bf16[128,1024]{1,0:T(8,128)(2,1)}, f32[128,1024]{1,0:T(8,128)}, f32[8,1280]{1,0:T(8,128)}) custom-call(bf16[128,2048]{1,0:T(8,128)(2,1)} %get-tuple-element.163.gates, bf16[128,1408]{1,0:T(8,128)(2,1)} %get-tuple-element.192.sums, f32[8,1280]{1,0:T(8,128)} %get-tuple-element.164.tail, f32[128,1024]{1,0:T(8,128)} %get-tuple-element.165.state, ...), custom_call_target="tpu_custom_call" | custom-call | flops 134217728 | bytes 2097152 | tf_op jit(solution)/shard_map/scan_block/pallas_call | solution.py:273
  251.0 4.9 %scan_block.15 = (bf16[128,1024]{1,0:T(8,128)(2,1)}, f32[128,1024]{1,0:T(8,128)}, f32[8,1280]{1,0:T(8,128)}) custom-call(bf16[128,1024]{1,0:T(8,128)(2,1)} %fusion.26.gates, bf16[128,1408]{1,0:T(8,128)(2,1)} %get-tuple-element.193.sums, f32[8,1280]{1,0:T(8,128)} %get-tuple-element.172.tail, f32[128,1024]{1,0:T(8,128)} %get-tuple-element.173.state, ...), custom_call_target="tpu_custom_call" | custom-call | flops 134217728 | bytes 2097152 | tf_op jit(solution)/shard_map/scan_block/pallas_call | solution.py:273
  260.5 8.0 %output_block.3 = bf16[512,1152]{1,0:T(8,128)(2,1)} custom-call(s32[1]{0:T(128)} %bitcast.where, bf16[128,2048]{1,0:T(8,128)(2,1)} %get-tuple-element.118.refs_0_.refs_4_, bf16[128,2048]{1,0:T(8,128)(2,1)} %copy-done.8, bf16[128,2048]{1,0:T(8,128)(2,1)} %copy-done.10, bf16[128,2048]{1,0:T(8,128)(2,1)} %copy-done.2, ...), custom_call_target="tpu_custom_call" | custom-call | flops 2147483648 | bytes 8388608 | tf_op jit(solution)/shard_map/output_block/pallas_call | solution.py:349
  281.1 6.4 %output_block.4 = bf16[256,1152]{1,0:T(8,128)(2,1)} custom-call(s32[1]{0:T(128)} %bitcast.where, bf16[128,2048]{1,0:T(8,128)(2,1)} %get-tuple-element.154.refs_0_.refs_4_, bf16[128,2048]{1,0:T(8,128)(2,1)} %copy-done.4, bf16[128,2048]{1,0:T(8,128)(2,1)} %copy-done.16, bf16[128,1024]{1,0:T(8,128)(2,1)} %copy-done.14, ...), custom_call_target="tpu_custom_call" | custom-call | flops 1073741824 | bytes 6291456 | tf_op jit(solution)/shard_map/output_block/pallas_call | solution.py:349
  291.3 5.2 %collective-permute-done.49.refs_11_.refs_15_ = bf16[128,1024]{1,0:T(8,128)(2,1)S(1)} collective-permute-done((bf16[128,1024]{1,0:T(8,128)(2,1)}, bf16[128,1024]{1,0:T(8,128)(2,1)S(1)}, u32[]{:S(2)}, u32[]{:S(2)}) %collective-permute-start.49) | collective-permute-done | bytes 262176 | tf_op jit(solution)/shard_map/ppermute | solution.py:507
  297.7 6.0 %output_block.5 = bf16[256,1152]{1,0:T(8,128)(2,1)} custom-call(s32[1]{0:T(128)} %bitcast.where, bf16[128,1024]{1,0:T(8,128)(2,1)} %copy-done.20, bf16[128,1024]{1,0:T(8,128)(2,1)} %copy-done.14, bf16[128,1024]{1,0:T(8,128)(2,1)} %copy-done.35, bf16[128,1024]{1,0:T(8,128)(2,1)} %copy-done.36, bf16[128,1024]{1,0:T(8,128)(2,1)} %copy-done.20, ...), custom_call_target="tpu_custom_call" | custom-call | flops 1073741824 | bytes 6291456 | tf_op jit(solution)/shard_map/output_block/pallas_call | solution.py:349
  303.8 4.0 %collective-permute-start.50 = (bf16[256,1152]{1,0:T(8,128)(2,1)}, bf16[256,1152]{1,0:T(8,128)(2,1)S(1)}, u32[]{:S(2)}, u32[]{:S(2)}) collective-permute-start(bf16[256,1152]{1,0:T(8,128)(2,1)} %output_block.5), channel_id=1, source_target_pairs={{0,1},{2,3},{4,5},{6,7},{8,9},{10,11},{12,13},{14,15},{16,17},{18,... | collective-permute-start | bytes 1769480 | tf_op jit(solution)/shard_map/ppermute | solution.py:599
  311.6 5.4 %collective-permute-start.53 = (bf16[256,1152]{1,0:T(8,128)(2,1)S(1)}, bf16[256,1152]{1,0:T(8,128)(2,1)}, u32[]{:S(2)}, u32[]{:S(2)}) collective-permute-start(bf16[256,1152]{1,0:T(8,128)(2,1)S(1)} %add_convert_fusion.1), channel_id=1, source_target_pairs={{0,2},{4,6},{8,10},{12,14},{16,18},{20,22},{24,26},{28,30}} | collective-permute-start | bytes 1769480 | tf_op jit(solution)/shard_map/ppermute | solution.py:601
  321.4 4.1 %collective-permute-done.55 = bf16[256,1152]{1,0:T(8,128)(2,1)S(1)} collective-permute-done((bf16[256,1152]{1,0:T(8,128)(2,1)S(1)}, bf16[256,1152]{1,0:T(8,128)(2,1)S(1)}, u32[]{:S(2)}, u32[]{:S(2)}) %collective-permute-start.55) | collective-permute-done | bytes 589856 | tf_op jit(solution)/shard_map/ppermute | solution.py:595
  325.5 4.1 %collective-permute-done.53 = bf16[256,1152]{1,0:T(8,128)(2,1)} collective-permute-done((bf16[256,1152]{1,0:T(8,128)(2,1)S(1)}, bf16[256,1152]{1,0:T(8,128)(2,1)}, u32[]{:S(2)}, u32[]{:S(2)}) %collective-permute-start.53) | collective-permute-done | bytes 589856 | tf_op jit(solution)/shard_map/ppermute | solution.py:601
  (288 shorter events, 184.2 us)
Async XLA Ops:
  3.6 23.8 %collective-permute-start.2 = (bf16[272,512]{1,0:T(8,128)(2,1)}, bf16[272,512]{1,0:T(8,128)(2,1)}, u32[]{:S(2)}, u32[]{:S(2)}) collective-permute-start(bf16[272,512]{1,0:T(8,128)(2,1)} %get-tuple-element.237), channel_id=1, source_target_pairs={{0,12},{4,0},{8,4},{12,8},{1,13},{5,1},{9,5},{13,9},{2,14},{6,2},{... | collective-permute-start | bytes 835592 | tf_op jit(solution)/shard_map/ppermute | solution.py:429
  8.7 24.0 %collective-permute-start.1 = (bf16[272,512]{1,0:T(8,128)(2,1)S(1)}, bf16[272,512]{1,0:T(8,128)(2,1)}, u32[]{:S(2)}, u32[]{:S(2)}) collective-permute-start(bf16[272,512]{1,0:T(8,128)(2,1)S(1)} %get-tuple-element.236), channel_id=1, source_target_pairs={{0,8},{4,12},{8,0},{12,4},{1,9},{5,13},{9,1},{13,5},{2,10},{6,14},... | collective-permute-start | bytes 835592 | tf_op jit(solution)/shard_map/ppermute | solution.py:429
  8.7 24.0 %collective-permute-start = (bf16[272,512]{1,0:T(8,128)(2,1)S(1)}, bf16[272,512]{1,0:T(8,128)(2,1)}, u32[]{:S(2)}, u32[]{:S(2)}) collective-permute-start(bf16[272,512]{1,0:T(8,128)(2,1)S(1)} %get-tuple-element.235), channel_id=1, source_target_pairs={{0,4},{4,8},{8,12},{12,0},{1,5},{5,9},{9,13},{13,1},{2,6},{6,10},{... | collective-permute-start | bytes 835592 | tf_op jit(solution)/shard_map/ppermute | solution.py:429
  54.4 30.8 %collective-permute-start.4 = (bf16[128,1024]{1,0:T(8,128)(2,1)}, bf16[128,1024]{1,0:T(8,128)(2,1)}, u32[]{:S(2)}, u32[]{:S(2)}) collective-permute-start(bf16[128,1024]{1,0:T(8,128)(2,1)} %get-tuple-element.231), channel_id=1, source_target_pairs={{0,4},{4,0},{8,12},{12,8},{1,5},{5,1},{9,13},{13,9},{2,6},{6,2},{1... | collective-permute-start | bytes 786440 | tf_op jit(solution)/shard_map/ppermute | solution.py:507
  58.2 27.0 %collective-permute-start.5 = (bf16[128,1024]{1,0:T(8,128)(2,1)}, bf16[128,1024]{1,0:T(8,128)(2,1)}, u32[]{:S(2)}, u32[]{:S(2)}) collective-permute-start(bf16[128,1024]{1,0:T(8,128)(2,1)} %get-tuple-element.230), channel_id=1, source_target_pairs={{4,8},{8,4},{5,9},{9,5},{6,10},{10,6},{7,11},{11,7},{20,24},{24,20... | collective-permute-start | bytes 786440 | tf_op jit(solution)/shard_map/ppermute | solution.py:508
  60.9 24.3 %collective-permute-start.10 = (bf16[128,1408]{1,0:T(8,128)(2,1)}, bf16[128,1408]{1,0:T(8,128)(2,1)S(1)}, u32[]{:S(2)}, u32[]{:S(2)}) collective-permute-start(bf16[128,1408]{1,0:T(8,128)(2,1)} %get-tuple-element.219), channel_id=1, source_target_pairs={{0,4},{4,0},{8,12},{12,8},{1,5},{5,1},{9,13},{13,9},{2,6},{6,2},{1... | collective-permute-start | bytes 1081352 | tf_op jit(solution)/shard_map/ppermute | solution.py:507
  64.1 21.1 %collective-permute-start.11 = (bf16[128,1408]{1,0:T(8,128)(2,1)}, bf16[128,1408]{1,0:T(8,128)(2,1)S(1)}, u32[]{:S(2)}, u32[]{:S(2)}) collective-permute-start(bf16[128,1408]{1,0:T(8,128)(2,1)} %get-tuple-element.218), channel_id=1, source_target_pairs={{4,8},{8,4},{5,9},{9,5},{6,10},{10,6},{7,11},{11,7},{20,24},{24,20... | collective-permute-start | bytes 1081352 | tf_op jit(solution)/shard_map/ppermute | solution.py:508
  86.5 15.8 %collective-permute-start.14 = (bf16[128,1408]{1,0:T(8,128)(2,1)S(1)}, bf16[128,1408]{1,0:T(8,128)(2,1)S(1)}, u32[]{:S(2)}, u32[]{:S(2)}) collective-permute-start(bf16[128,1408]{1,0:T(8,128)(2,1)S(1)} %get-tuple-element.207), channel_id=1, source_target_pairs={{0,4},{4,0},{8,12},{12,8},{1,5},{5,1},{9,13},{13,9},{2,6},{6,2},{1... | collective-permute-start | bytes 1081352 | tf_op jit(solution)/shard_map/ppermute | solution.py:507
  120.2 22.5 %collective-permute-start.22 = (bf16[128,1408]{1,0:T(8,128)(2,1)S(1)}, bf16[128,1408]{1,0:T(8,128)(2,1)S(1)}, u32[]{:S(2)}, u32[]{:S(2)}) collective-permute-start(bf16[128,1408]{1,0:T(8,128)(2,1)S(1)} %get-tuple-element.203), channel_id=1, source_target_pairs={{0,4},{4,0},{8,12},{12,8},{1,5},{5,1},{9,13},{13,9},{2,6},{6,2},{1... | collective-permute-start | bytes 1081352 | tf_op jit(solution)/shard_map/ppermute | solution.py:507
  123.9 18.8 %collective-permute-start.23 = (bf16[128,1408]{1,0:T(8,128)(2,1)S(1)}, bf16[128,1408]{1,0:T(8,128)(2,1)S(1)}, u32[]{:S(2)}, u32[]{:S(2)}) collective-permute-start(bf16[128,1408]{1,0:T(8,128)(2,1)S(1)} %get-tuple-element.202.sums), channel_id=1, source_target_pairs={{4,8},{8,4},{5,9},{9,5},{6,10},{10,6},{7,11},{11,7},{20,24},{24,20... | collective-permute-start | bytes 1081352 | tf_op jit(solution)/shard_map/ppermute | solution.py:508
  144.0 18.2 %collective-permute-start.26 = (bf16[128,1408]{1,0:T(8,128)(2,1)S(1)}, bf16[128,1408]{1,0:T(8,128)(2,1)S(1)}, u32[]{:S(2)}, u32[]{:S(2)}) collective-permute-start(bf16[128,1408]{1,0:T(8,128)(2,1)S(1)} %get-tuple-element.201), channel_id=1, source_target_pairs={{0,4},{4,0},{8,12},{12,8},{1,5},{5,1},{9,13},{13,9},{2,6},{6,2},{1... | collective-permute-start | bytes 1081352 | tf_op jit(solution)/shard_map/ppermute | solution.py:507
  146.4 15.8 %collective-permute-start.27 = (bf16[128,1408]{1,0:T(8,128)(2,1)S(1)}, bf16[128,1408]{1,0:T(8,128)(2,1)S(1)}, u32[]{:S(2)}, u32[]{:S(2)}) collective-permute-start(bf16[128,1408]{1,0:T(8,128)(2,1)S(1)} %get-tuple-element.200.sums), channel_id=1, source_target_pairs={{4,8},{8,4},{5,9},{9,5},{6,10},{10,6},{7,11},{11,7},{20,24},{24,20... | collective-permute-start | bytes 1081352 | tf_op jit(solution)/shard_map/ppermute | solution.py:508
  158.1 15.4 %collective-permute-start.24 = (bf16[128,2048]{1,0:T(8,128)(2,1)}, bf16[128,2048]{1,0:T(8,128)(2,1)S(1)}, u32[]{:S(2)}, u32[]{:S(2)}) collective-permute-start(bf16[128,2048]{1,0:T(8,128)(2,1)} %get-tuple-element.127.refs_8_.refs_12_), channel_id=1, source_target_pairs={{0,4},{4,0},{8,12},{12,8},{1,5},{5,1},{9,13},{13,9},{2,6},{6,2},{1... | collective-permute-start | bytes 1572872 | tf_op jit(solution)/shard_map/ppermute | solution.py:507
  163.5 18.3 %collective-permute-start.30 = (bf16[128,1408]{1,0:T(8,128)(2,1)S(1)}, bf16[128,1408]{1,0:T(8,128)(2,1)S(1)}, u32[]{:S(2)}, u32[]{:S(2)}) collective-permute-start(bf16[128,1408]{1,0:T(8,128)(2,1)S(1)} %get-tuple-element.199), channel_id=1, source_target_pairs={{0,4},{4,0},{8,12},{12,8},{1,5},{5,1},{9,13},{13,9},{2,6},{6,2},{1... | collective-permute-start | bytes 1081352 | tf_op jit(solution)/shard_map/ppermute | solution.py:507
  183.1 17.7 %collective-permute-start.34 = (bf16[128,1408]{1,0:T(8,128)(2,1)S(1)}, bf16[128,1408]{1,0:T(8,128)(2,1)S(1)}, u32[]{:S(2)}, u32[]{:S(2)}) collective-permute-start(bf16[128,1408]{1,0:T(8,128)(2,1)S(1)} %get-tuple-element.197), channel_id=1, source_target_pairs={{0,4},{4,0},{8,12},{12,8},{1,5},{5,1},{9,13},{13,9},{2,6},{6,2},{1... | collective-permute-start | bytes 1081352 | tf_op jit(solution)/shard_map/ppermute | solution.py:507
  202.1 17.7 %collective-permute-start.38 = (bf16[128,1408]{1,0:T(8,128)(2,1)S(1)}, bf16[128,1408]{1,0:T(8,128)(2,1)S(1)}, u32[]{:S(2)}, u32[]{:S(2)}) collective-permute-start(bf16[128,1408]{1,0:T(8,128)(2,1)S(1)} %get-tuple-element.195), channel_id=1, source_target_pairs={{0,4},{4,0},{8,12},{12,8},{1,5},{5,1},{9,13},{13,9},{2,6},{6,2},{1... | collective-permute-start | bytes 1081352 | tf_op jit(solution)/shard_map/ppermute | solution.py:507
  220.8 17.3 %collective-permute-start.42 = (bf16[128,1408]{1,0:T(8,128)(2,1)S(1)}, bf16[128,1408]{1,0:T(8,128)(2,1)S(1)}, u32[]{:S(2)}, u32[]{:S(2)}) collective-permute-start(bf16[128,1408]{1,0:T(8,128)(2,1)S(1)} %fusion.8), channel_id=1, source_target_pairs={{0,4},{4,0},{8,12},{12,8},{1,5},{5,1},{9,13},{13,9},{2,6},{6,2},{1... | collective-permute-start | bytes 1081352 | tf_op jit(solution)/shard_map/ppermute | solution.py:507
  270.8 33.0 %collective-permute-start.54 = (bf16[256,1152]{1,0:T(8,128)(2,1)}, bf16[256,1152]{1,0:T(8,128)(2,1)}, u32[]{:S(2)}, u32[]{:S(2)}) collective-permute-start(bf16[256,1152]{1,0:T(8,128)(2,1)} %constant_dynamic-slice_fusion.2), channel_id=1, source_target_pairs={{0,1},{1,0},{2,3},{3,2},{4,5},{5,4},{6,7},{7,6},{8,9},{9,8},{10,11... | collective-permute-start | bytes 1769480 | tf_op jit(solution)/shard_map/ppermute | solution.py:593
  270.8 16.7 %collective-permute-start.47 = (bf16[128,1024]{1,0:T(8,128)(2,1)S(1)}, bf16[128,1024]{1,0:T(8,128)(2,1)S(1)}, u32[]{:S(2)}, u32[]{:S(2)}) collective-permute-start(bf16[128,1024]{1,0:T(8,128)(2,1)S(1)} %collective-permute-done.45.refs_2_.refs_6_), channel_id=1, source_target_pairs={{0,4},{4,0},{8,12},{12,8},{1,5},{5,1},{9,13},{13,9},{2,6},{6,2},{1... | collective-permute-start | bytes 786440 | tf_op jit(solution)/shard_map/ppermute | solution.py:507
  275.0 42.1 %collective-permute-start.56 = (bf16[1024,128]{0,1:T(8,128)(2,1)}, bf16[1024,128]{0,1:T(8,128)(2,1)}, u32[]{:S(2)}, u32[]{:S(2)}) collective-permute-start(bf16[1024,128]{0,1:T(8,128)(2,1)} %get-tuple-element.227), channel_id=1, source_target_pairs={{0,4},{12,8},{1,5},{13,9},{2,6},{14,10},{3,7},{15,11},{16,20},{28,... | collective-permute-start | bytes 786440 | tf_op jit(solution)/shard_map/ppermute | solution.py:588
  278.8 39.8 %collective-permute-start.57 = (bf16[1024,128]{0,1:T(8,128)(2,1)}, bf16[1024,128]{0,1:T(8,128)(2,1)}, u32[]{:S(2)}, u32[]{:S(2)}) collective-permute-start(bf16[1024,128]{0,1:T(8,128)(2,1)} %get-tuple-element.226), channel_id=1, source_target_pairs={{0,8},{12,4},{1,9},{13,5},{2,10},{14,6},{3,11},{15,7},{16,24},{28,... | collective-permute-start | bytes 786440 | tf_op jit(solution)/shard_map/ppermute | solution.py:588
  288.4 30.3 %collective-permute-start.58 = (bf16[1024,128]{0,1:T(8,128)(2,1)}, bf16[1024,128]{0,1:T(8,128)(2,1)}, u32[]{:S(2)}, u32[]{:S(2)}) collective-permute-start(bf16[1024,128]{0,1:T(8,128)(2,1)} %get-tuple-element.224), channel_id=1, source_target_pairs={{0,12},{12,0},{1,13},{13,1},{2,14},{14,2},{3,15},{15,3},{16,28},{2... | collective-permute-start | bytes 786440 | tf_op jit(solution)/shard_map/ppermute | solution.py:588
  309.1 16.5 %collective-permute-start.55 = (bf16[256,1152]{1,0:T(8,128)(2,1)S(1)}, bf16[256,1152]{1,0:T(8,128)(2,1)S(1)}, u32[]{:S(2)}, u32[]{:S(2)}) collective-permute-start(bf16[256,1152]{1,0:T(8,128)(2,1)S(1)} %add_convert_fusion), channel_id=1, source_target_pairs={{2,0},{3,1},{6,4},{7,5},{10,8},{11,9},{14,12},{15,13},{18,16},{19,... | collective-permute-start | bytes 1769480 | tf_op jit(solution)/shard_map/ppermute | solution.py:595
  311.6 18.0 %collective-permute-start.53 = (bf16[256,1152]{1,0:T(8,128)(2,1)S(1)}, bf16[256,1152]{1,0:T(8,128)(2,1)}, u32[]{:S(2)}, u32[]{:S(2)}) collective-permute-start(bf16[256,1152]{1,0:T(8,128)(2,1)S(1)} %add_convert_fusion.1), channel_id=1, source_target_pairs={{0,2},{4,6},{8,10},{12,14},{16,18},{20,22},{24,26},{28,30}} | collective-permute-start | bytes 1769480 | tf_op jit(solution)/shard_map/ppermute | solution.py:601
  (84 other events, 779.3 us)

commit v4 on v3

--- a/solution.py
+++ b/solution.py
@@ -144,8 +144,18 @@
     )(where, mine, other, down, weight, up, small, *earlier)
 
 
-def merge_kernel(where, gate_a, gate_b, came_a, came_b, gated, go_a, go_b, *, passing):
+def merge_kernel(
+    where, gate_a, gate_b, from_a, from_b, gated, go_a, go_b, came_a, came_b, sems, *, passing
+):
     ch = gated.shape[1]
+    copies = [
+        pltpu.make_async_copy(source, target, sems.at[k])
+        for k, (source, target) in enumerate(((from_a, came_a), (from_b, came_b)))
+    ]
+    for copy in copies:
+        copy.start()
+    for copy in copies:
+        copy.wait()
     go_a[:, :ch] = (gate_a[0].astype(f32) + came_b[:, :ch].astype(f32)).astype(bf16)
     go_b[:, :ch] = (gate_b[0].astype(f32) + came_a[:, :ch].astype(f32)).astype(bf16)
     own = gated[...]
@@ -171,9 +181,13 @@
             in_specs=[
                 pl.BlockSpec((1, BLOCK, ch), lambda b, w: (0, w[1], 0)),
                 pl.BlockSpec((1, BLOCK, ch), lambda b, w: (1, w[2], 0)),
-                whole(came[0]), whole(came[1]), whole(gated),
+                *(pl.BlockSpec(memory_space=pl.ANY) for _ in came), whole(gated),
             ],
             out_specs=[whole(out), whole(out)],
+            scratch_shapes=[
+                *(pltpu.VMEM(a.shape, bf16) for a in came),
+                pltpu.SemaphoreType.DMA((2,)),
+            ],
         ),
         cost_estimate=pl.CostEstimate(
             flops=4 * BLOCK * ch, bytes_accessed=22 * BLOCK * ch, transcendentals=0
@@ -352,7 +366,11 @@
         grid_spec=pltpu.PrefetchScalarGridSpec(
             num_scalar_prefetch=1,
             grid=(1,),
-            in_specs=[*(pl.BlockSpec(memory_space=pl.ANY) for _ in blocks), whole(gain), pl.BlockSpec(memory_space=pl.ANY)],
+            in_specs=[
+                *(pl.BlockSpec(memory_space=pl.ANY) for _ in blocks),
+                whole(gain),
+                pl.BlockSpec(memory_space=pl.ANY),
+            ],
             out_specs=pl.BlockSpec((count * BLOCK, width + LANES), lambda b, w: (0, 0)),
             scratch_shapes=[
                 pltpu.VMEM((count * BLOCK, 2 * ch), bf16),
@@ -588,20 +606,15 @@
         landed.append(lax.ppermute(leaving, "seq", [(0, k), (n - 1, n - 1 - k)]))
 
     if chips == 2:
-        keep = own(outs[0], core * size, size, 0)
-        give = own(outs[0], (1 - core) * size, size, 0)
-        back = lax.ppermute(give, "tensor", swap)
-        both = added(keep, back)
-        came = lax.ppermute(both, "tensor", [(2, 0), (3, 1)])
-        total = both.astype(f32) + came.astype(f32)
-        for t in range(2, shards):
-            give = [(j, j ^ 1) for j in range(shards) if j % 2 != t % 2]
-            back = lax.ppermute(outs[t - 1], "tensor", give)
-            both = added(outs[t - 1], back)
-            came = lax.ppermute(both, "tensor", [(t ^ 2, t)])
-            total = jnp.where(shard == t, both.astype(f32) + came.astype(f32), total)
-            if t == shards - 2:
-                total = lax.optimization_barrier(total)
+        first, *rest = outs
+        keep = own(first, core * size, size, 0), jnp.where(core == 0, *rest)
+        give = own(first, (1 - core) * size, size, 0), jnp.where(core == 0, *rest[::-1])
+        back = lax.ppermute(jnp.concatenate(give, axis=0), "tensor", swap)
+        both = added(jnp.concatenate(keep, axis=0), back)
+        total = own(both, chip * size, size, 0).astype(f32)
+        give = own(both, (1 - chip) * size, size, 0)
+        came = lax.ppermute(give, "tensor", [(j, j ^ 2) for j in range(shards)])
+        total = total + came.astype(f32)
     else:
         halves = []
         for k in range(chips):

time: 336 us -> 329 us (0.979)
  starting transfers between devices: 109 us -> 95.2 us
  Pallas kernels: 109 us -> 114 us
    ppermute x6 -> x2, starting transfers between devices: 13.5 us -> 1.49 us  [the longest x1 1.49 us: per_device(): came = lax.ppermute(give, 'tensor', [(j, j ^ 2) for j in range(shards)])]
    ppermute x3, waiting for transfers between devices: 0.01 us -> 8.06 us  [per_device(): landed.append(lax.ppermute(leaving, 'seq', [(0, k), (n - 1, n - 1 - k)]))]
    ppermute x6 -> x2, waiting for transfers between devices: 8.19 us -> 2.69 us  [the longest x1 2.68 us: per_device(): came = lax.ppermute(give, 'tensor', [(j, j ^ 2) for j in range(shards)])]
    pallas_call x6, Pallas kernels: 19.2 us -> 24.5 us  [merge(): pl.pallas_call(functools.partial(merge_kernel, passing=passing), out_shap...]
    convert_element_type x17 -> x15, other arithmetic: 21.9 us -> 21.2 us  [added(): return (a.astype(f32) + b.astype(f32)).astype(bf16)]
    unnamed x108 -> x110, local copies, waits for them, and re-layouts: 9.94 us -> 10.4 us
  transfers between devices with their start and end apart: 59 -> 55, of which waited for: 15 -> 15; matrix products, arithmetic and copies ran while one was open for 16% -> 16% of each run, Pallas kernels for 30% -> 30%
where the time goes in v4:
time: 329 us; the launch traced here: 327 us
  Pallas kernels  114 us (35%)
  starting transfers between devices  95.2 us (29%)
  other arithmetic  40.6 us (12%)
  waiting for transfers between devices  39.6 us (12%)
  local copies, waits for them, and re-layouts  35.4 us (11%)
    ppermute x24, starting transfers between devices, onward(): from_a = lax.ppermute(pair[0], 'seq', pairs_a)  62.2 us
    pallas_call x8, Pallas kernels, scan_block(): pl.pallas_call(scan_kernel, out_shape=outs, grid=(1,), in_specs=[pl.Block...  39 us
    pallas_call x2, Pallas kernels, project(): pl.pallas_call(functools.partial(project_kernel, rows=rows, first=first,...  30 us
    pallas_call x6, Pallas kernels, merge(): pl.pallas_call(functools.partial(merge_kernel, passing=passing), out_shap...  24.5 us
    ppermute x24, waiting for transfers between devices, onward(): from_a = lax.ppermute(pair[0], 'seq', pairs_a)  22.4 us
    convert_element_type x15, other arithmetic, added(): return (a.astype(f32) + b.astype(f32)).astype(bf16)  21.2 us
    pallas_call x3, Pallas kernels, output_block(): pl.pallas_call(functools.partial(output_kernel, n=n, count=count), out_sh...  20.5 us
    ppermute x22, starting transfers between devices, onward(): from_b = lax.ppermute(pair[1], 'seq', pairs_b)  15.9 us
  transfers between devices with their start and end apart: 55, of which 15 were waited for; matrix products, arithmetic and copies ran while one was open for 16% of the time, Pallas kernels for 30%

profile of v4, /device:TPU:0, one launch (start us, length us, event | category | flops | bytes accessed | tf_op | source)
XLA Modules:
  0.0 326.8 jit_solution(9096445895791562179)
XLA Ops:
  3.6 5.1 %collective-permute-start.2 = (bf16[272,512]{1,0:T(8,128)(2,1)}, bf16[272,512]{1,0:T(8,128)(2,1)}, u32[]{:S(2)}, u32[]{:S(2)}) collective-permute-start(bf16[272,512]{1,0:T(8,128)(2,1)} %get-tuple-element.241), channel_id=1, source_target_pairs={{0,12},{4,0},{8,4},{12,8},{1,13},{5,1},{9,5},{13,9},{2,14},{6,2},{... | collective-permute-start | bytes 835592 | tf_op jit(solution)/shard_map/ppermute | solution.py:447
  9.7 11.5 %copy.48 = bf16[64,16,2,2048]{3,1,2,0:T(8,128)(2,1)} copy(bf16[64,16,2,2048]{3,2,1,0:T(2,128)(2,1)} %bitcast.183) | data formatting | bytes 16777216 | tf_op jit(solution)/shard_map/reshape | solution.py:450
  27.4 5.3 %collective-permute-done.1 = bf16[272,512]{1,0:T(8,128)(2,1)} collective-permute-done((bf16[272,512]{1,0:T(8,128)(2,1)S(1)}, bf16[272,512]{1,0:T(8,128)(2,1)}, u32[]{:S(2)}, u32[]{:S(2)}) %collective-permute-start.1) | collective-permute-done | bytes 278560 | tf_op jit(solution)/shard_map/ppermute | solution.py:447
  37.0 9.8 %project.2 = (bf16[2,256,1408]{2,1,0:T(8,128)(2,1)}, bf16[2,256,1024]{2,1,0:T(8,128)(2,1)}) custom-call(s32[6]{0:T(128)} %stack.131.where, bf16[4,272,512]{2,1,0:T(8,128)(2,1)} %copy-done.6, bf16[4,272,512]{2,1,0:T(8,128)(2,1)} %collective-permute-done.3.refs_1_, bf16[1024,256]{1,0:T(8,128)(2,1)} %refs_2_.3, bf16[64,2,16,2048]{3,2,1,0:T(8,128)(2,1)} %bitcast.181, ...), custom_call_target="tpu_custom_call" | custom-call | flops 3187671040 | bytes 10878976 | tf_op jit(solution)/shard_map/project/pallas_call | solution.py:119
  65.5 20.1 %project.3 = (bf16[2,1024,1408]{2,1,0:T(8,128)(2,1)}, bf16[2,1024,1024]{2,1,0:T(8,128)(2,1)}) custom-call(s32[6]{0:T(128)} %stack.131.where, bf16[4,272,512]{2,1,0:T(8,128)(2,1)} %copy-done.6, bf16[4,272,512]{2,1,0:T(8,128)(2,1)} %collective-permute-done.3.refs_1_, bf16[1024,256]{1,0:T(8,128)(2,1)} %refs_2_.3, bf16[64,2,16,2048]{3,2,1,0:T(8,128)(2,1)} %bitcast.182, ...), custom_call_target="tpu_custom_call" | custom-call | flops 9563013120 | bytes 18350080 | tf_op jit(solution)/shard_map/project/pallas_call | solution.py:119
  96.2 5.6 %collective-permute-done.8 = bf16[128,1024]{1,0:T(8,128)(2,1)S(1)} collective-permute-done((bf16[128,1024]{1,0:T(8,128)(2,1)}, bf16[128,1024]{1,0:T(8,128)(2,1)S(1)}, u32[]{:S(2)}, u32[]{:S(2)}) %collective-permute-start.8) | collective-permute-done | bytes 262176 | tf_op jit(solution)/shard_map/ppermute | solution.py:525
  115.2 4.0 %collective-permute-done.12 = bf16[128,1024]{1,0:T(8,128)(2,1)S(1)} collective-permute-done((bf16[128,1024]{1,0:T(8,128)(2,1)S(1)}, bf16[128,1024]{1,0:T(8,128)(2,1)S(1)}, u32[]{:S(2)}, u32[]{:S(2)}) %collective-permute-start.12) | collective-permute-done | bytes 262176 | tf_op jit(solution)/shard_map/ppermute | solution.py:525
  129.6 4.8 %scan_block.8 = (bf16[128,1024]{1,0:T(8,128)(2,1)}, f32[128,1024]{1,0:T(8,128)}, f32[8,1280]{1,0:T(8,128)}) custom-call(bf16[128,1024]{1,0:T(8,128)(2,1)} %copy-done.34, bf16[128,1408]{1,0:T(8,128)(2,1)} %copy-done.26, f32[8,1280]{1,0:T(8,128)} %fusion.40.tail, f32[128,1024]{1,0:T(8,128)} %bitcast.189, f32[1,128]{1,0:T(1,128)} %get-tuple-element.249.index, ...), custom_call_target="tpu_custom_call" | custom-call | flops 134217728 | bytes 2097152 | tf_op jit(solution)/shard_map/scan_block/pallas_call | solution.py:287
  149.2 4.9 %scan_block.9 = (bf16[128,1024]{1,0:T(8,128)(2,1)}, f32[128,1024]{1,0:T(8,128)}, f32[8,1280]{1,0:T(8,128)}) custom-call(bf16[128,2048]{1,0:T(8,128)(2,1)} %get-tuple-element.119.gates, bf16[128,1408]{1,0:T(8,128)(2,1)} %copy-done.27, f32[8,1280]{1,0:T(8,128)} %get-tuple-element.124.tail, f32[128,1024]{1,0:T(8,128)} %get-tuple-element.125.state, ...), custom_call_target="tpu_custom_call" | custom-call | flops 134217728 | bytes 2097152 | tf_op jit(solution)/shard_map/scan_block/pallas_call | solution.py:287
  156.8 4.1 %merge.7 = (bf16[128,2048]{1,0:T(8,128)(2,1)}, bf16[128,2048]{1,0:T(8,128)(2,1)}) custom-call(s32[3]{0:T(128)} %get-tuple-element.253.where, bf16[2,1024,1024]{2,1,0:T(8,128)(2,1)} %get-tuple-element.101.gate_a.gate_b, bf16[2,1024,1024]{2,1,0:T(8,128)(2,1)} %get-tuple-element.101.gate_a.gate_b, bf16[128,2048]{1,0:T(8,128)(2,1)} %copy-done.8, ...), custom_call_target="tpu_custom_call" | custom-call | flops 524288 | bytes 2883584 | tf_op jit(solution)/shard_map/merge/pallas_call | solution.py:175
  169.4 4.9 %scan_block.10 = (bf16[128,1024]{1,0:T(8,128)(2,1)}, f32[128,1024]{1,0:T(8,128)}, f32[8,1280]{1,0:T(8,128)}) custom-call(bf16[128,2048]{1,0:T(8,128)(2,1)} %get-tuple-element.128.gates, bf16[128,1408]{1,0:T(8,128)(2,1)} %copy-done.28, f32[8,1280]{1,0:T(8,128)} %get-tuple-element.133.tail, f32[128,1024]{1,0:T(8,128)} %get-tuple-element.134.state, ...), custom_call_target="tpu_custom_call" | custom-call | flops 134217728 | bytes 2097152 | tf_op jit(solution)/shard_map/scan_block/pallas_call | solution.py:287
  175.8 4.1 %merge.8 = (bf16[128,2048]{1,0:T(8,128)(2,1)}, bf16[128,2048]{1,0:T(8,128)(2,1)}) custom-call(s32[3]{0:T(128)} %get-tuple-element.252.where, bf16[2,1024,1024]{2,1,0:T(8,128)(2,1)} %get-tuple-element.101.gate_a.gate_b, bf16[2,1024,1024]{2,1,0:T(8,128)(2,1)} %get-tuple-element.101.gate_a.gate_b, bf16[128,2048]{1,0:T(8,128)(2,1)} %copy-done.9, ...), custom_call_target="tpu_custom_call" | custom-call | flops 524288 | bytes 2883584 | tf_op jit(solution)/shard_map/merge/pallas_call | solution.py:175
  189.0 4.9 %scan_block.11 = (bf16[128,1024]{1,0:T(8,128)(2,1)}, f32[128,1024]{1,0:T(8,128)}, f32[8,1280]{1,0:T(8,128)}) custom-call(bf16[128,2048]{1,0:T(8,128)(2,1)} %get-tuple-element.137.gates, bf16[128,1408]{1,0:T(8,128)(2,1)} %copy-done.29, f32[8,1280]{1,0:T(8,128)} %get-tuple-element.142.tail, f32[128,1024]{1,0:T(8,128)} %get-tuple-element.143.state, ...), custom_call_target="tpu_custom_call" | custom-call | flops 134217728 | bytes 2097152 | tf_op jit(solution)/shard_map/scan_block/pallas_call | solution.py:287
  194.9 4.1 %merge.9 = (bf16[128,2048]{1,0:T(8,128)(2,1)}, bf16[128,2048]{1,0:T(8,128)(2,1)}) custom-call(s32[3]{0:T(128)} %get-tuple-element.251.where, bf16[2,1024,1024]{2,1,0:T(8,128)(2,1)} %get-tuple-element.101.gate_a.gate_b, bf16[2,1024,1024]{2,1,0:T(8,128)(2,1)} %get-tuple-element.101.gate_a.gate_b, bf16[128,2048]{1,0:T(8,128)(2,1)} %copy-done.2, ...), custom_call_target="tpu_custom_call" | custom-call | flops 524288 | bytes 2883584 | tf_op jit(solution)/shard_map/merge/pallas_call | solution.py:175
  207.6 4.9 %scan_block.12 = (bf16[128,1024]{1,0:T(8,128)(2,1)}, f32[128,1024]{1,0:T(8,128)}, f32[8,1280]{1,0:T(8,128)}) custom-call(bf16[128,2048]{1,0:T(8,128)(2,1)} %get-tuple-element.146.gates, bf16[128,1408]{1,0:T(8,128)(2,1)} %copy-done.30, f32[8,1280]{1,0:T(8,128)} %get-tuple-element.151.tail, f32[128,1024]{1,0:T(8,128)} %get-tuple-element.152.state, ...), custom_call_target="tpu_custom_call" | custom-call | flops 134217728 | bytes 2097152 | tf_op jit(solution)/shard_map/scan_block/pallas_call | solution.py:287
  213.7 4.1 %merge.10 = (bf16[128,2048]{1,0:T(8,128)(2,1)}, bf16[128,2048]{1,0:T(8,128)(2,1)}) custom-call(s32[3]{0:T(128)} %get-tuple-element.250.where, bf16[2,1024,1024]{2,1,0:T(8,128)(2,1)} %get-tuple-element.101.gate_a.gate_b, bf16[2,1024,1024]{2,1,0:T(8,128)(2,1)} %get-tuple-element.101.gate_a.gate_b, bf16[128,2048]{1,0:T(8,128)(2,1)} %copy-done.3, ...), custom_call_target="tpu_custom_call" | custom-call | flops 524288 | bytes 2883584 | tf_op jit(solution)/shard_map/merge/pallas_call | solution.py:175
  226.0 4.9 %scan_block.13 = (bf16[128,1024]{1,0:T(8,128)(2,1)}, f32[128,1024]{1,0:T(8,128)}, f32[8,1280]{1,0:T(8,128)}) custom-call(bf16[128,2048]{1,0:T(8,128)(2,1)} %get-tuple-element.155.gates, bf16[128,1408]{1,0:T(8,128)(2,1)} %copy-done.31, f32[8,1280]{1,0:T(8,128)} %get-tuple-element.160.tail, f32[128,1024]{1,0:T(8,128)} %get-tuple-element.161.state, ...), custom_call_target="tpu_custom_call" | custom-call | flops 134217728 | bytes 2097152 | tf_op jit(solution)/shard_map/scan_block/pallas_call | solution.py:287
  232.7 4.1 %merge.11 = (bf16[128,2048]{1,0:T(8,128)(2,1)}, bf16[128,2048]{1,0:T(8,128)(2,1)}) custom-call(s32[3]{0:T(128)} %pad_add_fusion.where, bf16[2,1024,1024]{2,1,0:T(8,128)(2,1)} %get-tuple-element.101.gate_a.gate_b, bf16[2,1024,1024]{2,1,0:T(8,128)(2,1)} %get-tuple-element.101.gate_a.gate_b, bf16[128,2048]{1,0:T(8,128)(2,1)} %copy-done.4, ...), custom_call_target="tpu_custom_call" | custom-call | flops 524288 | bytes 2883584 | tf_op jit(solution)/shard_map/merge/pallas_call | solution.py:175
  241.5 4.9 %scan_block.14 = (bf16[128,1024]{1,0:T(8,128)(2,1)}, f32[128,1024]{1,0:T(8,128)}, f32[8,1280]{1,0:T(8,128)}) custom-call(bf16[128,2048]{1,0:T(8,128)(2,1)} %get-tuple-element.164.gates, bf16[128,1408]{1,0:T(8,128)(2,1)} %get-tuple-element.193.sums, f32[8,1280]{1,0:T(8,128)} %get-tuple-element.167.tail, f32[128,1024]{1,0:T(8,128)} %get-tuple-element.168.state, ...), custom_call_target="tpu_custom_call" | custom-call | flops 134217728 | bytes 2097152 | tf_op jit(solution)/shard_map/scan_block/pallas_call | solution.py:287
  253.6 4.9 %scan_block.15 = (bf16[128,1024]{1,0:T(8,128)(2,1)}, f32[128,1024]{1,0:T(8,128)}, f32[8,1280]{1,0:T(8,128)}) custom-call(bf16[128,1024]{1,0:T(8,128)(2,1)} %fusion.32.gates, bf16[128,1408]{1,0:T(8,128)(2,1)} %get-tuple-element.192.sums, f32[8,1280]{1,0:T(8,128)} %get-tuple-element.169.tail, f32[128,1024]{1,0:T(8,128)} %get-tuple-element.170.state, ...), custom_call_target="tpu_custom_call" | custom-call | flops 134217728 | bytes 2097152 | tf_op jit(solution)/shard_map/scan_block/pallas_call | solution.py:287
  262.1 8.0 %output_block.3 = bf16[512,1152]{1,0:T(8,128)(2,1)} custom-call(s32[1]{0:T(128)} %bitcast.70.where, bf16[128,2048]{1,0:T(8,128)(2,1)} %get-tuple-element.118.refs_0_.refs_4_, bf16[128,2048]{1,0:T(8,128)(2,1)} %copy-done.8, bf16[128,2048]{1,0:T(8,128)(2,1)} %copy-done.10, bf16[128,2048]{1,0:T(8,128)(2,1)} %copy-done.2, ...), custom_call_target="tpu_custom_call" | custom-call | flops 2147483648 | bytes 8388608 | tf_op jit(solution)/shard_map/output_block/pallas_call | solution.py:363
  273.2 6.5 %output_block.4 = bf16[256,1152]{1,0:T(8,128)(2,1)} custom-call(s32[1]{0:T(128)} %bitcast.70.where, bf16[128,2048]{1,0:T(8,128)(2,1)} %get-tuple-element.154.refs_0_.refs_4_, bf16[128,2048]{1,0:T(8,128)(2,1)} %copy-done.4, bf16[128,2048]{1,0:T(8,128)(2,1)} %copy-done.16, bf16[128,1024]{1,0:T(8,128)(2,1)} %copy-done.14, ...), custom_call_target="tpu_custom_call" | custom-call | flops 1073741824 | bytes 6291456 | tf_op jit(solution)/shard_map/output_block/pallas_call | solution.py:363
  286.9 6.0 %output_block.5 = bf16[256,1152]{1,0:T(8,128)(2,1)} custom-call(s32[1]{0:T(128)} %bitcast.70.where, bf16[128,1024]{1,0:T(8,128)(2,1)} %copy-done.20, bf16[128,1024]{1,0:T(8,128)(2,1)} %copy-done.14, bf16[128,1024]{1,0:T(8,128)(2,1)} %copy-done.35, bf16[128,1024]{1,0:T(8,128)(2,1)} %copy-done.36, bf16[128,1024]{1,0:T(8,128)(2,1)} %copy-done.20, ...), custom_call_target="tpu_custom_call" | custom-call | flops 1073741824 | bytes 6291456 | tf_op jit(solution)/shard_map/output_block/pallas_call | solution.py:363
  312.2 6.9 %collective-permute-done.54 = bf16[1024,128]{0,1:T(8,128)(2,1)} collective-permute-done((bf16[1024,128]{0,1:T(8,128)(2,1)S(1)}, bf16[1024,128]{0,1:T(8,128)(2,1)}, u32[]{:S(2)}, u32[]{:S(2)}) %collective-permute-start.54) | collective-permute-done | bytes 262176 | tf_op jit(solution)/shard_map/ppermute | solution.py:606
  (282 shorter events, 176.3 us)
Async XLA Ops:
  3.6 23.8 %collective-permute-start.2 = (bf16[272,512]{1,0:T(8,128)(2,1)}, bf16[272,512]{1,0:T(8,128)(2,1)}, u32[]{:S(2)}, u32[]{:S(2)}) collective-permute-start(bf16[272,512]{1,0:T(8,128)(2,1)} %get-tuple-element.241), channel_id=1, source_target_pairs={{0,12},{4,0},{8,4},{12,8},{1,13},{5,1},{9,5},{13,9},{2,14},{6,2},{... | collective-permute-start | bytes 835592 | tf_op jit(solution)/shard_map/ppermute | solution.py:447
  8.7 24.0 %collective-permute-start.1 = (bf16[272,512]{1,0:T(8,128)(2,1)S(1)}, bf16[272,512]{1,0:T(8,128)(2,1)}, u32[]{:S(2)}, u32[]{:S(2)}) collective-permute-start(bf16[272,512]{1,0:T(8,128)(2,1)S(1)} %get-tuple-element.240), channel_id=1, source_target_pairs={{0,8},{4,12},{8,0},{12,4},{1,9},{5,13},{9,1},{13,5},{2,10},{6,14},... | collective-permute-start | bytes 835592 | tf_op jit(solution)/shard_map/ppermute | solution.py:447
  8.7 24.0 %collective-permute-start = (bf16[272,512]{1,0:T(8,128)(2,1)S(1)}, bf16[272,512]{1,0:T(8,128)(2,1)}, u32[]{:S(2)}, u32[]{:S(2)}) collective-permute-start(bf16[272,512]{1,0:T(8,128)(2,1)S(1)} %get-tuple-element.239), channel_id=1, source_target_pairs={{0,4},{4,8},{8,12},{12,0},{1,5},{5,9},{9,13},{13,1},{2,6},{6,10},{... | collective-permute-start | bytes 835592 | tf_op jit(solution)/shard_map/ppermute | solution.py:447
  51.6 34.1 %collective-permute-start.4 = (bf16[128,1024]{1,0:T(8,128)(2,1)}, bf16[128,1024]{1,0:T(8,128)(2,1)}, u32[]{:S(2)}, u32[]{:S(2)}) collective-permute-start(bf16[128,1024]{1,0:T(8,128)(2,1)} %get-tuple-element.235), channel_id=1, source_target_pairs={{0,4},{4,0},{8,12},{12,8},{1,5},{5,1},{9,13},{13,9},{2,6},{6,2},{1... | collective-permute-start | bytes 786440 | tf_op jit(solution)/shard_map/ppermute | solution.py:525
  55.4 30.2 %collective-permute-start.5 = (bf16[128,1024]{1,0:T(8,128)(2,1)}, bf16[128,1024]{1,0:T(8,128)(2,1)}, u32[]{:S(2)}, u32[]{:S(2)}) collective-permute-start(bf16[128,1024]{1,0:T(8,128)(2,1)} %get-tuple-element.234), channel_id=1, source_target_pairs={{4,8},{8,4},{5,9},{9,5},{6,10},{10,6},{7,11},{11,7},{20,24},{24,20... | collective-permute-start | bytes 786440 | tf_op jit(solution)/shard_map/ppermute | solution.py:526
  60.7 25.0 %collective-permute-start.10 = (bf16[128,1408]{1,0:T(8,128)(2,1)S(1)}, bf16[128,1408]{1,0:T(8,128)(2,1)S(1)}, u32[]{:S(2)}, u32[]{:S(2)}) collective-permute-start(bf16[128,1408]{1,0:T(8,128)(2,1)S(1)} %get-tuple-element.219), channel_id=1, source_target_pairs={{0,4},{4,0},{8,12},{12,8},{1,5},{5,1},{9,13},{13,9},{2,6},{6,2},{1... | collective-permute-start | bytes 1081352 | tf_op jit(solution)/shard_map/ppermute | solution.py:525
  64.6 21.0 %collective-permute-start.11 = (bf16[128,1408]{1,0:T(8,128)(2,1)S(1)}, bf16[128,1408]{1,0:T(8,128)(2,1)S(1)}, u32[]{:S(2)}, u32[]{:S(2)}) collective-permute-start(bf16[128,1408]{1,0:T(8,128)(2,1)S(1)} %get-tuple-element.218), channel_id=1, source_target_pairs={{4,8},{8,4},{5,9},{9,5},{6,10},{10,6},{7,11},{11,7},{20,24},{24,20... | collective-permute-start | bytes 1081352 | tf_op jit(solution)/shard_map/ppermute | solution.py:526
  87.0 14.8 %collective-permute-start.14 = (bf16[128,1408]{1,0:T(8,128)(2,1)S(1)}, bf16[128,1408]{1,0:T(8,128)(2,1)S(1)}, u32[]{:S(2)}, u32[]{:S(2)}) collective-permute-start(bf16[128,1408]{1,0:T(8,128)(2,1)S(1)} %get-tuple-element.207), channel_id=1, source_target_pairs={{0,4},{4,0},{8,12},{12,8},{1,5},{5,1},{9,13},{13,9},{2,6},{6,2},{1... | collective-permute-start | bytes 1081352 | tf_op jit(solution)/shard_map/ppermute | solution.py:525
  103.9 15.3 %collective-permute-start.18 = (bf16[128,1408]{1,0:T(8,128)(2,1)S(1)}, bf16[128,1408]{1,0:T(8,128)(2,1)S(1)}, u32[]{:S(2)}, u32[]{:S(2)}) collective-permute-start(bf16[128,1408]{1,0:T(8,128)(2,1)S(1)} %get-tuple-element.205), channel_id=1, source_target_pairs={{0,4},{4,0},{8,12},{12,8},{1,5},{5,1},{9,13},{13,9},{2,6},{6,2},{1... | collective-permute-start | bytes 1081352 | tf_op jit(solution)/shard_map/ppermute | solution.py:525
  120.5 23.8 %collective-permute-start.22 = (bf16[128,1408]{1,0:T(8,128)(2,1)S(1)}, bf16[128,1408]{1,0:T(8,128)(2,1)S(1)}, u32[]{:S(2)}, u32[]{:S(2)}) collective-permute-start(bf16[128,1408]{1,0:T(8,128)(2,1)S(1)} %get-tuple-element.203), channel_id=1, source_target_pairs={{0,4},{4,0},{8,12},{12,8},{1,5},{5,1},{9,13},{13,9},{2,6},{6,2},{1... | collective-permute-start | bytes 1081352 | tf_op jit(solution)/shard_map/ppermute | solution.py:525
  124.2 20.1 %collective-permute-start.23 = (bf16[128,1408]{1,0:T(8,128)(2,1)S(1)}, bf16[128,1408]{1,0:T(8,128)(2,1)S(1)}, u32[]{:S(2)}, u32[]{:S(2)}) collective-permute-start(bf16[128,1408]{1,0:T(8,128)(2,1)S(1)} %get-tuple-element.202.sums), channel_id=1, source_target_pairs={{4,8},{8,4},{5,9},{9,5},{6,10},{10,6},{7,11},{11,7},{20,24},{24,20... | collective-permute-start | bytes 1081352 | tf_op jit(solution)/shard_map/ppermute | solution.py:526
  139.9 15.9 %collective-permute-start.20 = (bf16[128,2048]{1,0:T(8,128)(2,1)}, bf16[128,2048]{1,0:T(8,128)(2,1)S(1)}, u32[]{:S(2)}, u32[]{:S(2)}) collective-permute-start(bf16[128,2048]{1,0:T(8,128)(2,1)} %get-tuple-element.118.refs_0_.refs_4_), channel_id=1, source_target_pairs={{0,4},{4,0},{8,12},{12,8},{1,5},{5,1},{9,13},{13,9},{2,6},{6,2},{1... | collective-permute-start | bytes 1572872 | tf_op jit(solution)/shard_map/ppermute | solution.py:525
  145.6 19.6 %collective-permute-start.26 = (bf16[128,1408]{1,0:T(8,128)(2,1)S(1)}, bf16[128,1408]{1,0:T(8,128)(2,1)S(1)}, u32[]{:S(2)}, u32[]{:S(2)}) collective-permute-start(bf16[128,1408]{1,0:T(8,128)(2,1)S(1)} %get-tuple-element.201), channel_id=1, source_target_pairs={{0,4},{4,0},{8,12},{12,8},{1,5},{5,1},{9,13},{13,9},{2,6},{6,2},{1... | collective-permute-start | bytes 1081352 | tf_op jit(solution)/shard_map/ppermute | solution.py:525
  147.8 17.4 %collective-permute-start.27 = (bf16[128,1408]{1,0:T(8,128)(2,1)S(1)}, bf16[128,1408]{1,0:T(8,128)(2,1)S(1)}, u32[]{:S(2)}, u32[]{:S(2)}) collective-permute-start(bf16[128,1408]{1,0:T(8,128)(2,1)S(1)} %get-tuple-element.200.sums), channel_id=1, source_target_pairs={{4,8},{8,4},{5,9},{9,5},{6,10},{10,6},{7,11},{11,7},{20,24},{24,20... | collective-permute-start | bytes 1081352 | tf_op jit(solution)/shard_map/ppermute | solution.py:526
  166.5 17.7 %collective-permute-start.30 = (bf16[128,1408]{1,0:T(8,128)(2,1)S(1)}, bf16[128,1408]{1,0:T(8,128)(2,1)S(1)}, u32[]{:S(2)}, u32[]{:S(2)}) collective-permute-start(bf16[128,1408]{1,0:T(8,128)(2,1)S(1)} %get-tuple-element.199), channel_id=1, source_target_pairs={{0,4},{4,0},{8,12},{12,8},{1,5},{5,1},{9,13},{13,9},{2,6},{6,2},{1... | collective-permute-start | bytes 1081352 | tf_op jit(solution)/shard_map/ppermute | solution.py:525
  168.7 15.4 %collective-permute-start.31 = (bf16[128,1408]{1,0:T(8,128)(2,1)S(1)}, bf16[128,1408]{1,0:T(8,128)(2,1)S(1)}, u32[]{:S(2)}, u32[]{:S(2)}) collective-permute-start(bf16[128,1408]{1,0:T(8,128)(2,1)S(1)} %get-tuple-element.198.sums), channel_id=1, source_target_pairs={{4,8},{8,4},{5,9},{9,5},{6,10},{10,6},{7,11},{11,7},{20,24},{24,20... | collective-permute-start | bytes 1081352 | tf_op jit(solution)/shard_map/ppermute | solution.py:526
  185.5 17.6 %collective-permute-start.34 = (bf16[128,1408]{1,0:T(8,128)(2,1)S(1)}, bf16[128,1408]{1,0:T(8,128)(2,1)S(1)}, u32[]{:S(2)}, u32[]{:S(2)}) collective-permute-start(bf16[128,1408]{1,0:T(8,128)(2,1)S(1)} %get-tuple-element.197), channel_id=1, source_target_pairs={{0,4},{4,0},{8,12},{12,8},{1,5},{5,1},{9,13},{13,9},{2,6},{6,2},{1... | collective-permute-start | bytes 1081352 | tf_op jit(solution)/shard_map/ppermute | solution.py:525
  187.7 15.4 %collective-permute-start.35 = (bf16[128,1408]{1,0:T(8,128)(2,1)S(1)}, bf16[128,1408]{1,0:T(8,128)(2,1)S(1)}, u32[]{:S(2)}, u32[]{:S(2)}) collective-permute-start(bf16[128,1408]{1,0:T(8,128)(2,1)S(1)} %get-tuple-element.196.sums), channel_id=1, source_target_pairs={{4,8},{8,4},{5,9},{9,5},{6,10},{10,6},{7,11},{11,7},{20,24},{24,20... | collective-permute-start | bytes 1081352 | tf_op jit(solution)/shard_map/ppermute | solution.py:526
  204.4 17.7 %collective-permute-start.38 = (bf16[128,1408]{1,0:T(8,128)(2,1)S(1)}, bf16[128,1408]{1,0:T(8,128)(2,1)S(1)}, u32[]{:S(2)}, u32[]{:S(2)}) collective-permute-start(bf16[128,1408]{1,0:T(8,128)(2,1)S(1)} %get-tuple-element.195), channel_id=1, source_target_pairs={{0,4},{4,0},{8,12},{12,8},{1,5},{5,1},{9,13},{13,9},{2,6},{6,2},{1... | collective-permute-start | bytes 1081352 | tf_op jit(solution)/shard_map/ppermute | solution.py:525
  206.7 15.5 %collective-permute-start.39 = (bf16[128,1408]{1,0:T(8,128)(2,1)S(1)}, bf16[128,1408]{1,0:T(8,128)(2,1)S(1)}, u32[]{:S(2)}, u32[]{:S(2)}) collective-permute-start(bf16[128,1408]{1,0:T(8,128)(2,1)S(1)} %get-tuple-element.194.sums), channel_id=1, source_target_pairs={{4,8},{8,4},{5,9},{9,5},{6,10},{10,6},{7,11},{11,7},{20,24},{24,20... | collective-permute-start | bytes 1081352 | tf_op jit(solution)/shard_map/ppermute | solution.py:526
  223.2 16.1 %collective-permute-start.42 = (bf16[128,1408]{1,0:T(8,128)(2,1)S(1)}, bf16[128,1408]{1,0:T(8,128)(2,1)S(1)}, u32[]{:S(2)}, u32[]{:S(2)}) collective-permute-start(bf16[128,1408]{1,0:T(8,128)(2,1)S(1)} %fusion.9), channel_id=1, source_target_pairs={{0,4},{4,0},{8,12},{12,8},{1,5},{5,1},{9,13},{13,9},{2,6},{6,2},{1... | collective-permute-start | bytes 1081352 | tf_op jit(solution)/shard_map/ppermute | solution.py:525
  296.6 14.4 %collective-permute-start.52 = (bf16[1024,128]{0,1:T(8,128)(2,1)}, bf16[1024,128]{0,1:T(8,128)(2,1)}, u32[]{:S(2)}, u32[]{:S(2)}) collective-permute-start(bf16[1024,128]{0,1:T(8,128)(2,1)} %get-tuple-element.231), channel_id=1, source_target_pairs={{0,4},{12,8},{1,5},{13,9},{2,6},{14,10},{3,7},{15,11},{16,20},{28,... | collective-permute-start | bytes 786440 | tf_op jit(solution)/shard_map/ppermute | solution.py:606
  303.5 15.6 %collective-permute-start.54 = (bf16[1024,128]{0,1:T(8,128)(2,1)S(1)}, bf16[1024,128]{0,1:T(8,128)(2,1)}, u32[]{:S(2)}, u32[]{:S(2)}) collective-permute-start(bf16[1024,128]{0,1:T(8,128)(2,1)S(1)} %get-tuple-element.228), channel_id=1, source_target_pairs={{0,12},{12,0},{1,13},{13,1},{2,14},{14,2},{3,15},{15,3},{16,28},{2... | collective-permute-start | bytes 786440 | tf_op jit(solution)/shard_map/ppermute | solution.py:606
  309.5 15.0 %collective-permute-start.51 = (bf16[256,1152]{1,0:T(8,128)(2,1)}, bf16[256,1152]{1,0:T(8,128)(2,1)}, u32[]{:S(2)}, u32[]{:S(2)}) collective-permute-start(bf16[256,1152]{1,0:T(8,128)(2,1)} %constant_dynamic-slice_fusion.2), channel_id=1, source_target_pairs={{0,2},{1,3},{2,0},{3,1},{4,6},{5,7},{6,4},{7,5},{8,10},{9,11},{10,... | collective-permute-start | bytes 1769480 | tf_op jit(solution)/shard_map/ppermute | solution.py:616
  (81 other events, 653.0 us)

commit v5 on v3

--- a/solution.py
+++ b/solution.py
@@ -352,7 +352,11 @@
         grid_spec=pltpu.PrefetchScalarGridSpec(
             num_scalar_prefetch=1,
             grid=(1,),
-            in_specs=[*(pl.BlockSpec(memory_space=pl.ANY) for _ in blocks), whole(gain), pl.BlockSpec(memory_space=pl.ANY)],
+            in_specs=[
+                *(pl.BlockSpec(memory_space=pl.ANY) for _ in blocks),
+                whole(gain),
+                pl.BlockSpec(memory_space=pl.ANY),
+            ],
             out_specs=pl.BlockSpec((count * BLOCK, width + LANES), lambda b, w: (0, 0)),
             scratch_shapes=[
                 pltpu.VMEM((count * BLOCK, 2 * ch), bf16),
@@ -453,7 +457,7 @@
     order = jnp.stack(order)
     projected = ()
     versions = []
-    for count in (1, n - 1):
+    for count in (n,):
         projected = project(
             order, mine, other, adapter_down_maps, weight, up, small, rows, ch, count, projected
         )
@@ -588,20 +592,18 @@
         landed.append(lax.ppermute(leaving, "seq", [(0, k), (n - 1, n - 1 - k)]))
 
     if chips == 2:
-        keep = own(outs[0], core * size, size, 0)
-        give = own(outs[0], (1 - core) * size, size, 0)
+        first, *rest = outs
+        keep = own(first, core * size, size, 0)
+        give = own(first, (1 - core) * size, size, 0)
         back = lax.ppermute(give, "tensor", swap)
-        both = added(keep, back)
-        came = lax.ppermute(both, "tensor", [(2, 0), (3, 1)])
-        total = both.astype(f32) + came.astype(f32)
-        for t in range(2, shards):
-            give = [(j, j ^ 1) for j in range(shards) if j % 2 != t % 2]
-            back = lax.ppermute(outs[t - 1], "tensor", give)
-            both = added(outs[t - 1], back)
-            came = lax.ppermute(both, "tensor", [(t ^ 2, t)])
-            total = jnp.where(shard == t, both.astype(f32) + came.astype(f32), total)
-            if t == shards - 2:
-                total = lax.optimization_barrier(total)
+        both_first = added(keep, back)
+        give = jnp.where(core == 0, *rest[::-1])
+        back = lax.ppermute(give, "tensor", swap)
+        both_last = added(jnp.where(core == 0, *rest), back)
+        total = jnp.where(chip == 0, both_first, both_last).astype(f32)
+        both = give = jnp.where(chip == 0, both_last, both_first)
+        came = lax.ppermute(give, "tensor", [(j, j ^ 2) for j in range(shards)])
+        total = total + came.astype(f32)
     else:
         halves = []
         for k in range(chips):

time: 336 us -> 337 us (level)
  waiting for transfers between devices: 36.8 us -> 50 us
  Pallas kernels: 109 us -> 102 us
  starting transfers between devices: 109 us -> 105 us
    ppermute x24, waiting for transfers between devices: 22 us -> 39.4 us  [onward(): from_a = lax.ppermute(pair[0], 'seq', pairs_a)]
    ppermute x5 -> x1, starting transfers between devices: 13.5 us -> 1.5 us  [per_device(): came = lax.ppermute(give, 'tensor', [(j, j ^ 2) for j in range(shards)])]
    ppermute x3, waiting for transfers between devices: 0.01 us -> 8.57 us  [per_device(): landed.append(lax.ppermute(leaving, 'seq', [(0, k), (n - 1, n - 1 - k)]))]
    ppermute x5 -> x1, waiting for transfers between devices: 8.19 us -> 0.01 us  [per_device(): came = lax.ppermute(give, 'tensor', [(j, j ^ 2) for j in range(shards)])]
    ppermute x24, starting transfers between devices: 63.4 us -> 71 us  [onward(): from_a = lax.ppermute(pair[0], 'seq', pairs_a)]
    pallas_call x2 -> x1, Pallas kernels: 30 us -> 23.4 us  [project(): pl.pallas_call(functools.partial(project_kernel, rows=rows, first=first,...]
    ppermute x3, waiting for transfers between devices: 5.31 us -> 0.01 us  [per_device(): pieces.append(lax.ppermute(piece((here + k) % n), 'seq', pairs))]
    convert_element_type x17 -> x14, other arithmetic: 21.9 us -> 18.8 us  [added(): return (a.astype(f32) + b.astype(f32)).astype(bf16)]
  transfers between devices with their start and end apart: 59 -> 56, of which waited for: 15 -> 15; matrix products, arithmetic and copies ran while one was open for 16% -> 17% of each run, Pallas kernels for 30% -> 22%
where the time goes in v5:
time: 337 us; the launch traced here: 335 us
  starting transfers between devices  105 us (31%)
  Pallas kernels  102 us (30%)
  waiting for transfers between devices  50 us (15%)
  other arithmetic  41.4 us (12%)
  local copies, waits for them, and re-layouts  34.8 us (10%)
    ppermute x24, starting transfers between devices, onward(): from_a = lax.ppermute(pair[0], 'seq', pairs_a)  71 us
    ppermute x24, waiting for transfers between devices, onward(): from_a = lax.ppermute(pair[0], 'seq', pairs_a)  39.4 us
    pallas_call x8, Pallas kernels, scan_block(): pl.pallas_call(scan_kernel, out_shape=outs, grid=(1,), in_specs=[pl.Block...  39 us
    pallas_call x1, Pallas kernels, project(): pl.pallas_call(functools.partial(project_kernel, rows=rows, first=first,...  23.4 us
    pallas_call x3, Pallas kernels, output_block(): pl.pallas_call(functools.partial(output_kernel, n=n, count=count), out_sh...  20.5 us
    pallas_call x6, Pallas kernels, merge(): pl.pallas_call(functools.partial(merge_kernel, passing=passing), out_shap...  19.1 us
    convert_element_type x14, other arithmetic, added(): return (a.astype(f32) + b.astype(f32)).astype(bf16)  18.8 us
    ppermute x22, starting transfers between devices, onward(): from_b = lax.ppermute(pair[1], 'seq', pairs_b)  15.2 us
  transfers between devices with their start and end apart: 56, of which 15 were waited for; matrix products, arithmetic and copies ran while one was open for 17% of the time, Pallas kernels for 22%

profile of v5, /device:TPU:0, one launch (start us, length us, event | category | flops | bytes accessed | tf_op | source)
XLA Modules:
  0.0 334.7 jit_solution(11556012031728483518)
XLA Ops:
  13.7 11.5 %copy.48 = bf16[64,16,2,2048]{3,1,2,0:T(8,128)(2,1)} copy(bf16[64,16,2,2048]{3,2,1,0:T(2,128)(2,1)} %bitcast.181) | data formatting | bytes 16777216 | tf_op jit(solution)/shard_map/reshape | solution.py:436
  33.2 23.4 %project.1 = (bf16[2,1024,1408]{2,1,0:T(8,128)(2,1)}, bf16[2,1024,1024]{2,1,0:T(8,128)(2,1)}) custom-call(s32[6]{0:T(128)} %stack.131.where, bf16[4,272,512]{2,1,0:T(8,128)(2,1)} %copy-done.29, bf16[4,272,512]{2,1,0:T(8,128)(2,1)} %collective-permute-done.3.refs_1_, bf16[1024,256]{1,0:T(8,128)(2,1)} %refs_2_.1, bf16[64,2,16,2048]{3,2,1,0:T(8,128)(2,1)} %bitcast.182, ...), custom_call_target="tpu_custom_call" | custom-call | flops 12750684160 | bytes 18350080 | tf_op jit(solution)/shard_map/project/pallas_call | solution.py:119
  57.8 5.1 %collective-permute-start.6 = (bf16[128,1408]{1,0:T(8,128)(2,1)S(1)}, bf16[128,1408]{1,0:T(8,128)(2,1)S(1)}, u32[]{:S(2)}, u32[]{:S(2)}) collective-permute-start(bf16[128,1408]{1,0:T(8,128)(2,1)S(1)} %get-tuple-element.209), channel_id=1, source_target_pairs={{0,4},{4,0},{8,12},{12,8},{1,5},{5,1},{9,13},{13,9},{2,6},{6,2},{1... | collective-permute-start | bytes 1081352 | tf_op jit(solution)/shard_map/ppermute | solution.py:511
  64.5 7.1 %collective-permute-done.6 = bf16[128,1408]{1,0:T(8,128)(2,1)S(1)} collective-permute-done((bf16[128,1408]{1,0:T(8,128)(2,1)S(1)}, bf16[128,1408]{1,0:T(8,128)(2,1)S(1)}, u32[]{:S(2)}, u32[]{:S(2)}) %collective-permute-start.6) | collective-permute-done | bytes 360480 | tf_op jit(solution)/shard_map/ppermute | solution.py:511
  72.9 3.8 %collective-permute-start.10 = (bf16[128,1408]{1,0:T(8,128)(2,1)S(1)}, bf16[128,1408]{1,0:T(8,128)(2,1)S(1)}, u32[]{:S(2)}, u32[]{:S(2)}) collective-permute-start(bf16[128,1408]{1,0:T(8,128)(2,1)S(1)} %get-tuple-element.207), channel_id=1, source_target_pairs={{0,4},{4,0},{8,12},{12,8},{1,5},{5,1},{9,13},{13,9},{2,6},{6,2},{1... | collective-permute-start | bytes 1081352 | tf_op jit(solution)/shard_map/ppermute | solution.py:511
  83.7 6.4 %collective-permute-done.4 = bf16[128,1024]{1,0:T(8,128)(2,1)S(1)} collective-permute-done((bf16[128,1024]{1,0:T(8,128)(2,1)S(1)}, bf16[128,1024]{1,0:T(8,128)(2,1)S(1)}, u32[]{:S(2)}, u32[]{:S(2)}) %collective-permute-start.4) | collective-permute-done | bytes 262176 | tf_op jit(solution)/shard_map/ppermute | solution.py:511
  91.4 3.7 %collective-permute-start.14 = (bf16[128,1408]{1,0:T(8,128)(2,1)S(1)}, bf16[128,1408]{1,0:T(8,128)(2,1)S(1)}, u32[]{:S(2)}, u32[]{:S(2)}) collective-permute-start(bf16[128,1408]{1,0:T(8,128)(2,1)S(1)} %get-tuple-element.205), channel_id=1, source_target_pairs={{0,4},{4,0},{8,12},{12,8},{1,5},{5,1},{9,13},{13,9},{2,6},{6,2},{1... | collective-permute-start | bytes 1081352 | tf_op jit(solution)/shard_map/ppermute | solution.py:511
  101.6 6.1 %collective-permute-done.8 = bf16[128,1024]{1,0:T(8,128)(2,1)S(1)} collective-permute-done((bf16[128,1024]{1,0:T(8,128)(2,1)S(1)}, bf16[128,1024]{1,0:T(8,128)(2,1)S(1)}, u32[]{:S(2)}, u32[]{:S(2)}) %collective-permute-start.8) | collective-permute-done | bytes 262176 | tf_op jit(solution)/shard_map/ppermute | solution.py:511
  109.1 3.7 %collective-permute-start.18 = (bf16[128,1408]{1,0:T(8,128)(2,1)S(1)}, bf16[128,1408]{1,0:T(8,128)(2,1)S(1)}, u32[]{:S(2)}, u32[]{:S(2)}) collective-permute-start(bf16[128,1408]{1,0:T(8,128)(2,1)S(1)} %get-tuple-element.203), channel_id=1, source_target_pairs={{0,4},{4,0},{8,12},{12,8},{1,5},{5,1},{9,13},{13,9},{2,6},{6,2},{1... | collective-permute-start | bytes 1081352 | tf_op jit(solution)/shard_map/ppermute | solution.py:511
  125.8 3.7 %collective-permute-start.22 = (bf16[128,1408]{1,0:T(8,128)(2,1)S(1)}, bf16[128,1408]{1,0:T(8,128)(2,1)S(1)}, u32[]{:S(2)}, u32[]{:S(2)}) collective-permute-start(bf16[128,1408]{1,0:T(8,128)(2,1)S(1)} %get-tuple-element.201), channel_id=1, source_target_pairs={{0,4},{4,0},{8,12},{12,8},{1,5},{5,1},{9,13},{13,9},{2,6},{6,2},{1... | collective-permute-start | bytes 1081352 | tf_op jit(solution)/shard_map/ppermute | solution.py:511
  135.0 4.8 %scan_block.8 = (bf16[128,1024]{1,0:T(8,128)(2,1)}, f32[128,1024]{1,0:T(8,128)}, f32[8,1280]{1,0:T(8,128)}) custom-call(bf16[128,1024]{1,0:T(8,128)(2,1)} %copy-done.30, bf16[128,1408]{1,0:T(8,128)(2,1)} %copy-done.23, f32[8,1280]{1,0:T(8,128)} %fusion.40.tail, f32[128,1024]{1,0:T(8,128)} %bitcast.187, f32[1,128]{1,0:T(1,128)} %get-tuple-element.243.index, ...), custom_call_target="tpu_custom_call" | custom-call | flops 134217728 | bytes 2097152 | tf_op jit(solution)/shard_map/scan_block/pallas_call | solution.py:273
  153.5 4.9 %scan_block.9 = (bf16[128,1024]{1,0:T(8,128)(2,1)}, f32[128,1024]{1,0:T(8,128)}, f32[8,1280]{1,0:T(8,128)}) custom-call(bf16[128,2048]{1,0:T(8,128)(2,1)} %get-tuple-element.115.gates, bf16[128,1408]{1,0:T(8,128)(2,1)} %copy-done.24, f32[8,1280]{1,0:T(8,128)} %get-tuple-element.120.tail, f32[128,1024]{1,0:T(8,128)} %get-tuple-element.121.state, ...), custom_call_target="tpu_custom_call" | custom-call | flops 134217728 | bytes 2097152 | tf_op jit(solution)/shard_map/scan_block/pallas_call | solution.py:273
  172.8 4.9 %scan_block.10 = (bf16[128,1024]{1,0:T(8,128)(2,1)}, f32[128,1024]{1,0:T(8,128)}, f32[8,1280]{1,0:T(8,128)}) custom-call(bf16[128,2048]{1,0:T(8,128)(2,1)} %get-tuple-element.124.gates, bf16[128,1408]{1,0:T(8,128)(2,1)} %copy-done.25, f32[8,1280]{1,0:T(8,128)} %get-tuple-element.129.tail, f32[128,1024]{1,0:T(8,128)} %get-tuple-element.130.state, ...), custom_call_target="tpu_custom_call" | custom-call | flops 134217728 | bytes 2097152 | tf_op jit(solution)/shard_map/scan_block/pallas_call | solution.py:273
  193.4 4.9 %scan_block.11 = (bf16[128,1024]{1,0:T(8,128)(2,1)}, f32[128,1024]{1,0:T(8,128)}, f32[8,1280]{1,0:T(8,128)}) custom-call(bf16[128,2048]{1,0:T(8,128)(2,1)} %get-tuple-element.133.gates, bf16[128,1408]{1,0:T(8,128)(2,1)} %copy-done.26, f32[8,1280]{1,0:T(8,128)} %get-tuple-element.138.tail, f32[128,1024]{1,0:T(8,128)} %get-tuple-element.139.state, ...), custom_call_target="tpu_custom_call" | custom-call | flops 134217728 | bytes 2097152 | tf_op jit(solution)/shard_map/scan_block/pallas_call | solution.py:273
  213.8 4.9 %scan_block.12 = (bf16[128,1024]{1,0:T(8,128)(2,1)}, f32[128,1024]{1,0:T(8,128)}, f32[8,1280]{1,0:T(8,128)}) custom-call(bf16[128,2048]{1,0:T(8,128)(2,1)} %get-tuple-element.142.gates, bf16[128,1408]{1,0:T(8,128)(2,1)} %copy-done.27, f32[8,1280]{1,0:T(8,128)} %get-tuple-element.147.tail, f32[128,1024]{1,0:T(8,128)} %get-tuple-element.148.state, ...), custom_call_target="tpu_custom_call" | custom-call | flops 134217728 | bytes 2097152 | tf_op jit(solution)/shard_map/scan_block/pallas_call | solution.py:273
  225.4 3.6 %collective-permute-start.36 = (bf16[128,2048]{1,0:T(8,128)(2,1)}, bf16[128,2048]{1,0:T(8,128)(2,1)S(1)}, u32[]{:S(2)}, u32[]{:S(2)}) collective-permute-start(bf16[128,2048]{1,0:T(8,128)(2,1)} %get-tuple-element.150.refs_0_.refs_4_), channel_id=1, source_target_pairs={{0,4},{4,0},{8,12},{12,8},{1,5},{5,1},{9,13},{13,9},{2,6},{6,2},{1... | collective-permute-start | bytes 1572872 | tf_op jit(solution)/shard_map/ppermute | solution.py:511
  234.3 4.9 %scan_block.13 = (bf16[128,1024]{1,0:T(8,128)(2,1)}, f32[128,1024]{1,0:T(8,128)}, f32[8,1280]{1,0:T(8,128)}) custom-call(bf16[128,2048]{1,0:T(8,128)(2,1)} %get-tuple-element.151.gates, bf16[128,1408]{1,0:T(8,128)(2,1)} %copy-done.28, f32[8,1280]{1,0:T(8,128)} %get-tuple-element.156.tail, f32[128,1024]{1,0:T(8,128)} %get-tuple-element.157.state, ...), custom_call_target="tpu_custom_call" | custom-call | flops 134217728 | bytes 2097152 | tf_op jit(solution)/shard_map/scan_block/pallas_call | solution.py:273
  248.0 4.9 %scan_block.14 = (bf16[128,1024]{1,0:T(8,128)(2,1)}, f32[128,1024]{1,0:T(8,128)}, f32[8,1280]{1,0:T(8,128)}) custom-call(bf16[128,2048]{1,0:T(8,128)(2,1)} %get-tuple-element.160.gates, bf16[128,1408]{1,0:T(8,128)(2,1)} %get-tuple-element.190.sums, f32[8,1280]{1,0:T(8,128)} %get-tuple-element.163.tail, f32[128,1024]{1,0:T(8,128)} %get-tuple-element.164.state, ...), custom_call_target="tpu_custom_call" | custom-call | flops 134217728 | bytes 2097152 | tf_op jit(solution)/shard_map/scan_block/pallas_call | solution.py:273
  260.5 4.9 %scan_block.15 = (bf16[128,1024]{1,0:T(8,128)(2,1)}, f32[128,1024]{1,0:T(8,128)}, f32[8,1280]{1,0:T(8,128)}) custom-call(bf16[128,1024]{1,0:T(8,128)(2,1)} %fusion.32.gates, bf16[128,1408]{1,0:T(8,128)(2,1)} %get-tuple-element.191.sums, f32[8,1280]{1,0:T(8,128)} %get-tuple-element.165.tail, f32[128,1024]{1,0:T(8,128)} %get-tuple-element.166.state, ...), custom_call_target="tpu_custom_call" | custom-call | flops 134217728 | bytes 2097152 | tf_op jit(solution)/shard_map/scan_block/pallas_call | solution.py:273
  268.7 8.1 %output_block.3 = bf16[512,1152]{1,0:T(8,128)(2,1)} custom-call(s32[1]{0:T(128)} %bitcast.70.where, bf16[128,2048]{1,0:T(8,128)(2,1)} %get-tuple-element.114.refs_0_.refs_4_, bf16[128,2048]{1,0:T(8,128)(2,1)} %copy-done.9, bf16[128,2048]{1,0:T(8,128)(2,1)} %copy-done.11, bf16[128,2048]{1,0:T(8,128)(2,1)} %copy-done.2, ...), custom_call_target="tpu_custom_call" | custom-call | flops 2147483648 | bytes 8388608 | tf_op jit(solution)/shard_map/output_block/pallas_call | solution.py:349
  279.8 6.4 %output_block.4 = bf16[256,1152]{1,0:T(8,128)(2,1)} custom-call(s32[1]{0:T(128)} %bitcast.70.where, bf16[128,2048]{1,0:T(8,128)(2,1)} %get-tuple-element.150.refs_0_.refs_4_, bf16[128,2048]{1,0:T(8,128)(2,1)} %copy-done.4, bf16[128,2048]{1,0:T(8,128)(2,1)} %copy-done.17, bf16[128,1024]{1,0:T(8,128)(2,1)} %copy-done.15, ...), custom_call_target="tpu_custom_call" | custom-call | flops 1073741824 | bytes 6291456 | tf_op jit(solution)/shard_map/output_block/pallas_call | solution.py:349
  293.4 6.0 %output_block.5 = bf16[256,1152]{1,0:T(8,128)(2,1)} custom-call(s32[1]{0:T(128)} %bitcast.70.where, bf16[128,1024]{1,0:T(8,128)(2,1)} %copy-done.19, bf16[128,1024]{1,0:T(8,128)(2,1)} %copy-done.15, bf16[128,1024]{1,0:T(8,128)(2,1)} %copy-done.31, bf16[128,1024]{1,0:T(8,128)(2,1)} %copy-done.32, bf16[128,1024]{1,0:T(8,128)(2,1)} %copy-done.19, ...), custom_call_target="tpu_custom_call" | custom-call | flops 1073741824 | bytes 6291456 | tf_op jit(solution)/shard_map/output_block/pallas_call | solution.py:349
  303.6 4.3 %collective-permute-start.53 = (bf16[1024,128]{0,1:T(8,128)(2,1)}, bf16[1024,128]{0,1:T(8,128)(2,1)}, u32[]{:S(2)}, u32[]{:S(2)}) collective-permute-start(bf16[1024,128]{0,1:T(8,128)(2,1)} %get-tuple-element.229), channel_id=1, source_target_pairs={{0,4},{12,8},{1,5},{13,9},{2,6},{14,10},{3,7},{15,11},{16,20},{28,... | collective-permute-start | bytes 786440 | tf_op jit(solution)/shard_map/ppermute | solution.py:592
  319.6 7.0 %collective-permute-done.55 = bf16[1024,128]{0,1:T(8,128)(2,1)} collective-permute-done((bf16[1024,128]{0,1:T(8,128)(2,1)}, bf16[1024,128]{0,1:T(8,128)(2,1)}, u32[]{:S(2)}, u32[]{:S(2)}) %collective-permute-start.55) | collective-permute-done | bytes 262176 | tf_op jit(solution)/shard_map/ppermute | solution.py:592
  (271 shorter events, 183.9 us)
Async XLA Ops:
  3.6 25.4 %collective-permute-start = (bf16[272,512]{1,0:T(8,128)(2,1)}, bf16[272,512]{1,0:T(8,128)(2,1)}, u32[]{:S(2)}, u32[]{:S(2)}) collective-permute-start(bf16[272,512]{1,0:T(8,128)(2,1)} %get-tuple-element.233), channel_id=1, source_target_pairs={{0,4},{4,8},{8,12},{12,0},{1,5},{5,9},{9,13},{13,1},{2,6},{6,10},{... | collective-permute-start | bytes 835592 | tf_op jit(solution)/shard_map/ppermute | solution.py:433
  6.7 22.3 %collective-permute-start.1 = (bf16[272,512]{1,0:T(8,128)(2,1)S(1)}, bf16[272,512]{1,0:T(8,128)(2,1)}, u32[]{:S(2)}, u32[]{:S(2)}) collective-permute-start(bf16[272,512]{1,0:T(8,128)(2,1)S(1)} %get-tuple-element.234), channel_id=1, source_target_pairs={{0,8},{4,12},{8,0},{12,4},{1,9},{5,13},{9,1},{13,5},{2,10},{6,14},... | collective-permute-start | bytes 835592 | tf_op jit(solution)/shard_map/ppermute | solution.py:433
  9.3 19.7 %collective-permute-start.2 = (bf16[272,512]{1,0:T(8,128)(2,1)S(1)}, bf16[272,512]{1,0:T(8,128)(2,1)}, u32[]{:S(2)}, u32[]{:S(2)}) collective-permute-start(bf16[272,512]{1,0:T(8,128)(2,1)S(1)} %get-tuple-element.235), channel_id=1, source_target_pairs={{0,12},{4,0},{8,4},{12,8},{1,13},{5,1},{9,5},{13,9},{2,14},{6,2},{... | collective-permute-start | bytes 835592 | tf_op jit(solution)/shard_map/ppermute | solution.py:433
  57.8 13.8 %collective-permute-start.6 = (bf16[128,1408]{1,0:T(8,128)(2,1)S(1)}, bf16[128,1408]{1,0:T(8,128)(2,1)S(1)}, u32[]{:S(2)}, u32[]{:S(2)}) collective-permute-start(bf16[128,1408]{1,0:T(8,128)(2,1)S(1)} %get-tuple-element.209), channel_id=1, source_target_pairs={{0,4},{4,0},{8,12},{12,8},{1,5},{5,1},{9,13},{13,9},{2,6},{6,2},{1... | collective-permute-start | bytes 1081352 | tf_op jit(solution)/shard_map/ppermute | solution.py:511
  72.9 17.3 %collective-permute-start.10 = (bf16[128,1408]{1,0:T(8,128)(2,1)S(1)}, bf16[128,1408]{1,0:T(8,128)(2,1)S(1)}, u32[]{:S(2)}, u32[]{:S(2)}) collective-permute-start(bf16[128,1408]{1,0:T(8,128)(2,1)S(1)} %get-tuple-element.207), channel_id=1, source_target_pairs={{0,4},{4,0},{8,12},{12,8},{1,5},{5,1},{9,13},{13,9},{2,6},{6,2},{1... | collective-permute-start | bytes 1081352 | tf_op jit(solution)/shard_map/ppermute | solution.py:511
  76.7 13.5 %collective-permute-start.11 = (bf16[128,1408]{1,0:T(8,128)(2,1)S(1)}, bf16[128,1408]{1,0:T(8,128)(2,1)S(1)}, u32[]{:S(2)}, u32[]{:S(2)}) collective-permute-start(bf16[128,1408]{1,0:T(8,128)(2,1)S(1)} %get-tuple-element.206), channel_id=1, source_target_pairs={{4,8},{8,4},{5,9},{9,5},{6,10},{10,6},{7,11},{11,7},{20,24},{24,20... | collective-permute-start | bytes 1081352 | tf_op jit(solution)/shard_map/ppermute | solution.py:512
  91.4 16.3 %collective-permute-start.14 = (bf16[128,1408]{1,0:T(8,128)(2,1)S(1)}, bf16[128,1408]{1,0:T(8,128)(2,1)S(1)}, u32[]{:S(2)}, u32[]{:S(2)}) collective-permute-start(bf16[128,1408]{1,0:T(8,128)(2,1)S(1)} %get-tuple-element.205), channel_id=1, source_target_pairs={{0,4},{4,0},{8,12},{12,8},{1,5},{5,1},{9,13},{13,9},{2,6},{6,2},{1... | collective-permute-start | bytes 1081352 | tf_op jit(solution)/shard_map/ppermute | solution.py:511
  109.1 15.5 %collective-permute-start.18 = (bf16[128,1408]{1,0:T(8,128)(2,1)S(1)}, bf16[128,1408]{1,0:T(8,128)(2,1)S(1)}, u32[]{:S(2)}, u32[]{:S(2)}) collective-permute-start(bf16[128,1408]{1,0:T(8,128)(2,1)S(1)} %get-tuple-element.203), channel_id=1, source_target_pairs={{0,4},{4,0},{8,12},{12,8},{1,5},{5,1},{9,13},{13,9},{2,6},{6,2},{1... | collective-permute-start | bytes 1081352 | tf_op jit(solution)/shard_map/ppermute | solution.py:511
  125.8 22.6 %collective-permute-start.22 = (bf16[128,1408]{1,0:T(8,128)(2,1)S(1)}, bf16[128,1408]{1,0:T(8,128)(2,1)S(1)}, u32[]{:S(2)}, u32[]{:S(2)}) collective-permute-start(bf16[128,1408]{1,0:T(8,128)(2,1)S(1)} %get-tuple-element.201), channel_id=1, source_target_pairs={{0,4},{4,0},{8,12},{12,8},{1,5},{5,1},{9,13},{13,9},{2,6},{6,2},{1... | collective-permute-start | bytes 1081352 | tf_op jit(solution)/shard_map/ppermute | solution.py:511
  129.5 18.9 %collective-permute-start.23 = (bf16[128,1408]{1,0:T(8,128)(2,1)S(1)}, bf16[128,1408]{1,0:T(8,128)(2,1)S(1)}, u32[]{:S(2)}, u32[]{:S(2)}) collective-permute-start(bf16[128,1408]{1,0:T(8,128)(2,1)S(1)} %get-tuple-element.200.sums), channel_id=1, source_target_pairs={{4,8},{8,4},{5,9},{9,5},{6,10},{10,6},{7,11},{11,7},{20,24},{24,20... | collective-permute-start | bytes 1081352 | tf_op jit(solution)/shard_map/ppermute | solution.py:512
  144.3 15.5 %collective-permute-start.20 = (bf16[128,2048]{1,0:T(8,128)(2,1)}, bf16[128,2048]{1,0:T(8,128)(2,1)S(1)}, u32[]{:S(2)}, u32[]{:S(2)}) collective-permute-start(bf16[128,2048]{1,0:T(8,128)(2,1)} %get-tuple-element.114.refs_0_.refs_4_), channel_id=1, source_target_pairs={{0,4},{4,0},{8,12},{12,8},{1,5},{5,1},{9,13},{13,9},{2,6},{6,2},{1... | collective-permute-start | bytes 1572872 | tf_op jit(solution)/shard_map/ppermute | solution.py:511
  149.8 18.3 %collective-permute-start.26 = (bf16[128,1408]{1,0:T(8,128)(2,1)S(1)}, bf16[128,1408]{1,0:T(8,128)(2,1)S(1)}, u32[]{:S(2)}, u32[]{:S(2)}) collective-permute-start(bf16[128,1408]{1,0:T(8,128)(2,1)S(1)} %get-tuple-element.199), channel_id=1, source_target_pairs={{0,4},{4,0},{8,12},{12,8},{1,5},{5,1},{9,13},{13,9},{2,6},{6,2},{1... | collective-permute-start | bytes 1081352 | tf_op jit(solution)/shard_map/ppermute | solution.py:511
  152.2 15.9 %collective-permute-start.27 = (bf16[128,1408]{1,0:T(8,128)(2,1)S(1)}, bf16[128,1408]{1,0:T(8,128)(2,1)S(1)}, u32[]{:S(2)}, u32[]{:S(2)}) collective-permute-start(bf16[128,1408]{1,0:T(8,128)(2,1)S(1)} %get-tuple-element.198.sums), channel_id=1, source_target_pairs={{4,8},{8,4},{5,9},{9,5},{6,10},{10,6},{7,11},{11,7},{20,24},{24,20... | collective-permute-start | bytes 1081352 | tf_op jit(solution)/shard_map/ppermute | solution.py:512
  164.0 15.4 %collective-permute-start.24 = (bf16[128,2048]{1,0:T(8,128)(2,1)}, bf16[128,2048]{1,0:T(8,128)(2,1)S(1)}, u32[]{:S(2)}, u32[]{:S(2)}) collective-permute-start(bf16[128,2048]{1,0:T(8,128)(2,1)} %get-tuple-element.123.refs_8_.refs_12_), channel_id=1, source_target_pairs={{0,4},{4,0},{8,12},{12,8},{1,5},{5,1},{9,13},{13,9},{2,6},{6,2},{1... | collective-permute-start | bytes 1572872 | tf_op jit(solution)/shard_map/ppermute | solution.py:511
  169.4 18.3 %collective-permute-start.30 = (bf16[128,1408]{1,0:T(8,128)(2,1)S(1)}, bf16[128,1408]{1,0:T(8,128)(2,1)S(1)}, u32[]{:S(2)}, u32[]{:S(2)}) collective-permute-start(bf16[128,1408]{1,0:T(8,128)(2,1)S(1)} %get-tuple-element.197), channel_id=1, source_target_pairs={{0,4},{4,0},{8,12},{12,8},{1,5},{5,1},{9,13},{13,9},{2,6},{6,2},{1... | collective-permute-start | bytes 1081352 | tf_op jit(solution)/shard_map/ppermute | solution.py:511
  172.1 15.7 %collective-permute-start.31 = (bf16[128,1408]{1,0:T(8,128)(2,1)S(1)}, bf16[128,1408]{1,0:T(8,128)(2,1)S(1)}, u32[]{:S(2)}, u32[]{:S(2)}) collective-permute-start(bf16[128,1408]{1,0:T(8,128)(2,1)S(1)} %get-tuple-element.196.sums), channel_id=1, source_target_pairs={{4,8},{8,4},{5,9},{9,5},{6,10},{10,6},{7,11},{11,7},{20,24},{24,20... | collective-permute-start | bytes 1081352 | tf_op jit(solution)/shard_map/ppermute | solution.py:512
  183.6 14.7 %collective-permute-start.28 = (bf16[128,2048]{1,0:T(8,128)(2,1)}, bf16[128,2048]{1,0:T(8,128)(2,1)S(1)}, u32[]{:S(2)}, u32[]{:S(2)}) collective-permute-start(bf16[128,2048]{1,0:T(8,128)(2,1)} %get-tuple-element.132.refs_16_.refs_20_), channel_id=1, source_target_pairs={{0,4},{4,0},{8,12},{12,8},{1,5},{5,1},{9,13},{13,9},{2,6},{6,2},{1... | collective-permute-start | bytes 1572872 | tf_op jit(solution)/shard_map/ppermute | solution.py:511
  204.8 13.8 %collective-permute-start.32 = (bf16[128,2048]{1,0:T(8,128)(2,1)}, bf16[128,2048]{1,0:T(8,128)(2,1)S(1)}, u32[]{:S(2)}, u32[]{:S(2)}) collective-permute-start(bf16[128,2048]{1,0:T(8,128)(2,1)} %get-tuple-element.141.refs_24_.refs_28_), channel_id=1, source_target_pairs={{0,4},{4,0},{8,12},{12,8},{1,5},{5,1},{9,13},{13,9},{2,6},{6,2},{1... | collective-permute-start | bytes 1572872 | tf_op jit(solution)/shard_map/ppermute | solution.py:511
  225.4 13.8 %collective-permute-start.36 = (bf16[128,2048]{1,0:T(8,128)(2,1)}, bf16[128,2048]{1,0:T(8,128)(2,1)S(1)}, u32[]{:S(2)}, u32[]{:S(2)}) collective-permute-start(bf16[128,2048]{1,0:T(8,128)(2,1)} %get-tuple-element.150.refs_0_.refs_4_), channel_id=1, source_target_pairs={{0,4},{4,0},{8,12},{12,8},{1,5},{5,1},{9,13},{13,9},{2,6},{6,2},{1... | collective-permute-start | bytes 1572872 | tf_op jit(solution)/shard_map/ppermute | solution.py:511
  231.0 14.8 %collective-permute-start.42 = (bf16[128,1408]{1,0:T(8,128)(2,1)S(1)}, bf16[128,1408]{1,0:T(8,128)(2,1)S(1)}, u32[]{:S(2)}, u32[]{:S(2)}) collective-permute-start(bf16[128,1408]{1,0:T(8,128)(2,1)S(1)} %fusion.9), channel_id=1, source_target_pairs={{0,4},{4,0},{8,12},{12,8},{1,5},{5,1},{9,13},{13,9},{2,6},{6,2},{1... | collective-permute-start | bytes 1081352 | tf_op jit(solution)/shard_map/ppermute | solution.py:511
  289.2 25.1 %collective-permute-start.47 = (bf16[256,1152]{1,0:T(8,128)(2,1)}, bf16[256,1152]{1,0:T(8,128)(2,1)S(1)}, u32[]{:S(2)}, u32[]{:S(2)}) collective-permute-start(bf16[256,1152]{1,0:T(8,128)(2,1)} %constant_dynamic-slice_fusion.2), channel_id=1, source_target_pairs={{0,1},{1,0},{2,3},{3,2},{4,5},{5,4},{6,7},{7,6},{8,9},{9,8},{10,11... | collective-permute-start | bytes 1769480 | tf_op jit(solution)/shard_map/ppermute | solution.py:598
  303.6 14.5 %collective-permute-start.53 = (bf16[1024,128]{0,1:T(8,128)(2,1)}, bf16[1024,128]{0,1:T(8,128)(2,1)}, u32[]{:S(2)}, u32[]{:S(2)}) collective-permute-start(bf16[1024,128]{0,1:T(8,128)(2,1)} %get-tuple-element.229), channel_id=1, source_target_pairs={{0,4},{12,8},{1,5},{13,9},{2,6},{14,10},{3,7},{15,11},{16,20},{28,... | collective-permute-start | bytes 786440 | tf_op jit(solution)/shard_map/ppermute | solution.py:592
  310.7 16.0 %collective-permute-start.55 = (bf16[1024,128]{0,1:T(8,128)(2,1)}, bf16[1024,128]{0,1:T(8,128)(2,1)}, u32[]{:S(2)}, u32[]{:S(2)}) collective-permute-start(bf16[1024,128]{0,1:T(8,128)(2,1)} %get-tuple-element.226), channel_id=1, source_target_pairs={{0,12},{12,0},{1,13},{13,1},{2,14},{14,2},{3,15},{15,3},{16,28},{2... | collective-permute-start | bytes 786440 | tf_op jit(solution)/shard_map/ppermute | solution.py:592
  316.6 15.6 %collective-permute-start.52 = (bf16[256,1152]{1,0:T(8,128)(2,1)}, bf16[256,1152]{1,0:T(8,128)(2,1)}, u32[]{:S(2)}, u32[]{:S(2)}) collective-permute-start(bf16[256,1152]{1,0:T(8,128)(2,1)} %get-tuple-element.188), channel_id=1, source_target_pairs={{0,2},{1,3},{2,0},{3,1},{4,6},{5,7},{6,4},{7,5},{8,10},{9,11},{10,... | collective-permute-start | bytes 1769480 | tf_op jit(solution)/shard_map/ppermute | solution.py:605
  (77 other events, 718.3 us)

commit v6 on v5

--- a/solution.py
+++ b/solution.py
@@ -290,9 +290,12 @@
     )(gates, *others)
 
 
-def output_kernel(where, *refs, n, count):
+def output_kernel(where, *refs, n, count, paired):
     blocks = refs[: 2 * n * count]
-    gain, weight_source, out, held, weight, sems, weight_sems = refs[2 * n * count :]
+    gain, weight_source, *refs = refs[2 * n * count :]
+    prior, (out, *handed), (held, weight, sems, weight_sems) = (
+        (refs[0], refs[1:3], refs[3:]) if paired else (None, refs[:1], refs[1:])
+    )
     ch = held.shape[1] // 2
     width = weight.shape[1]
     here = where[0]
@@ -324,31 +327,53 @@
             weight_source.at[:, columns], weight.at[:, columns], weight_sems.at[k]
         ).start()
     fetch(lambda copy: copy.wait())
-    values = held[...].astype(f32)
-    squares = jnp.sum(values * values, axis=1, keepdims=True)
-    held[...] = (values * gain[...]).astype(bf16)
+
+    def put(columns, result):
+        if paired:
+            mine = where[1] == 0
+            before = prior[:, columns].astype(f32)
+            out[:, columns] = jnp.where(mine, before, result).astype(bf16)
+            handed[0][:, columns] = jnp.where(mine, result, before).astype(bf16)
+        else:
+            out[:, columns] = result.astype(bf16)
+
+    sums = []
+    for block in range(count):
+        part = slice(block * BLOCK, (block + 1) * BLOCK)
+
+        def some_channels(at, total):
+            lanes = pl.ds(pl.multiple_of(at * LANES, LANES), LANES)
+            values = held[part, lanes].astype(f32)
+            held[part, lanes] = (values * gain[:, lanes]).astype(bf16)
+            return total + values * values
+
+        total = lax.fori_loop(
+            0, 2 * ch // LANES, some_channels, jnp.zeros((BLOCK, LANES), f32), unroll=2
+        )
+        sums.append(jnp.sum(total, axis=1, keepdims=True))
+    squares = jnp.concatenate(sums, axis=0)
 
     def some_columns(at, carry):
         part = pl.ds(pl.multiple_of(at * tile, tile), tile)
         pltpu.make_async_copy(
             weight_source.at[:, part], weight.at[:, part], weight_sems.at[at]
         ).wait()
-        out[:, part] = jnp.dot(
-            held[...], weight[:, part], preferred_element_type=f32
-        ).astype(bf16)
+        put(part, jnp.dot(held[...], weight[:, part], preferred_element_type=f32))
         return carry
 
     lax.fori_loop(0, tiles, some_columns, 0)
-    out[:, width:] = jnp.broadcast_to(squares, (count * BLOCK, LANES)).astype(bf16)
-
-
-def output_block(where, blocks, n, gain, weight, ch):
+    put(slice(width, width + LANES), jnp.broadcast_to(squares, (count * BLOCK, LANES)))
+
+
+def output_block(where, blocks, n, gain, weight, ch, prior=None):
     count = len(blocks) // (2 * n)
     width = weight.shape[1]
     whole = lambda a: pl.BlockSpec(a.shape, lambda b, w: (0, 0))
+    result = jax.ShapeDtypeStruct((count * BLOCK, width + LANES), bf16)
+    extra = () if prior is None else (prior,)
     return pl.pallas_call(
-        functools.partial(output_kernel, n=n, count=count),
-        out_shape=jax.ShapeDtypeStruct((count * BLOCK, width + LANES), bf16),
+        functools.partial(output_kernel, n=n, count=count, paired=prior is not None),
+        out_shape=result if prior is None else (result, result),
         grid_spec=pltpu.PrefetchScalarGridSpec(
             num_scalar_prefetch=1,
             grid=(1,),
@@ -356,8 +381,9 @@
                 *(pl.BlockSpec(memory_space=pl.ANY) for _ in blocks),
                 whole(gain),
                 pl.BlockSpec(memory_space=pl.ANY),
+                *map(whole, extra),
             ],
-            out_specs=pl.BlockSpec((count * BLOCK, width + LANES), lambda b, w: (0, 0)),
+            out_specs=whole(result) if prior is None else [whole(result)] * 2,
             scratch_shapes=[
                 pltpu.VMEM((count * BLOCK, 2 * ch), bf16),
                 pltpu.VMEM(weight.shape, bf16),
@@ -369,7 +395,7 @@
             flops=4 * count * BLOCK * ch * width, bytes_accessed=4 * ch * width + 8 * count * BLOCK * ch, transcendentals=0
         ),
         name="output_block",
-    )(where, *blocks, gain, weight)
+    )(where, *blocks, gain, weight, *extra)
 
 
 def per_device(
@@ -521,6 +547,7 @@
     per = size // BLOCK
     chips = shards // 2
     chip = shard // 2
+    spot = jnp.stack([as_int(here), as_int(core)])
     groups = [2, 1, 1] if chips == 2 else [1] * shards
     group_ends = [sum(groups[: k + 1]) for k in range(len(groups))]
     sums = came = before = gated = None
@@ -582,8 +609,11 @@
                     needed.append(went[b])
                     needed.extend(arrived[b + n - 1 + k][1 - k % 2] for k in range(1, n))
             pending = len(outs)
+            prior = outs[-1] if chips == 2 and pending == len(groups) - 1 else None
             outs.append(
-                output_block(as_int(here)[None], needed, n, gain, output_projection_weight, ch)
+                output_block(
+                    spot, needed, n, gain, output_projection_weight, ch, prior
+                )
             )
 
     landed = [jnp.where(at_first, states[0], states[n - 1])]
@@ -592,14 +622,13 @@
         landed.append(lax.ppermute(leaving, "seq", [(0, k), (n - 1, n - 1 - k)]))
 
     if chips == 2:
-        first, *rest = outs
+        first, _, (keep_last, give_last) = outs
         keep = own(first, core * size, size, 0)
         give = own(first, (1 - core) * size, size, 0)
         back = lax.ppermute(give, "tensor", swap)
         both_first = added(keep, back)
-        give = jnp.where(core == 0, *rest[::-1])
-        back = lax.ppermute(give, "tensor", swap)
-        both_last = added(jnp.where(core == 0, *rest), back)
+        back = lax.ppermute(give_last, "tensor", swap)
+        both_last = added(keep_last, back)
         total = jnp.where(chip == 0, both_first, both_last).astype(f32)
         both = give = jnp.where(chip == 0, both_last, both_first)
         came = lax.ppermute(give, "tensor", [(j, j ^ 2) for j in range(shards)])

time: 337 us -> 341 us (1.012)
  Pallas kernels: 102 us -> 106 us
    pallas_call x3, Pallas kernels: 20.5 us -> 24.8 us  [output_block(): pl.pallas_call(functools.partial(output_kernel, n=n, count=count, paired=...]
    unnamed x100 -> x98, local copies, waits for them, and re-layouts: 8.09 us -> 8.06 us
  transfers between devices with their start and end apart: 56 -> 56, of which waited for: 15 -> 15; matrix products, arithmetic and copies ran while one was open for 17% -> 17% of each run, Pallas kernels for 22% -> 23%
where the time goes in v6:
time: 341 us; the launch traced here: 338 us
  Pallas kernels  106 us (31%)
  starting transfers between devices  104 us (30%)
  waiting for transfers between devices  49.6 us (15%)
  other arithmetic  41.2 us (12%)
  local copies, waits for them, and re-layouts  35.3 us (10%)
    ppermute x24, starting transfers between devices, onward(): from_a = lax.ppermute(pair[0], 'seq', pairs_a)  70.7 us
    ppermute x24, waiting for transfers between devices, onward(): from_a = lax.ppermute(pair[0], 'seq', pairs_a)  39.5 us
    pallas_call x8, Pallas kernels, scan_block(): pl.pallas_call(scan_kernel, out_shape=outs, grid=(1,), in_specs=[pl.Block...  39 us
    pallas_call x3, Pallas kernels, output_block(): pl.pallas_call(functools.partial(output_kernel, n=n, count=count, paired=...  24.8 us
    pallas_call x1, Pallas kernels, project(): pl.pallas_call(functools.partial(project_kernel, rows=rows, first=first,...  23.4 us
    pallas_call x6, Pallas kernels, merge(): pl.pallas_call(functools.partial(merge_kernel, passing=passing), out_shap...  19.1 us
    convert_element_type x14, other arithmetic, added(): return (a.astype(f32) + b.astype(f32)).astype(bf16)  18.8 us
    ppermute x22, starting transfers between devices, onward(): from_b = lax.ppermute(pair[1], 'seq', pairs_b)  15.2 us
  transfers between devices with their start and end apart: 56, of which 15 were waited for; matrix products, arithmetic and copies ran while one was open for 17% of the time, Pallas kernels for 23%

profile of v6, /device:TPU:0, one launch (start us, length us, event | category | flops | bytes accessed | tf_op | source)
XLA Modules:
  0.0 338.5 jit_solution(13711383591172234181)
XLA Ops:
  13.7 11.5 %copy.48 = bf16[64,16,2,2048]{3,1,2,0:T(8,128)(2,1)} copy(bf16[64,16,2,2048]{3,2,1,0:T(2,128)(2,1)} %bitcast.181) | data formatting | bytes 16777216 | tf_op jit(solution)/shard_map/reshape | solution.py:462
  33.2 23.4 %project.1 = (bf16[2,1024,1408]{2,1,0:T(8,128)(2,1)}, bf16[2,1024,1024]{2,1,0:T(8,128)(2,1)}) custom-call(s32[6]{0:T(128)} %stack.138.where, bf16[4,272,512]{2,1,0:T(8,128)(2,1)} %copy-done.29, bf16[4,272,512]{2,1,0:T(8,128)(2,1)} %collective-permute-done.3.refs_1_, bf16[1024,256]{1,0:T(8,128)(2,1)} %refs_2_.1, bf16[64,2,16,2048]{3,2,1,0:T(8,128)(2,1)} %bitcast.182, ...), custom_call_target="tpu_custom_call" | custom-call | flops 12750684160 | bytes 18350080 | tf_op jit(solution)/shard_map/project/pallas_call | solution.py:119
  57.8 5.1 %collective-permute-start.6 = (bf16[128,1408]{1,0:T(8,128)(2,1)S(1)}, bf16[128,1408]{1,0:T(8,128)(2,1)S(1)}, u32[]{:S(2)}, u32[]{:S(2)}) collective-permute-start(bf16[128,1408]{1,0:T(8,128)(2,1)S(1)} %get-tuple-element.211), channel_id=1, source_target_pairs={{0,4},{4,0},{8,12},{12,8},{1,5},{5,1},{9,13},{13,9},{2,6},{6,2},{1... | collective-permute-start | bytes 1081352 | tf_op jit(solution)/shard_map/ppermute | solution.py:537
  64.5 7.1 %collective-permute-done.6 = bf16[128,1408]{1,0:T(8,128)(2,1)S(1)} collective-permute-done((bf16[128,1408]{1,0:T(8,128)(2,1)S(1)}, bf16[128,1408]{1,0:T(8,128)(2,1)S(1)}, u32[]{:S(2)}, u32[]{:S(2)}) %collective-permute-start.6) | collective-permute-done | bytes 360480 | tf_op jit(solution)/shard_map/ppermute | solution.py:537
  72.9 3.8 %collective-permute-start.10 = (bf16[128,1408]{1,0:T(8,128)(2,1)S(1)}, bf16[128,1408]{1,0:T(8,128)(2,1)S(1)}, u32[]{:S(2)}, u32[]{:S(2)}) collective-permute-start(bf16[128,1408]{1,0:T(8,128)(2,1)S(1)} %get-tuple-element.209), channel_id=1, source_target_pairs={{0,4},{4,0},{8,12},{12,8},{1,5},{5,1},{9,13},{13,9},{2,6},{6,2},{1... | collective-permute-start | bytes 1081352 | tf_op jit(solution)/shard_map/ppermute | solution.py:537
  83.7 6.4 %collective-permute-done.4 = bf16[128,1024]{1,0:T(8,128)(2,1)S(1)} collective-permute-done((bf16[128,1024]{1,0:T(8,128)(2,1)S(1)}, bf16[128,1024]{1,0:T(8,128)(2,1)S(1)}, u32[]{:S(2)}, u32[]{:S(2)}) %collective-permute-start.4) | collective-permute-done | bytes 262176 | tf_op jit(solution)/shard_map/ppermute | solution.py:537
  91.5 3.7 %collective-permute-start.14 = (bf16[128,1408]{1,0:T(8,128)(2,1)S(1)}, bf16[128,1408]{1,0:T(8,128)(2,1)S(1)}, u32[]{:S(2)}, u32[]{:S(2)}) collective-permute-start(bf16[128,1408]{1,0:T(8,128)(2,1)S(1)} %get-tuple-element.207), channel_id=1, source_target_pairs={{0,4},{4,0},{8,12},{12,8},{1,5},{5,1},{9,13},{13,9},{2,6},{6,2},{1... | collective-permute-start | bytes 1081352 | tf_op jit(solution)/shard_map/ppermute | solution.py:537
  101.7 6.1 %collective-permute-done.8 = bf16[128,1024]{1,0:T(8,128)(2,1)S(1)} collective-permute-done((bf16[128,1024]{1,0:T(8,128)(2,1)S(1)}, bf16[128,1024]{1,0:T(8,128)(2,1)S(1)}, u32[]{:S(2)}, u32[]{:S(2)}) %collective-permute-start.8) | collective-permute-done | bytes 262176 | tf_op jit(solution)/shard_map/ppermute | solution.py:537
  109.1 3.7 %collective-permute-start.18 = (bf16[128,1408]{1,0:T(8,128)(2,1)S(1)}, bf16[128,1408]{1,0:T(8,128)(2,1)S(1)}, u32[]{:S(2)}, u32[]{:S(2)}) collective-permute-start(bf16[128,1408]{1,0:T(8,128)(2,1)S(1)} %get-tuple-element.205), channel_id=1, source_target_pairs={{0,4},{4,0},{8,12},{12,8},{1,5},{5,1},{9,13},{13,9},{2,6},{6,2},{1... | collective-permute-start | bytes 1081352 | tf_op jit(solution)/shard_map/ppermute | solution.py:537
  125.8 3.7 %collective-permute-start.22 = (bf16[128,1408]{1,0:T(8,128)(2,1)S(1)}, bf16[128,1408]{1,0:T(8,128)(2,1)S(1)}, u32[]{:S(2)}, u32[]{:S(2)}) collective-permute-start(bf16[128,1408]{1,0:T(8,128)(2,1)S(1)} %get-tuple-element.203), channel_id=1, source_target_pairs={{0,4},{4,0},{8,12},{12,8},{1,5},{5,1},{9,13},{13,9},{2,6},{6,2},{1... | collective-permute-start | bytes 1081352 | tf_op jit(solution)/shard_map/ppermute | solution.py:537
  135.0 4.8 %scan_block.8 = (bf16[128,1024]{1,0:T(8,128)(2,1)}, f32[128,1024]{1,0:T(8,128)}, f32[8,1280]{1,0:T(8,128)}) custom-call(bf16[128,1024]{1,0:T(8,128)(2,1)} %copy-done.30, bf16[128,1408]{1,0:T(8,128)(2,1)} %copy-done.23, f32[8,1280]{1,0:T(8,128)} %fusion.40.tail, f32[128,1024]{1,0:T(8,128)} %bitcast.187, f32[1,128]{1,0:T(1,128)} %get-tuple-element.245.index, ...), custom_call_target="tpu_custom_call" | custom-call | flops 134217728 | bytes 2097152 | tf_op jit(solution)/shard_map/scan_block/pallas_call | solution.py:273
  153.5 4.9 %scan_block.9 = (bf16[128,1024]{1,0:T(8,128)(2,1)}, f32[128,1024]{1,0:T(8,128)}, f32[8,1280]{1,0:T(8,128)}) custom-call(bf16[128,2048]{1,0:T(8,128)(2,1)} %get-tuple-element.117.gates, bf16[128,1408]{1,0:T(8,128)(2,1)} %copy-done.24, f32[8,1280]{1,0:T(8,128)} %get-tuple-element.122.tail, f32[128,1024]{1,0:T(8,128)} %get-tuple-element.123.state, ...), custom_call_target="tpu_custom_call" | custom-call | flops 134217728 | bytes 2097152 | tf_op jit(solution)/shard_map/scan_block/pallas_call | solution.py:273
  172.8 4.9 %scan_block.10 = (bf16[128,1024]{1,0:T(8,128)(2,1)}, f32[128,1024]{1,0:T(8,128)}, f32[8,1280]{1,0:T(8,128)}) custom-call(bf16[128,2048]{1,0:T(8,128)(2,1)} %get-tuple-element.126.gates, bf16[128,1408]{1,0:T(8,128)(2,1)} %copy-done.25, f32[8,1280]{1,0:T(8,128)} %get-tuple-element.131.tail, f32[128,1024]{1,0:T(8,128)} %get-tuple-element.132.state, ...), custom_call_target="tpu_custom_call" | custom-call | flops 134217728 | bytes 2097152 | tf_op jit(solution)/shard_map/scan_block/pallas_call | solution.py:273
  193.5 4.9 %scan_block.11 = (bf16[128,1024]{1,0:T(8,128)(2,1)}, f32[128,1024]{1,0:T(8,128)}, f32[8,1280]{1,0:T(8,128)}) custom-call(bf16[128,2048]{1,0:T(8,128)(2,1)} %get-tuple-element.135.gates, bf16[128,1408]{1,0:T(8,128)(2,1)} %copy-done.26, f32[8,1280]{1,0:T(8,128)} %get-tuple-element.140.tail, f32[128,1024]{1,0:T(8,128)} %get-tuple-element.141.state, ...), custom_call_target="tpu_custom_call" | custom-call | flops 134217728 | bytes 2097152 | tf_op jit(solution)/shard_map/scan_block/pallas_call | solution.py:273
  213.8 4.9 %scan_block.12 = (bf16[128,1024]{1,0:T(8,128)(2,1)}, f32[128,1024]{1,0:T(8,128)}, f32[8,1280]{1,0:T(8,128)}) custom-call(bf16[128,2048]{1,0:T(8,128)(2,1)} %get-tuple-element.144.gates, bf16[128,1408]{1,0:T(8,128)(2,1)} %copy-done.27, f32[8,1280]{1,0:T(8,128)} %get-tuple-element.149.tail, f32[128,1024]{1,0:T(8,128)} %get-tuple-element.150.state, ...), custom_call_target="tpu_custom_call" | custom-call | flops 134217728 | bytes 2097152 | tf_op jit(solution)/shard_map/scan_block/pallas_call | solution.py:273
  234.2 4.9 %scan_block.13 = (bf16[128,1024]{1,0:T(8,128)(2,1)}, f32[128,1024]{1,0:T(8,128)}, f32[8,1280]{1,0:T(8,128)}) custom-call(bf16[128,2048]{1,0:T(8,128)(2,1)} %get-tuple-element.153.gates, bf16[128,1408]{1,0:T(8,128)(2,1)} %copy-done.28, f32[8,1280]{1,0:T(8,128)} %get-tuple-element.158.tail, f32[128,1024]{1,0:T(8,128)} %get-tuple-element.159.state, ...), custom_call_target="tpu_custom_call" | custom-call | flops 134217728 | bytes 2097152 | tf_op jit(solution)/shard_map/scan_block/pallas_call | solution.py:273
  248.0 4.9 %scan_block.14 = (bf16[128,1024]{1,0:T(8,128)(2,1)}, f32[128,1024]{1,0:T(8,128)}, f32[8,1280]{1,0:T(8,128)}) custom-call(bf16[128,2048]{1,0:T(8,128)(2,1)} %get-tuple-element.162.gates, bf16[128,1408]{1,0:T(8,128)(2,1)} %get-tuple-element.193.sums, f32[8,1280]{1,0:T(8,128)} %get-tuple-element.165.tail, f32[128,1024]{1,0:T(8,128)} %get-tuple-element.166.state, ...), custom_call_target="tpu_custom_call" | custom-call | flops 134217728 | bytes 2097152 | tf_op jit(solution)/shard_map/scan_block/pallas_call | solution.py:273
  260.3 4.9 %scan_block.15 = (bf16[128,1024]{1,0:T(8,128)(2,1)}, f32[128,1024]{1,0:T(8,128)}, f32[8,1280]{1,0:T(8,128)}) custom-call(bf16[128,1024]{1,0:T(8,128)(2,1)} %fusion.32.gates, bf16[128,1408]{1,0:T(8,128)(2,1)} %get-tuple-element.192.sums, f32[8,1280]{1,0:T(8,128)} %get-tuple-element.167.tail, f32[128,1024]{1,0:T(8,128)} %get-tuple-element.168.state, ...), custom_call_target="tpu_custom_call" | custom-call | flops 134217728 | bytes 2097152 | tf_op jit(solution)/shard_map/scan_block/pallas_call | solution.py:273
  269.3 9.4 %output_block.3 = bf16[512,1152]{1,0:T(8,128)(2,1)} custom-call(s32[2]{0:T(128)} %pad_add_fusion.6.where, bf16[128,2048]{1,0:T(8,128)(2,1)} %get-tuple-element.116.refs_0_.refs_4_, bf16[128,2048]{1,0:T(8,128)(2,1)} %copy-done.7, bf16[128,2048]{1,0:T(8,128)(2,1)} %copy-done.9, bf16[128,2048]{1,0:T(8,128)(2,1)} %copy-done.2, ...), custom_call_target="tpu_custom_call" | custom-call | flops 2147483648 | bytes 8388608 | tf_op jit(solution)/shard_map/output_block/pallas_call | solution.py:374
  281.8 7.4 %output_block.4.refs_18_ = bf16[256,1152]{1,0:T(8,128)(2,1)} custom-call(s32[2]{0:T(128)} %pad_add_fusion.6.where, bf16[128,2048]{1,0:T(8,128)(2,1)} %get-tuple-element.152.refs_0_.refs_4_, bf16[128,2048]{1,0:T(8,128)(2,1)} %copy-done.4, bf16[128,2048]{1,0:T(8,128)(2,1)} %copy-done.15, bf16[128,1024]{1,0:T(8,128)(2,1)} %copy-done.13, ...), custom_call_target="tpu_custom_call" | custom-call | flops 1073741824 | bytes 6291456 | tf_op jit(solution)/shard_map/output_block/pallas_call | solution.py:374
  291.8 3.9 %collective-permute-done.50.refs_11_.refs_15_ = bf16[128,1024]{1,0:T(8,128)(2,1)S(1)} collective-permute-done((bf16[128,1024]{1,0:T(8,128)(2,1)S(1)}, bf16[128,1024]{1,0:T(8,128)(2,1)S(1)}, u32[]{:S(2)}, u32[]{:S(2)}) %collective-permute-start.50) | collective-permute-done | bytes 262176 | tf_op jit(solution)/shard_map/ppermute | solution.py:537
  296.4 8.0 %output_block.5 = (bf16[256,1152]{1,0:T(8,128)(2,1)}, bf16[256,1152]{1,0:T(8,128)(2,1)}) custom-call(s32[2]{0:T(128)} %pad_add_fusion.6.where, bf16[128,1024]{1,0:T(8,128)(2,1)} %copy-done.20, bf16[128,1024]{1,0:T(8,128)(2,1)} %copy-done.13, bf16[128,1024]{1,0:T(8,128)(2,1)} %copy-done.31, bf16[128,1024]{1,0:T(8,128)(2,1)} %copy-done.32, ...), custom_call_target="tpu_custom_call" | custom-call | flops 1073741824 | bytes 6291456 | tf_op jit(solution)/shard_map/output_block/pallas_call | solution.py:374
  306.6 4.2 %collective-permute-start.53 = (bf16[1024,128]{0,1:T(8,128)(2,1)}, bf16[1024,128]{0,1:T(8,128)(2,1)}, u32[]{:S(2)}, u32[]{:S(2)}) collective-permute-start(bf16[1024,128]{0,1:T(8,128)(2,1)} %get-tuple-element.231), channel_id=1, source_target_pairs={{0,4},{12,8},{1,5},{13,9},{2,6},{14,10},{3,7},{15,11},{16,20},{28,... | collective-permute-start | bytes 786440 | tf_op jit(solution)/shard_map/ppermute | solution.py:622
  322.8 6.3 %collective-permute-done.55 = bf16[1024,128]{0,1:T(8,128)(2,1)} collective-permute-done((bf16[1024,128]{0,1:T(8,128)(2,1)}, bf16[1024,128]{0,1:T(8,128)(2,1)}, u32[]{:S(2)}, u32[]{:S(2)}) %collective-permute-start.55) | collective-permute-done | bytes 262176 | tf_op jit(solution)/shard_map/ppermute | solution.py:622
  (269 shorter events, 183.9 us)
Async XLA Ops:
  3.6 25.4 %collective-permute-start = (bf16[272,512]{1,0:T(8,128)(2,1)}, bf16[272,512]{1,0:T(8,128)(2,1)}, u32[]{:S(2)}, u32[]{:S(2)}) collective-permute-start(bf16[272,512]{1,0:T(8,128)(2,1)} %get-tuple-element.235), channel_id=1, source_target_pairs={{0,4},{4,8},{8,12},{12,0},{1,5},{5,9},{9,13},{13,1},{2,6},{6,10},{... | collective-permute-start | bytes 835592 | tf_op jit(solution)/shard_map/ppermute | solution.py:459
  6.7 22.3 %collective-permute-start.1 = (bf16[272,512]{1,0:T(8,128)(2,1)S(1)}, bf16[272,512]{1,0:T(8,128)(2,1)}, u32[]{:S(2)}, u32[]{:S(2)}) collective-permute-start(bf16[272,512]{1,0:T(8,128)(2,1)S(1)} %get-tuple-element.236), channel_id=1, source_target_pairs={{0,8},{4,12},{8,0},{12,4},{1,9},{5,13},{9,1},{13,5},{2,10},{6,14},... | collective-permute-start | bytes 835592 | tf_op jit(solution)/shard_map/ppermute | solution.py:459
  9.3 19.7 %collective-permute-start.2 = (bf16[272,512]{1,0:T(8,128)(2,1)S(1)}, bf16[272,512]{1,0:T(8,128)(2,1)}, u32[]{:S(2)}, u32[]{:S(2)}) collective-permute-start(bf16[272,512]{1,0:T(8,128)(2,1)S(1)} %get-tuple-element.237), channel_id=1, source_target_pairs={{0,12},{4,0},{8,4},{12,8},{1,13},{5,1},{9,5},{13,9},{2,14},{6,2},{... | collective-permute-start | bytes 835592 | tf_op jit(solution)/shard_map/ppermute | solution.py:459
  57.8 13.8 %collective-permute-start.6 = (bf16[128,1408]{1,0:T(8,128)(2,1)S(1)}, bf16[128,1408]{1,0:T(8,128)(2,1)S(1)}, u32[]{:S(2)}, u32[]{:S(2)}) collective-permute-start(bf16[128,1408]{1,0:T(8,128)(2,1)S(1)} %get-tuple-element.211), channel_id=1, source_target_pairs={{0,4},{4,0},{8,12},{12,8},{1,5},{5,1},{9,13},{13,9},{2,6},{6,2},{1... | collective-permute-start | bytes 1081352 | tf_op jit(solution)/shard_map/ppermute | solution.py:537
  72.9 17.3 %collective-permute-start.10 = (bf16[128,1408]{1,0:T(8,128)(2,1)S(1)}, bf16[128,1408]{1,0:T(8,128)(2,1)S(1)}, u32[]{:S(2)}, u32[]{:S(2)}) collective-permute-start(bf16[128,1408]{1,0:T(8,128)(2,1)S(1)} %get-tuple-element.209), channel_id=1, source_target_pairs={{0,4},{4,0},{8,12},{12,8},{1,5},{5,1},{9,13},{13,9},{2,6},{6,2},{1... | collective-permute-start | bytes 1081352 | tf_op jit(solution)/shard_map/ppermute | solution.py:537
  91.5 16.3 %collective-permute-start.14 = (bf16[128,1408]{1,0:T(8,128)(2,1)S(1)}, bf16[128,1408]{1,0:T(8,128)(2,1)S(1)}, u32[]{:S(2)}, u32[]{:S(2)}) collective-permute-start(bf16[128,1408]{1,0:T(8,128)(2,1)S(1)} %get-tuple-element.207), channel_id=1, source_target_pairs={{0,4},{4,0},{8,12},{12,8},{1,5},{5,1},{9,13},{13,9},{2,6},{6,2},{1... | collective-permute-start | bytes 1081352 | tf_op jit(solution)/shard_map/ppermute | solution.py:537
  109.1 15.5 %collective-permute-start.18 = (bf16[128,1408]{1,0:T(8,128)(2,1)S(1)}, bf16[128,1408]{1,0:T(8,128)(2,1)S(1)}, u32[]{:S(2)}, u32[]{:S(2)}) collective-permute-start(bf16[128,1408]{1,0:T(8,128)(2,1)S(1)} %get-tuple-element.205), channel_id=1, source_target_pairs={{0,4},{4,0},{8,12},{12,8},{1,5},{5,1},{9,13},{13,9},{2,6},{6,2},{1... | collective-permute-start | bytes 1081352 | tf_op jit(solution)/shard_map/ppermute | solution.py:537
  125.8 22.6 %collective-permute-start.22 = (bf16[128,1408]{1,0:T(8,128)(2,1)S(1)}, bf16[128,1408]{1,0:T(8,128)(2,1)S(1)}, u32[]{:S(2)}, u32[]{:S(2)}) collective-permute-start(bf16[128,1408]{1,0:T(8,128)(2,1)S(1)} %get-tuple-element.203), channel_id=1, source_target_pairs={{0,4},{4,0},{8,12},{12,8},{1,5},{5,1},{9,13},{13,9},{2,6},{6,2},{1... | collective-permute-start | bytes 1081352 | tf_op jit(solution)/shard_map/ppermute | solution.py:537
  129.5 18.9 %collective-permute-start.23 = (bf16[128,1408]{1,0:T(8,128)(2,1)S(1)}, bf16[128,1408]{1,0:T(8,128)(2,1)S(1)}, u32[]{:S(2)}, u32[]{:S(2)}) collective-permute-start(bf16[128,1408]{1,0:T(8,128)(2,1)S(1)} %get-tuple-element.202.sums), channel_id=1, source_target_pairs={{4,8},{8,4},{5,9},{9,5},{6,10},{10,6},{7,11},{11,7},{20,24},{24,20... | collective-permute-start | bytes 1081352 | tf_op jit(solution)/shard_map/ppermute | solution.py:538
  144.2 15.6 %collective-permute-start.20 = (bf16[128,2048]{1,0:T(8,128)(2,1)}, bf16[128,2048]{1,0:T(8,128)(2,1)S(1)}, u32[]{:S(2)}, u32[]{:S(2)}) collective-permute-start(bf16[128,2048]{1,0:T(8,128)(2,1)} %get-tuple-element.116.refs_0_.refs_4_), channel_id=1, source_target_pairs={{0,4},{4,0},{8,12},{12,8},{1,5},{5,1},{9,13},{13,9},{2,6},{6,2},{1... | collective-permute-start | bytes 1572872 | tf_op jit(solution)/shard_map/ppermute | solution.py:537
  149.8 18.4 %collective-permute-start.26 = (bf16[128,1408]{1,0:T(8,128)(2,1)S(1)}, bf16[128,1408]{1,0:T(8,128)(2,1)S(1)}, u32[]{:S(2)}, u32[]{:S(2)}) collective-permute-start(bf16[128,1408]{1,0:T(8,128)(2,1)S(1)} %get-tuple-element.201), channel_id=1, source_target_pairs={{0,4},{4,0},{8,12},{12,8},{1,5},{5,1},{9,13},{13,9},{2,6},{6,2},{1... | collective-permute-start | bytes 1081352 | tf_op jit(solution)/shard_map/ppermute | solution.py:537
  152.2 16.0 %collective-permute-start.27 = (bf16[128,1408]{1,0:T(8,128)(2,1)S(1)}, bf16[128,1408]{1,0:T(8,128)(2,1)S(1)}, u32[]{:S(2)}, u32[]{:S(2)}) collective-permute-start(bf16[128,1408]{1,0:T(8,128)(2,1)S(1)} %get-tuple-element.200.sums), channel_id=1, source_target_pairs={{4,8},{8,4},{5,9},{9,5},{6,10},{10,6},{7,11},{11,7},{20,24},{24,20... | collective-permute-start | bytes 1081352 | tf_op jit(solution)/shard_map/ppermute | solution.py:538
  164.0 15.4 %collective-permute-start.24 = (bf16[128,2048]{1,0:T(8,128)(2,1)}, bf16[128,2048]{1,0:T(8,128)(2,1)S(1)}, u32[]{:S(2)}, u32[]{:S(2)}) collective-permute-start(bf16[128,2048]{1,0:T(8,128)(2,1)} %get-tuple-element.125.refs_8_.refs_12_), channel_id=1, source_target_pairs={{0,4},{4,0},{8,12},{12,8},{1,5},{5,1},{9,13},{13,9},{2,6},{6,2},{1... | collective-permute-start | bytes 1572872 | tf_op jit(solution)/shard_map/ppermute | solution.py:537
  169.4 18.3 %collective-permute-start.30 = (bf16[128,1408]{1,0:T(8,128)(2,1)S(1)}, bf16[128,1408]{1,0:T(8,128)(2,1)S(1)}, u32[]{:S(2)}, u32[]{:S(2)}) collective-permute-start(bf16[128,1408]{1,0:T(8,128)(2,1)S(1)} %get-tuple-element.199), channel_id=1, source_target_pairs={{0,4},{4,0},{8,12},{12,8},{1,5},{5,1},{9,13},{13,9},{2,6},{6,2},{1... | collective-permute-start | bytes 1081352 | tf_op jit(solution)/shard_map/ppermute | solution.py:537
  172.1 15.7 %collective-permute-start.31 = (bf16[128,1408]{1,0:T(8,128)(2,1)S(1)}, bf16[128,1408]{1,0:T(8,128)(2,1)S(1)}, u32[]{:S(2)}, u32[]{:S(2)}) collective-permute-start(bf16[128,1408]{1,0:T(8,128)(2,1)S(1)} %get-tuple-element.198.sums), channel_id=1, source_target_pairs={{4,8},{8,4},{5,9},{9,5},{6,10},{10,6},{7,11},{11,7},{20,24},{24,20... | collective-permute-start | bytes 1081352 | tf_op jit(solution)/shard_map/ppermute | solution.py:538
  183.6 14.8 %collective-permute-start.28 = (bf16[128,2048]{1,0:T(8,128)(2,1)}, bf16[128,2048]{1,0:T(8,128)(2,1)S(1)}, u32[]{:S(2)}, u32[]{:S(2)}) collective-permute-start(bf16[128,2048]{1,0:T(8,128)(2,1)} %get-tuple-element.134.refs_16_.refs_20_), channel_id=1, source_target_pairs={{0,4},{4,0},{8,12},{12,8},{1,5},{5,1},{9,13},{13,9},{2,6},{6,2},{1... | collective-permute-start | bytes 1572872 | tf_op jit(solution)/shard_map/ppermute | solution.py:537
  204.8 13.8 %collective-permute-start.32 = (bf16[128,2048]{1,0:T(8,128)(2,1)}, bf16[128,2048]{1,0:T(8,128)(2,1)S(1)}, u32[]{:S(2)}, u32[]{:S(2)}) collective-permute-start(bf16[128,2048]{1,0:T(8,128)(2,1)} %get-tuple-element.143.refs_24_.refs_28_), channel_id=1, source_target_pairs={{0,4},{4,0},{8,12},{12,8},{1,5},{5,1},{9,13},{13,9},{2,6},{6,2},{1... | collective-permute-start | bytes 1572872 | tf_op jit(solution)/shard_map/ppermute | solution.py:537
  225.4 13.7 %collective-permute-start.36 = (bf16[128,2048]{1,0:T(8,128)(2,1)}, bf16[128,2048]{1,0:T(8,128)(2,1)S(1)}, u32[]{:S(2)}, u32[]{:S(2)}) collective-permute-start(bf16[128,2048]{1,0:T(8,128)(2,1)} %get-tuple-element.152.refs_0_.refs_4_), channel_id=1, source_target_pairs={{0,4},{4,0},{8,12},{12,8},{1,5},{5,1},{9,13},{13,9},{2,6},{6,2},{1... | collective-permute-start | bytes 1572872 | tf_op jit(solution)/shard_map/ppermute | solution.py:537
  231.0 14.8 %collective-permute-start.42 = (bf16[128,1408]{1,0:T(8,128)(2,1)S(1)}, bf16[128,1408]{1,0:T(8,128)(2,1)S(1)}, u32[]{:S(2)}, u32[]{:S(2)}) collective-permute-start(bf16[128,1408]{1,0:T(8,128)(2,1)S(1)} %fusion.9), channel_id=1, source_target_pairs={{0,4},{4,0},{8,12},{12,8},{1,5},{5,1},{9,13},{13,9},{2,6},{6,2},{1... | collective-permute-start | bytes 1081352 | tf_op jit(solution)/shard_map/ppermute | solution.py:537
  291.8 26.6 %collective-permute-start.47 = (bf16[256,1152]{1,0:T(8,128)(2,1)}, bf16[256,1152]{1,0:T(8,128)(2,1)S(1)}, u32[]{:S(2)}, u32[]{:S(2)}) collective-permute-start(bf16[256,1152]{1,0:T(8,128)(2,1)} %constant_dynamic-slice_fusion.2), channel_id=1, source_target_pairs={{0,1},{1,0},{2,3},{3,2},{4,5},{5,4},{6,7},{7,6},{8,9},{9,8},{10,11... | collective-permute-start | bytes 1769480 | tf_op jit(solution)/shard_map/ppermute | solution.py:628
  304.4 14.0 %collective-permute-start.51 = (bf16[256,1152]{1,0:T(8,128)(2,1)}, bf16[256,1152]{1,0:T(8,128)(2,1)S(1)}, u32[]{:S(2)}, u32[]{:S(2)}) collective-permute-start(bf16[256,1152]{1,0:T(8,128)(2,1)} %get-tuple-element.183), channel_id=1, source_target_pairs={{0,1},{1,0},{2,3},{3,2},{4,5},{5,4},{6,7},{7,6},{8,9},{9,8},{10,11... | collective-permute-start | bytes 1769480 | tf_op jit(solution)/shard_map/ppermute | solution.py:630
  306.6 14.4 %collective-permute-start.53 = (bf16[1024,128]{0,1:T(8,128)(2,1)}, bf16[1024,128]{0,1:T(8,128)(2,1)}, u32[]{:S(2)}, u32[]{:S(2)}) collective-permute-start(bf16[1024,128]{0,1:T(8,128)(2,1)} %get-tuple-element.231), channel_id=1, source_target_pairs={{0,4},{12,8},{1,5},{13,9},{2,6},{14,10},{3,7},{15,11},{16,20},{28,... | collective-permute-start | bytes 786440 | tf_op jit(solution)/shard_map/ppermute | solution.py:622
  314.8 14.2 %collective-permute-start.55 = (bf16[1024,128]{0,1:T(8,128)(2,1)}, bf16[1024,128]{0,1:T(8,128)(2,1)}, u32[]{:S(2)}, u32[]{:S(2)}) collective-permute-start(bf16[1024,128]{0,1:T(8,128)(2,1)} %get-tuple-element.228), channel_id=1, source_target_pairs={{0,12},{12,0},{1,13},{13,1},{2,14},{14,2},{3,15},{15,3},{16,28},{2... | collective-permute-start | bytes 786440 | tf_op jit(solution)/shard_map/ppermute | solution.py:622
  319.6 16.3 %collective-permute-start.52 = (bf16[256,1152]{1,0:T(8,128)(2,1)}, bf16[256,1152]{1,0:T(8,128)(2,1)}, u32[]{:S(2)}, u32[]{:S(2)}) collective-permute-start(bf16[256,1152]{1,0:T(8,128)(2,1)} %broadcast_select_fusion), channel_id=1, source_target_pairs={{0,2},{1,3},{2,0},{3,1},{4,6},{5,7},{6,4},{7,5},{8,10},{9,11},{10,... | collective-permute-start | bytes 1769480 | tf_op jit(solution)/shard_map/ppermute | solution.py:634
  (76 other events, 719.1 us)

commit v7 on v6

--- a/solution.py
+++ b/solution.py
@@ -328,41 +328,34 @@
         ).start()
     fetch(lambda copy: copy.wait())
 
-    def put(columns, result):
+    def put(part, columns, result):
         if paired:
             mine = where[1] == 0
-            before = prior[:, columns].astype(f32)
-            out[:, columns] = jnp.where(mine, before, result).astype(bf16)
-            handed[0][:, columns] = jnp.where(mine, result, before).astype(bf16)
+            before = prior[part, columns].astype(f32)
+            out[part, columns] = jnp.where(mine, before, result).astype(bf16)
+            handed[0][part, columns] = jnp.where(mine, result, before).astype(bf16)
         else:
-            out[:, columns] = result.astype(bf16)
-
-    sums = []
-    for block in range(count):
-        part = slice(block * BLOCK, (block + 1) * BLOCK)
-
-        def some_channels(at, total):
-            lanes = pl.ds(pl.multiple_of(at * LANES, LANES), LANES)
-            values = held[part, lanes].astype(f32)
-            held[part, lanes] = (values * gain[:, lanes]).astype(bf16)
-            return total + values * values
-
-        total = lax.fori_loop(
-            0, 2 * ch // LANES, some_channels, jnp.zeros((BLOCK, LANES), f32), unroll=2
-        )
-        sums.append(jnp.sum(total, axis=1, keepdims=True))
-    squares = jnp.concatenate(sums, axis=0)
+            out[part, columns] = result.astype(bf16)
+
+    def some_rows(at, carry):
+        part = pl.ds(pl.multiple_of(at * BLOCK, BLOCK), BLOCK)
+        values = held[part, :].astype(f32)
+        squares = jnp.sum(values * values, axis=1, keepdims=True)
+        held[part, :] = (values * gain[...]).astype(bf16)
+        put(part, slice(width, width + LANES), jnp.broadcast_to(squares, (BLOCK, LANES)))
+        return carry
+
+    lax.fori_loop(0, count, some_rows, 0)
 
     def some_columns(at, carry):
         part = pl.ds(pl.multiple_of(at * tile, tile), tile)
         pltpu.make_async_copy(
             weight_source.at[:, part], weight.at[:, part], weight_sems.at[at]
         ).wait()
-        put(part, jnp.dot(held[...], weight[:, part], preferred_element_type=f32))
+        put(slice(None), part, jnp.dot(held[...], weight[:, part], preferred_element_type=f32))
         return carry
 
     lax.fori_loop(0, tiles, some_columns, 0)
-    put(slice(width, width + LANES), jnp.broadcast_to(squares, (count * BLOCK, LANES)))
 
 
 def output_block(where, blocks, n, gain, weight, ch, prior=None):

time: 341 us -> 339 us (level)
  transfers between devices with their start and end apart: 56 -> 56, of which waited for: 15 -> 15; matrix products, arithmetic and copies ran while one was open for 17% -> 17% of each run, Pallas kernels for 23% -> 22%
where the time goes in v7:
time: 339 us; the launch traced here: 337 us
  Pallas kernels  105 us (31%)
  starting transfers between devices  104 us (31%)
  waiting for transfers between devices  49.6 us (15%)
  other arithmetic  41.2 us (12%)
  local copies, waits for them, and re-layouts  35.3 us (10%)
    ppermute x24, starting transfers between devices, onward(): from_a = lax.ppermute(pair[0], 'seq', pairs_a)  70.7 us
    ppermute x24, waiting for transfers between devices, onward(): from_a = lax.ppermute(pair[0], 'seq', pairs_a)  39.5 us
    pallas_call x8, Pallas kernels, scan_block(): pl.pallas_call(scan_kernel, out_shape=outs, grid=(1,), in_specs=[pl.Block...  39 us
    pallas_call x3, Pallas kernels, output_block(): pl.pallas_call(functools.partial(output_kernel, n=n, count=count, paired=...  23.7 us
    pallas_call x1, Pallas kernels, project(): pl.pallas_call(functools.partial(project_kernel, rows=rows, first=first,...  23.4 us
    pallas_call x6, Pallas kernels, merge(): pl.pallas_call(functools.partial(merge_kernel, passing=passing), out_shap...  19.1 us
    convert_element_type x14, other arithmetic, added(): return (a.astype(f32) + b.astype(f32)).astype(bf16)  18.8 us
    ppermute x22, starting transfers between devices, onward(): from_b = lax.ppermute(pair[1], 'seq', pairs_b)  15.2 us
  transfers between devices with their start and end apart: 56, of which 15 were waited for; matrix products, arithmetic and copies ran while one was open for 17% of the time, Pallas kernels for 22%

profile of v7, /device:TPU:0, one launch (start us, length us, event | category | flops | bytes accessed | tf_op | source)
XLA Modules:
  0.0 337.4 jit_solution(1325780216008902869)
XLA Ops:
  13.7 11.5 %copy.48 = bf16[64,16,2,2048]{3,1,2,0:T(8,128)(2,1)} copy(bf16[64,16,2,2048]{3,2,1,0:T(2,128)(2,1)} %bitcast.181) | data formatting | bytes 16777216 | tf_op jit(solution)/shard_map/reshape | solution.py:455
  33.2 23.4 %project.1 = (bf16[2,1024,1408]{2,1,0:T(8,128)(2,1)}, bf16[2,1024,1024]{2,1,0:T(8,128)(2,1)}) custom-call(s32[6]{0:T(128)} %stack.138.where, bf16[4,272,512]{2,1,0:T(8,128)(2,1)} %copy-done.29, bf16[4,272,512]{2,1,0:T(8,128)(2,1)} %collective-permute-done.3.refs_1_, bf16[1024,256]{1,0:T(8,128)(2,1)} %refs_2_.1, bf16[64,2,16,2048]{3,2,1,0:T(8,128)(2,1)} %bitcast.182, ...), custom_call_target="tpu_custom_call" | custom-call | flops 12750684160 | bytes 18350080 | tf_op jit(solution)/shard_map/project/pallas_call | solution.py:119
  57.8 5.1 %collective-permute-start.6 = (bf16[128,1408]{1,0:T(8,128)(2,1)S(1)}, bf16[128,1408]{1,0:T(8,128)(2,1)S(1)}, u32[]{:S(2)}, u32[]{:S(2)}) collective-permute-start(bf16[128,1408]{1,0:T(8,128)(2,1)S(1)} %get-tuple-element.211), channel_id=1, source_target_pairs={{0,4},{4,0},{8,12},{12,8},{1,5},{5,1},{9,13},{13,9},{2,6},{6,2},{1... | collective-permute-start | bytes 1081352 | tf_op jit(solution)/shard_map/ppermute | solution.py:530
  64.5 7.1 %collective-permute-done.6 = bf16[128,1408]{1,0:T(8,128)(2,1)S(1)} collective-permute-done((bf16[128,1408]{1,0:T(8,128)(2,1)S(1)}, bf16[128,1408]{1,0:T(8,128)(2,1)S(1)}, u32[]{:S(2)}, u32[]{:S(2)}) %collective-permute-start.6) | collective-permute-done | bytes 360480 | tf_op jit(solution)/shard_map/ppermute | solution.py:530
  72.9 3.8 %collective-permute-start.10 = (bf16[128,1408]{1,0:T(8,128)(2,1)S(1)}, bf16[128,1408]{1,0:T(8,128)(2,1)S(1)}, u32[]{:S(2)}, u32[]{:S(2)}) collective-permute-start(bf16[128,1408]{1,0:T(8,128)(2,1)S(1)} %get-tuple-element.209), channel_id=1, source_target_pairs={{0,4},{4,0},{8,12},{12,8},{1,5},{5,1},{9,13},{13,9},{2,6},{6,2},{1... | collective-permute-start | bytes 1081352 | tf_op jit(solution)/shard_map/ppermute | solution.py:530
  83.7 6.4 %collective-permute-done.4 = bf16[128,1024]{1,0:T(8,128)(2,1)S(1)} collective-permute-done((bf16[128,1024]{1,0:T(8,128)(2,1)S(1)}, bf16[128,1024]{1,0:T(8,128)(2,1)S(1)}, u32[]{:S(2)}, u32[]{:S(2)}) %collective-permute-start.4) | collective-permute-done | bytes 262176 | tf_op jit(solution)/shard_map/ppermute | solution.py:530
  91.5 3.7 %collective-permute-start.14 = (bf16[128,1408]{1,0:T(8,128)(2,1)S(1)}, bf16[128,1408]{1,0:T(8,128)(2,1)S(1)}, u32[]{:S(2)}, u32[]{:S(2)}) collective-permute-start(bf16[128,1408]{1,0:T(8,128)(2,1)S(1)} %get-tuple-element.207), channel_id=1, source_target_pairs={{0,4},{4,0},{8,12},{12,8},{1,5},{5,1},{9,13},{13,9},{2,6},{6,2},{1... | collective-permute-start | bytes 1081352 | tf_op jit(solution)/shard_map/ppermute | solution.py:530
  101.7 6.1 %collective-permute-done.8 = bf16[128,1024]{1,0:T(8,128)(2,1)S(1)} collective-permute-done((bf16[128,1024]{1,0:T(8,128)(2,1)S(1)}, bf16[128,1024]{1,0:T(8,128)(2,1)S(1)}, u32[]{:S(2)}, u32[]{:S(2)}) %collective-permute-start.8) | collective-permute-done | bytes 262176 | tf_op jit(solution)/shard_map/ppermute | solution.py:530
  109.1 3.7 %collective-permute-start.18 = (bf16[128,1408]{1,0:T(8,128)(2,1)S(1)}, bf16[128,1408]{1,0:T(8,128)(2,1)S(1)}, u32[]{:S(2)}, u32[]{:S(2)}) collective-permute-start(bf16[128,1408]{1,0:T(8,128)(2,1)S(1)} %get-tuple-element.205), channel_id=1, source_target_pairs={{0,4},{4,0},{8,12},{12,8},{1,5},{5,1},{9,13},{13,9},{2,6},{6,2},{1... | collective-permute-start | bytes 1081352 | tf_op jit(solution)/shard_map/ppermute | solution.py:530
  125.8 3.7 %collective-permute-start.22 = (bf16[128,1408]{1,0:T(8,128)(2,1)S(1)}, bf16[128,1408]{1,0:T(8,128)(2,1)S(1)}, u32[]{:S(2)}, u32[]{:S(2)}) collective-permute-start(bf16[128,1408]{1,0:T(8,128)(2,1)S(1)} %get-tuple-element.203), channel_id=1, source_target_pairs={{0,4},{4,0},{8,12},{12,8},{1,5},{5,1},{9,13},{13,9},{2,6},{6,2},{1... | collective-permute-start | bytes 1081352 | tf_op jit(solution)/shard_map/ppermute | solution.py:530
  135.0 4.8 %scan_block.8 = (bf16[128,1024]{1,0:T(8,128)(2,1)}, f32[128,1024]{1,0:T(8,128)}, f32[8,1280]{1,0:T(8,128)}) custom-call(bf16[128,1024]{1,0:T(8,128)(2,1)} %copy-done.30, bf16[128,1408]{1,0:T(8,128)(2,1)} %copy-done.23, f32[8,1280]{1,0:T(8,128)} %fusion.40.tail, f32[128,1024]{1,0:T(8,128)} %bitcast.187, f32[1,128]{1,0:T(1,128)} %get-tuple-element.245.index, ...), custom_call_target="tpu_custom_call" | custom-call | flops 134217728 | bytes 2097152 | tf_op jit(solution)/shard_map/scan_block/pallas_call | solution.py:273
  153.5 4.9 %scan_block.9 = (bf16[128,1024]{1,0:T(8,128)(2,1)}, f32[128,1024]{1,0:T(8,128)}, f32[8,1280]{1,0:T(8,128)}) custom-call(bf16[128,2048]{1,0:T(8,128)(2,1)} %get-tuple-element.117.gates, bf16[128,1408]{1,0:T(8,128)(2,1)} %copy-done.24, f32[8,1280]{1,0:T(8,128)} %get-tuple-element.122.tail, f32[128,1024]{1,0:T(8,128)} %get-tuple-element.123.state, ...), custom_call_target="tpu_custom_call" | custom-call | flops 134217728 | bytes 2097152 | tf_op jit(solution)/shard_map/scan_block/pallas_call | solution.py:273
  172.8 4.9 %scan_block.10 = (bf16[128,1024]{1,0:T(8,128)(2,1)}, f32[128,1024]{1,0:T(8,128)}, f32[8,1280]{1,0:T(8,128)}) custom-call(bf16[128,2048]{1,0:T(8,128)(2,1)} %get-tuple-element.126.gates, bf16[128,1408]{1,0:T(8,128)(2,1)} %copy-done.25, f32[8,1280]{1,0:T(8,128)} %get-tuple-element.131.tail, f32[128,1024]{1,0:T(8,128)} %get-tuple-element.132.state, ...), custom_call_target="tpu_custom_call" | custom-call | flops 134217728 | bytes 2097152 | tf_op jit(solution)/shard_map/scan_block/pallas_call | solution.py:273
  193.5 4.9 %scan_block.11 = (bf16[128,1024]{1,0:T(8,128)(2,1)}, f32[128,1024]{1,0:T(8,128)}, f32[8,1280]{1,0:T(8,128)}) custom-call(bf16[128,2048]{1,0:T(8,128)(2,1)} %get-tuple-element.135.gates, bf16[128,1408]{1,0:T(8,128)(2,1)} %copy-done.26, f32[8,1280]{1,0:T(8,128)} %get-tuple-element.140.tail, f32[128,1024]{1,0:T(8,128)} %get-tuple-element.141.state, ...), custom_call_target="tpu_custom_call" | custom-call | flops 134217728 | bytes 2097152 | tf_op jit(solution)/shard_map/scan_block/pallas_call | solution.py:273
  213.8 4.9 %scan_block.12 = (bf16[128,1024]{1,0:T(8,128)(2,1)}, f32[128,1024]{1,0:T(8,128)}, f32[8,1280]{1,0:T(8,128)}) custom-call(bf16[128,2048]{1,0:T(8,128)(2,1)} %get-tuple-element.144.gates, bf16[128,1408]{1,0:T(8,128)(2,1)} %copy-done.27, f32[8,1280]{1,0:T(8,128)} %get-tuple-element.149.tail, f32[128,1024]{1,0:T(8,128)} %get-tuple-element.150.state, ...), custom_call_target="tpu_custom_call" | custom-call | flops 134217728 | bytes 2097152 | tf_op jit(solution)/shard_map/scan_block/pallas_call | solution.py:273
  234.2 4.9 %scan_block.13 = (bf16[128,1024]{1,0:T(8,128)(2,1)}, f32[128,1024]{1,0:T(8,128)}, f32[8,1280]{1,0:T(8,128)}) custom-call(bf16[128,2048]{1,0:T(8,128)(2,1)} %get-tuple-element.153.gates, bf16[128,1408]{1,0:T(8,128)(2,1)} %copy-done.28, f32[8,1280]{1,0:T(8,128)} %get-tuple-element.158.tail, f32[128,1024]{1,0:T(8,128)} %get-tuple-element.159.state, ...), custom_call_target="tpu_custom_call" | custom-call | flops 134217728 | bytes 2097152 | tf_op jit(solution)/shard_map/scan_block/pallas_call | solution.py:273
  248.0 4.9 %scan_block.14 = (bf16[128,1024]{1,0:T(8,128)(2,1)}, f32[128,1024]{1,0:T(8,128)}, f32[8,1280]{1,0:T(8,128)}) custom-call(bf16[128,2048]{1,0:T(8,128)(2,1)} %get-tuple-element.162.gates, bf16[128,1408]{1,0:T(8,128)(2,1)} %get-tuple-element.193.sums, f32[8,1280]{1,0:T(8,128)} %get-tuple-element.165.tail, f32[128,1024]{1,0:T(8,128)} %get-tuple-element.166.state, ...), custom_call_target="tpu_custom_call" | custom-call | flops 134217728 | bytes 2097152 | tf_op jit(solution)/shard_map/scan_block/pallas_call | solution.py:273
  260.3 4.9 %scan_block.15 = (bf16[128,1024]{1,0:T(8,128)(2,1)}, f32[128,1024]{1,0:T(8,128)}, f32[8,1280]{1,0:T(8,128)}) custom-call(bf16[128,1024]{1,0:T(8,128)(2,1)} %fusion.32.gates, bf16[128,1408]{1,0:T(8,128)(2,1)} %get-tuple-element.192.sums, f32[8,1280]{1,0:T(8,128)} %get-tuple-element.167.tail, f32[128,1024]{1,0:T(8,128)} %get-tuple-element.168.state, ...), custom_call_target="tpu_custom_call" | custom-call | flops 134217728 | bytes 2097152 | tf_op jit(solution)/shard_map/scan_block/pallas_call | solution.py:273
  269.3 8.9 %output_block.3 = bf16[512,1152]{1,0:T(8,128)(2,1)} custom-call(s32[2]{0:T(128)} %pad_add_fusion.6.where, bf16[128,2048]{1,0:T(8,128)(2,1)} %get-tuple-element.116.refs_0_.refs_4_, bf16[128,2048]{1,0:T(8,128)(2,1)} %copy-done.7, bf16[128,2048]{1,0:T(8,128)(2,1)} %copy-done.9, bf16[128,2048]{1,0:T(8,128)(2,1)} %copy-done.2, ...), custom_call_target="tpu_custom_call" | custom-call | flops 2147483648 | bytes 8388608 | tf_op jit(solution)/shard_map/output_block/pallas_call | solution.py:367
  281.3 7.1 %output_block.4.refs_18_ = bf16[256,1152]{1,0:T(8,128)(2,1)} custom-call(s32[2]{0:T(128)} %pad_add_fusion.6.where, bf16[128,2048]{1,0:T(8,128)(2,1)} %get-tuple-element.152.refs_0_.refs_4_, bf16[128,2048]{1,0:T(8,128)(2,1)} %copy-done.4, bf16[128,2048]{1,0:T(8,128)(2,1)} %copy-done.15, bf16[128,1024]{1,0:T(8,128)(2,1)} %copy-done.13, ...), custom_call_target="tpu_custom_call" | custom-call | flops 1073741824 | bytes 6291456 | tf_op jit(solution)/shard_map/output_block/pallas_call | solution.py:367
  291.0 3.9 %collective-permute-done.50.refs_11_.refs_15_ = bf16[128,1024]{1,0:T(8,128)(2,1)S(1)} collective-permute-done((bf16[128,1024]{1,0:T(8,128)(2,1)S(1)}, bf16[128,1024]{1,0:T(8,128)(2,1)S(1)}, u32[]{:S(2)}, u32[]{:S(2)}) %collective-permute-start.50) | collective-permute-done | bytes 262176 | tf_op jit(solution)/shard_map/ppermute | solution.py:530
  295.6 7.7 %output_block.5 = (bf16[256,1152]{1,0:T(8,128)(2,1)}, bf16[256,1152]{1,0:T(8,128)(2,1)}) custom-call(s32[2]{0:T(128)} %pad_add_fusion.6.where, bf16[128,1024]{1,0:T(8,128)(2,1)} %copy-done.20, bf16[128,1024]{1,0:T(8,128)(2,1)} %copy-done.13, bf16[128,1024]{1,0:T(8,128)(2,1)} %copy-done.31, bf16[128,1024]{1,0:T(8,128)(2,1)} %copy-done.32, ...), custom_call_target="tpu_custom_call" | custom-call | flops 1073741824 | bytes 6291456 | tf_op jit(solution)/shard_map/output_block/pallas_call | solution.py:367
  305.6 4.2 %collective-permute-start.53 = (bf16[1024,128]{0,1:T(8,128)(2,1)}, bf16[1024,128]{0,1:T(8,128)(2,1)}, u32[]{:S(2)}, u32[]{:S(2)}) collective-permute-start(bf16[1024,128]{0,1:T(8,128)(2,1)} %get-tuple-element.231), channel_id=1, source_target_pairs={{0,4},{12,8},{1,5},{13,9},{2,6},{14,10},{3,7},{15,11},{16,20},{28,... | collective-permute-start | bytes 786440 | tf_op jit(solution)/shard_map/ppermute | solution.py:615
  321.7 6.3 %collective-permute-done.55 = bf16[1024,128]{0,1:T(8,128)(2,1)} collective-permute-done((bf16[1024,128]{0,1:T(8,128)(2,1)}, bf16[1024,128]{0,1:T(8,128)(2,1)}, u32[]{:S(2)}, u32[]{:S(2)}) %collective-permute-start.55) | collective-permute-done | bytes 262176 | tf_op jit(solution)/shard_map/ppermute | solution.py:615
  (269 shorter events, 183.9 us)
Async XLA Ops:
  3.6 25.4 %collective-permute-start = (bf16[272,512]{1,0:T(8,128)(2,1)}, bf16[272,512]{1,0:T(8,128)(2,1)}, u32[]{:S(2)}, u32[]{:S(2)}) collective-permute-start(bf16[272,512]{1,0:T(8,128)(2,1)} %get-tuple-element.235), channel_id=1, source_target_pairs={{0,4},{4,8},{8,12},{12,0},{1,5},{5,9},{9,13},{13,1},{2,6},{6,10},{... | collective-permute-start | bytes 835592 | tf_op jit(solution)/shard_map/ppermute | solution.py:452
  6.7 22.3 %collective-permute-start.1 = (bf16[272,512]{1,0:T(8,128)(2,1)S(1)}, bf16[272,512]{1,0:T(8,128)(2,1)}, u32[]{:S(2)}, u32[]{:S(2)}) collective-permute-start(bf16[272,512]{1,0:T(8,128)(2,1)S(1)} %get-tuple-element.236), channel_id=1, source_target_pairs={{0,8},{4,12},{8,0},{12,4},{1,9},{5,13},{9,1},{13,5},{2,10},{6,14},... | collective-permute-start | bytes 835592 | tf_op jit(solution)/shard_map/ppermute | solution.py:452
  9.3 19.7 %collective-permute-start.2 = (bf16[272,512]{1,0:T(8,128)(2,1)S(1)}, bf16[272,512]{1,0:T(8,128)(2,1)}, u32[]{:S(2)}, u32[]{:S(2)}) collective-permute-start(bf16[272,512]{1,0:T(8,128)(2,1)S(1)} %get-tuple-element.237), channel_id=1, source_target_pairs={{0,12},{4,0},{8,4},{12,8},{1,13},{5,1},{9,5},{13,9},{2,14},{6,2},{... | collective-permute-start | bytes 835592 | tf_op jit(solution)/shard_map/ppermute | solution.py:452
  57.8 13.8 %collective-permute-start.6 = (bf16[128,1408]{1,0:T(8,128)(2,1)S(1)}, bf16[128,1408]{1,0:T(8,128)(2,1)S(1)}, u32[]{:S(2)}, u32[]{:S(2)}) collective-permute-start(bf16[128,1408]{1,0:T(8,128)(2,1)S(1)} %get-tuple-element.211), channel_id=1, source_target_pairs={{0,4},{4,0},{8,12},{12,8},{1,5},{5,1},{9,13},{13,9},{2,6},{6,2},{1... | collective-permute-start | bytes 1081352 | tf_op jit(solution)/shard_map/ppermute | solution.py:530
  72.9 17.3 %collective-permute-start.10 = (bf16[128,1408]{1,0:T(8,128)(2,1)S(1)}, bf16[128,1408]{1,0:T(8,128)(2,1)S(1)}, u32[]{:S(2)}, u32[]{:S(2)}) collective-permute-start(bf16[128,1408]{1,0:T(8,128)(2,1)S(1)} %get-tuple-element.209), channel_id=1, source_target_pairs={{0,4},{4,0},{8,12},{12,8},{1,5},{5,1},{9,13},{13,9},{2,6},{6,2},{1... | collective-permute-start | bytes 1081352 | tf_op jit(solution)/shard_map/ppermute | solution.py:530
  91.5 16.3 %collective-permute-start.14 = (bf16[128,1408]{1,0:T(8,128)(2,1)S(1)}, bf16[128,1408]{1,0:T(8,128)(2,1)S(1)}, u32[]{:S(2)}, u32[]{:S(2)}) collective-permute-start(bf16[128,1408]{1,0:T(8,128)(2,1)S(1)} %get-tuple-element.207), channel_id=1, source_target_pairs={{0,4},{4,0},{8,12},{12,8},{1,5},{5,1},{9,13},{13,9},{2,6},{6,2},{1... | collective-permute-start | bytes 1081352 | tf_op jit(solution)/shard_map/ppermute | solution.py:530
  109.1 15.5 %collective-permute-start.18 = (bf16[128,1408]{1,0:T(8,128)(2,1)S(1)}, bf16[128,1408]{1,0:T(8,128)(2,1)S(1)}, u32[]{:S(2)}, u32[]{:S(2)}) collective-permute-start(bf16[128,1408]{1,0:T(8,128)(2,1)S(1)} %get-tuple-element.205), channel_id=1, source_target_pairs={{0,4},{4,0},{8,12},{12,8},{1,5},{5,1},{9,13},{13,9},{2,6},{6,2},{1... | collective-permute-start | bytes 1081352 | tf_op jit(solution)/shard_map/ppermute | solution.py:530
  125.8 22.6 %collective-permute-start.22 = (bf16[128,1408]{1,0:T(8,128)(2,1)S(1)}, bf16[128,1408]{1,0:T(8,128)(2,1)S(1)}, u32[]{:S(2)}, u32[]{:S(2)}) collective-permute-start(bf16[128,1408]{1,0:T(8,128)(2,1)S(1)} %get-tuple-element.203), channel_id=1, source_target_pairs={{0,4},{4,0},{8,12},{12,8},{1,5},{5,1},{9,13},{13,9},{2,6},{6,2},{1... | collective-permute-start | bytes 1081352 | tf_op jit(solution)/shard_map/ppermute | solution.py:530
  129.5 18.9 %collective-permute-start.23 = (bf16[128,1408]{1,0:T(8,128)(2,1)S(1)}, bf16[128,1408]{1,0:T(8,128)(2,1)S(1)}, u32[]{:S(2)}, u32[]{:S(2)}) collective-permute-start(bf16[128,1408]{1,0:T(8,128)(2,1)S(1)} %get-tuple-element.202.sums), channel_id=1, source_target_pairs={{4,8},{8,4},{5,9},{9,5},{6,10},{10,6},{7,11},{11,7},{20,24},{24,20... | collective-permute-start | bytes 1081352 | tf_op jit(solution)/shard_map/ppermute | solution.py:531
  144.2 15.6 %collective-permute-start.20 = (bf16[128,2048]{1,0:T(8,128)(2,1)}, bf16[128,2048]{1,0:T(8,128)(2,1)S(1)}, u32[]{:S(2)}, u32[]{:S(2)}) collective-permute-start(bf16[128,2048]{1,0:T(8,128)(2,1)} %get-tuple-element.116.refs_0_.refs_4_), channel_id=1, source_target_pairs={{0,4},{4,0},{8,12},{12,8},{1,5},{5,1},{9,13},{13,9},{2,6},{6,2},{1... | collective-permute-start | bytes 1572872 | tf_op jit(solution)/shard_map/ppermute | solution.py:530
  149.8 18.4 %collective-permute-start.26 = (bf16[128,1408]{1,0:T(8,128)(2,1)S(1)}, bf16[128,1408]{1,0:T(8,128)(2,1)S(1)}, u32[]{:S(2)}, u32[]{:S(2)}) collective-permute-start(bf16[128,1408]{1,0:T(8,128)(2,1)S(1)} %get-tuple-element.201), channel_id=1, source_target_pairs={{0,4},{4,0},{8,12},{12,8},{1,5},{5,1},{9,13},{13,9},{2,6},{6,2},{1... | collective-permute-start | bytes 1081352 | tf_op jit(solution)/shard_map/ppermute | solution.py:530
  152.2 16.0 %collective-permute-start.27 = (bf16[128,1408]{1,0:T(8,128)(2,1)S(1)}, bf16[128,1408]{1,0:T(8,128)(2,1)S(1)}, u32[]{:S(2)}, u32[]{:S(2)}) collective-permute-start(bf16[128,1408]{1,0:T(8,128)(2,1)S(1)} %get-tuple-element.200.sums), channel_id=1, source_target_pairs={{4,8},{8,4},{5,9},{9,5},{6,10},{10,6},{7,11},{11,7},{20,24},{24,20... | collective-permute-start | bytes 1081352 | tf_op jit(solution)/shard_map/ppermute | solution.py:531
  164.0 15.4 %collective-permute-start.24 = (bf16[128,2048]{1,0:T(8,128)(2,1)}, bf16[128,2048]{1,0:T(8,128)(2,1)S(1)}, u32[]{:S(2)}, u32[]{:S(2)}) collective-permute-start(bf16[128,2048]{1,0:T(8,128)(2,1)} %get-tuple-element.125.refs_8_.refs_12_), channel_id=1, source_target_pairs={{0,4},{4,0},{8,12},{12,8},{1,5},{5,1},{9,13},{13,9},{2,6},{6,2},{1... | collective-permute-start | bytes 1572872 | tf_op jit(solution)/shard_map/ppermute | solution.py:530
  169.4 18.3 %collective-permute-start.30 = (bf16[128,1408]{1,0:T(8,128)(2,1)S(1)}, bf16[128,1408]{1,0:T(8,128)(2,1)S(1)}, u32[]{:S(2)}, u32[]{:S(2)}) collective-permute-start(bf16[128,1408]{1,0:T(8,128)(2,1)S(1)} %get-tuple-element.199), channel_id=1, source_target_pairs={{0,4},{4,0},{8,12},{12,8},{1,5},{5,1},{9,13},{13,9},{2,6},{6,2},{1... | collective-permute-start | bytes 1081352 | tf_op jit(solution)/shard_map/ppermute | solution.py:530
  172.1 15.7 %collective-permute-start.31 = (bf16[128,1408]{1,0:T(8,128)(2,1)S(1)}, bf16[128,1408]{1,0:T(8,128)(2,1)S(1)}, u32[]{:S(2)}, u32[]{:S(2)}) collective-permute-start(bf16[128,1408]{1,0:T(8,128)(2,1)S(1)} %get-tuple-element.198.sums), channel_id=1, source_target_pairs={{4,8},{8,4},{5,9},{9,5},{6,10},{10,6},{7,11},{11,7},{20,24},{24,20... | collective-permute-start | bytes 1081352 | tf_op jit(solution)/shard_map/ppermute | solution.py:531
  183.6 14.8 %collective-permute-start.28 = (bf16[128,2048]{1,0:T(8,128)(2,1)}, bf16[128,2048]{1,0:T(8,128)(2,1)S(1)}, u32[]{:S(2)}, u32[]{:S(2)}) collective-permute-start(bf16[128,2048]{1,0:T(8,128)(2,1)} %get-tuple-element.134.refs_16_.refs_20_), channel_id=1, source_target_pairs={{0,4},{4,0},{8,12},{12,8},{1,5},{5,1},{9,13},{13,9},{2,6},{6,2},{1... | collective-permute-start | bytes 1572872 | tf_op jit(solution)/shard_map/ppermute | solution.py:530
  204.8 13.8 %collective-permute-start.32 = (bf16[128,2048]{1,0:T(8,128)(2,1)}, bf16[128,2048]{1,0:T(8,128)(2,1)S(1)}, u32[]{:S(2)}, u32[]{:S(2)}) collective-permute-start(bf16[128,2048]{1,0:T(8,128)(2,1)} %get-tuple-element.143.refs_24_.refs_28_), channel_id=1, source_target_pairs={{0,4},{4,0},{8,12},{12,8},{1,5},{5,1},{9,13},{13,9},{2,6},{6,2},{1... | collective-permute-start | bytes 1572872 | tf_op jit(solution)/shard_map/ppermute | solution.py:530
  225.4 13.7 %collective-permute-start.36 = (bf16[128,2048]{1,0:T(8,128)(2,1)}, bf16[128,2048]{1,0:T(8,128)(2,1)S(1)}, u32[]{:S(2)}, u32[]{:S(2)}) collective-permute-start(bf16[128,2048]{1,0:T(8,128)(2,1)} %get-tuple-element.152.refs_0_.refs_4_), channel_id=1, source_target_pairs={{0,4},{4,0},{8,12},{12,8},{1,5},{5,1},{9,13},{13,9},{2,6},{6,2},{1... | collective-permute-start | bytes 1572872 | tf_op jit(solution)/shard_map/ppermute | solution.py:530
  231.0 14.8 %collective-permute-start.42 = (bf16[128,1408]{1,0:T(8,128)(2,1)S(1)}, bf16[128,1408]{1,0:T(8,128)(2,1)S(1)}, u32[]{:S(2)}, u32[]{:S(2)}) collective-permute-start(bf16[128,1408]{1,0:T(8,128)(2,1)S(1)} %fusion.9), channel_id=1, source_target_pairs={{0,4},{4,0},{8,12},{12,8},{1,5},{5,1},{9,13},{13,9},{2,6},{6,2},{1... | collective-permute-start | bytes 1081352 | tf_op jit(solution)/shard_map/ppermute | solution.py:530
  291.0 26.3 %collective-permute-start.47 = (bf16[256,1152]{1,0:T(8,128)(2,1)}, bf16[256,1152]{1,0:T(8,128)(2,1)S(1)}, u32[]{:S(2)}, u32[]{:S(2)}) collective-permute-start(bf16[256,1152]{1,0:T(8,128)(2,1)} %constant_dynamic-slice_fusion.2), channel_id=1, source_target_pairs={{0,1},{1,0},{2,3},{3,2},{4,5},{5,4},{6,7},{7,6},{8,9},{9,8},{10,11... | collective-permute-start | bytes 1769480 | tf_op jit(solution)/shard_map/ppermute | solution.py:621
  303.3 14.0 %collective-permute-start.51 = (bf16[256,1152]{1,0:T(8,128)(2,1)}, bf16[256,1152]{1,0:T(8,128)(2,1)S(1)}, u32[]{:S(2)}, u32[]{:S(2)}) collective-permute-start(bf16[256,1152]{1,0:T(8,128)(2,1)} %get-tuple-element.183), channel_id=1, source_target_pairs={{0,1},{1,0},{2,3},{3,2},{4,5},{5,4},{6,7},{7,6},{8,9},{9,8},{10,11... | collective-permute-start | bytes 1769480 | tf_op jit(solution)/shard_map/ppermute | solution.py:623
  305.6 14.4 %collective-permute-start.53 = (bf16[1024,128]{0,1:T(8,128)(2,1)}, bf16[1024,128]{0,1:T(8,128)(2,1)}, u32[]{:S(2)}, u32[]{:S(2)}) collective-permute-start(bf16[1024,128]{0,1:T(8,128)(2,1)} %get-tuple-element.231), channel_id=1, source_target_pairs={{0,4},{12,8},{1,5},{13,9},{2,6},{14,10},{3,7},{15,11},{16,20},{28,... | collective-permute-start | bytes 786440 | tf_op jit(solution)/shard_map/ppermute | solution.py:615
  313.7 14.3 %collective-permute-start.55 = (bf16[1024,128]{0,1:T(8,128)(2,1)}, bf16[1024,128]{0,1:T(8,128)(2,1)}, u32[]{:S(2)}, u32[]{:S(2)}) collective-permute-start(bf16[1024,128]{0,1:T(8,128)(2,1)} %get-tuple-element.228), channel_id=1, source_target_pairs={{0,12},{12,0},{1,13},{13,1},{2,14},{14,2},{3,15},{15,3},{16,28},{2... | collective-permute-start | bytes 786440 | tf_op jit(solution)/shard_map/ppermute | solution.py:615
  318.5 16.4 %collective-permute-start.52 = (bf16[256,1152]{1,0:T(8,128)(2,1)}, bf16[256,1152]{1,0:T(8,128)(2,1)}, u32[]{:S(2)}, u32[]{:S(2)}) collective-permute-start(bf16[256,1152]{1,0:T(8,128)(2,1)} %broadcast_select_fusion), channel_id=1, source_target_pairs={{0,2},{1,3},{2,0},{3,1},{4,6},{5,7},{6,4},{7,5},{8,10},{9,11},{10,... | collective-permute-start | bytes 1769480 | tf_op jit(solution)/shard_map/ppermute | solution.py:627
  (76 other events, 715.4 us)
